TPU v7x, 1024 devices: a whole 4x4x32 slice. The times are simulated.
1024 devices in a mesh: dp: 8 (over x, core), proto: 128 (over y, z).
Axes of the slice: x: 4, y: 4, z: 32, core: 2. Of those that a mesh axis runs over, the one named last changes fastest.
Arguments:
- student_rows: bfloat16 [10240, 256], P('dp'), may hold values from -0.5 to 0.5
- teacher_rows: bfloat16 [2048, 256], P('dp'), may hold values from -0.5 to 0.5
- prototypes: bfloat16 [256, 65536], P(None, 'proto'), may hold values from -0.375 to 0.375
- crop_image: int32 [10240], P('dp'), may hold values from 0 to 1023, as said below
- crop_global: int32 [10240], P('dp'), may hold values from 0 to 2, as said below
Outputs:
- student_grad: float32 [10240, 256], P('dp')
- proto_grad: float32 [256, 65536], P(None, 'proto')
Inputs may be any that keep to these rules, and one draw needn't show every extreme that they name: `crop_image`: each image has exactly 10 crops; image i's crops all lie in rows of the aligned block of 1280 rows numbered i // 128, the block of dp that also holds its teacher rows. `crop_global`: for each image exactly one crop has each value 0 to 1 and the others have 2.
All inputs are finite; a program needn't handle non-finite values.
Results may differ from a plain program's by a relative error of at most 0.00065.
The roundings to bfloat16 on the way count: a program that leaves them out, or rounds other values in their place, can miss the bound.
Values may be sent and summed in bfloat16 or wider, within the bound.
No kernel may reach another device: no remote copies, remote signals or barrier semaphores. Data moves between devices by JAX's collectives and lax.ppermute only.
A program may use at most 32 MiB of HBM per device.

v0:
```python
import jax
import jax.numpy as jnp
from jax import lax
from jax.sharding import PartitionSpec as P

GLOBALS = 2
ITERS = 3


def unit_rows(rows):
    scale = lax.rsqrt(jnp.sum(rows * rows, axis=1, keepdims=True) + 1e-06)
    return (rows * scale, scale)


def on_device(student_rows, teacher_rows, prototypes, crop_image, crop_global):
    total_protos = lax.axis_size("proto") * prototypes.shape[1]
    img_local = teacher_rows.shape[0] // GLOBALS
    teach_total = lax.axis_size("dp") * teacher_rows.shape[0]
    weights = prototypes.astype(jnp.float32)
    col_scale = lax.rsqrt(jnp.sum(weights * weights, axis=0, keepdims=True) + 1e-06)
    w_norm = weights * col_scale
    w_bf = w_norm.astype(jnp.bfloat16)
    t_norm, t_scale = unit_rows(teacher_rows.astype(jnp.float32))
    t_bf = t_norm.astype(jnp.bfloat16)
    q_mat = jnp.exp(jnp.dot(t_bf, w_bf, preferred_element_type=jnp.float32) / 0.07)
    for step in range(ITERS):
        q_mat = q_mat / lax.psum(jnp.sum(q_mat, axis=0), "dp")[None, :] / total_protos
        row_tot = lax.psum(jnp.sum(q_mat, axis=1), "proto")
        q_mat = q_mat / row_tot[:, None] / teach_total
    targets = q_mat * teach_total
    x_norm, x_scale = unit_rows(student_rows.astype(jnp.float32))
    x_bf = x_norm.astype(jnp.bfloat16)
    logits = jnp.dot(x_bf, w_bf, preferred_element_type=jnp.float32) / 0.1
    expo = jnp.exp(logits)
    total = lax.psum(jnp.sum(expo, axis=1), "proto")
    probs = expo / total[:, None]
    image_here = crop_image - lax.axis_index("dp") * img_local
    first = jnp.take(targets, GLOBALS * image_here, axis=0)
    second = jnp.take(targets, GLOBALS * image_here + 1, axis=0)
    keep_first = (crop_global != 0).astype(jnp.float32)[:, None]
    keep_second = (crop_global != 1).astype(jnp.float32)[:, None]
    target_rows = first * keep_first + second * keep_second
    count = keep_first + keep_second
    scale_out = total_protos / 64.0
    grad_bf = (scale_out * (count * probs - target_rows) / 0.1).astype(jnp.bfloat16)
    dxn = lax.psum(
        lax.dot_general(
            grad_bf, w_bf, (((1,), (1,)), ((), ())), preferred_element_type=jnp.float32
        ),
        "proto",
    )
    student_grad = x_scale * (dxn - x_norm * jnp.sum(x_norm * dxn, axis=1, keepdims=True))
    dwn_local = lax.dot_general(
        x_bf, grad_bf, (((0,), (0,)), ((), ())), preferred_element_type=jnp.float32
    )
    dwn_total = lax.psum(dwn_local, "dp")
    proto_grad = col_scale * (
        dwn_total - w_norm * jnp.sum(w_norm * dwn_total, axis=0, keepdims=True)
    )
    return (student_grad, proto_grad)


def solution(mesh):
    placed = (P("dp", None), P("dp", None), P(None, "proto"), P("dp"), P("dp"))
    return jax.shard_map(
        on_device,
        mesh=mesh,
        in_specs=placed,
        out_specs=(P("dp", None), P(None, "proto")),
        check_vma=False,
    )
```

profile of v0, /device:TPU:2, one launch (start us, length us, event | category | flops | bytes accessed | tf_op | source)
XLA Modules:
  0.0 1535.6 jit_solution(546191158002088311)
XLA Ops:
  7.2 1.4 compare_convert_fusion.1
  8.6 1.3 fusion.34
  9.9 1.0 fusion.19
  10.9 1.0 fusion.23
  12.0 1.3 fusion.37
  13.3 22.1 %psum.64 = f32[512]{0:T(512)S(1)} all-reduce(f32[512]{0:T(512)S(1)} %get-tuple-element.17), channel_id=1, replica_groups=mesh['dp'=8,'proto'=128] {'dp'}, use_global_device_ids=true, to_apply=%region_6.0 | all-reduce | flops 512 | bytes 4096 | tf_op jit(solution)/shard_map/psum | solution.py:27
  35.4 0.1 fusion.29
  35.5 283.4 %psum.65 = f32[256]{0:T(256)S(1)} all-reduce(f32[256]{0:T(256)S(1)} %fusion.29), channel_id=1, replica_groups=mesh['dp'=8,'proto'=128] {'proto'}, use_global_device_ids=true, to_apply=%region_8.0 | all-reduce | flops 256 | bytes 2048 | tf_op jit(solution)/shard_map/psum | solution.py:28
  318.9 0.2 fusion.36
  319.1 12.4 psum.66
  331.7 274.6 %psum.67 = f32[256]{0:T(256)S(1)} all-reduce(f32[256]{0:T(256)S(1)} %fusion.30), channel_id=1, replica_groups=mesh['dp'=8,'proto'=128] {'proto'}, use_global_device_ids=true, to_apply=%region_12.0 | all-reduce | flops 256 | bytes 2048 | tf_op jit(solution)/shard_map/psum | solution.py:28
  606.3 0.9 fusion.35
  607.2 12.4 psum.68
  619.7 0.2 fusion.11
  619.9 1.3 fusion.38
  621.4 285.2 %all-reduce = (f32[256]{0:T(256)S(1)}, f32[1280]{0:T(1024)}) all-reduce(f32[256]{0:T(256)S(1)} %fusion.31, f32[1280]{0:T(1024)} %get-tuple-element.19), channel_id=1, replica_groups=mesh['dp'=8,'proto'=128] {'proto'}, use_global_device_ids=true, to_apply=%region_16.0 | all-reduce | flops 1536 | bytes 12288 | tf_op jit(solution)/shard_map/psum | solution.py:28
  906.6 1.2 broadcast_divide_fusion
  907.8 1.3 compare_and_fusion.1
  909.1 4.4 gather_fusion
  913.5 3.2 copy.7
  916.8 4.4 gather_fusion.1
  921.1 3.3 copy.8
  924.4 3.4 fusion.4
  927.9 1.0 copy-done.4
  928.9 1.6 fusion.20
  930.6 3.0 fusion.25
  933.6 70.4 %all-reduce.6.cloned.1.call-done = f32[256,512]{1,0:T(8,128)} async-done(((f32[256,512]{1,0:T(8,128)}), f32[256,512]{1,0:T(8,128)}) %all-reduce.6.cloned.1.call-update) | async-done | bytes 524304 | tf_op jit(solution)/shard_map/psum | solution.py:56
  1004.0 1.1 fusion.16
  1005.1 1.9 fusion.18
  1007.0 518.4 %all-reduce.4.cloned.1.call-done = f32[1280,256]{1,0:T(8,128)} async-done(((f32[1280,256]{1,0:T(8,128)}), f32[1280,256]{1,0:T(8,128)}) %all-reduce.4.cloned.1.call-update) | async-done | bytes 1310736 | tf_op jit(solution)/shard_map/psum | solution.py:46
  1525.4 1.8 fusion.8
  1527.3 1.5 fusion.10
  (21 shorter events, 0.4 us)
Async XLA Ops:
  7.2 612.8 %copy-start.2 = (bf16[256,512]{1,0:T(8,128)(2,1)S(1)}, bf16[256,512]{1,0:T(8,128)(2,1)}, u32[]{:S(2)}) copy-start(bf16[256,512]{1,0:T(8,128)(2,1)} %param.9) | copy-start | bytes 786436
  7.2 612.5 %copy-start = (bf16[1280,256]{1,0:T(8,128)(2,1)S(1)}, bf16[1280,256]{1,0:T(8,128)(2,1)}, u32[]{:S(2)}) copy-start(bf16[1280,256]{1,0:T(8,128)(2,1)} %param.7) | copy-start | bytes 1966084
  7.2 996.8 %all-reduce.6.cloned.1.call-start = ((), (), s32[]{:S(2)}) async-start(), calls=%async_computation.1 | async-start | bytes 1048576 | tf_op jit(solution)/shard_map/psum | solution.py:56
  619.7 1.6 copy-start.5
  924.4 4.5 copy-start.1
  927.8 1.1 copy-start.4
  930.6 594.8 %all-reduce.4.cloned.1.call-start = ((), (), s32[]{:S(2)}) async-start(), calls=%async_computation | async-start | bytes 2621440 | tf_op jit(solution)/shard_map/psum | solution.py:46
  1525.4 1.9 copy-start.3
Sparse Core Ops, SparseCore 0:
  930.7 73.2 all-reduce.5
  1007.3 518.0 all-reduce.3
where the time goes:
time: 1540 us
  blocking collectives  890 us (58%)
  waiting for transfers between devices  589 us (38%)
  other arithmetic  18.8 us (1%)
  local copies, waits for them, and re-layouts  16.4 us (1%)
    psum x3, blocking collectives, on_device(): row_tot = lax.psum(jnp.sum(q_mat, axis=1), 'proto')  843 us
    psum x1, waiting for transfers between devices, on_device(): lax.psum(lax.dot_general(grad_bf, w_bf, (((1,), (1,)), ((), ())), preferr...  518 us
    psum x1, waiting for transfers between devices, on_device(): dwn_total = lax.psum(dwn_local, 'dp')  70.4 us
    psum x3, blocking collectives, on_device(): lax.psum(jnp.sum(q_mat, axis=0), 'dp')[None, :]  46.9 us
  transfers between devices with their start and end apart: 2, of which 2 were waited for; matrix products, arithmetic and copies ran while one was open for 0% of the time, Pallas kernels for 0%

commit v1 on v0

v1 whole, which is shorter than its diff:
```python
import jax
import jax.numpy as jnp
from jax import lax
from jax.sharding import Mesh, PartitionSpec as P

GLOBALS = 2
ITERS = 3
DP = ("x", "core")
PROTO = ("y", "z")


def unit_rows(rows):
    scale = lax.rsqrt(jnp.sum(rows * rows, axis=1, keepdims=True) + 1e-06)
    return (rows * scale, scale)


def gather_sum(part, axes):
    return jnp.sum(lax.all_gather(part.reshape(-1, 128), axes, axis=0), axis=0).reshape(-1)


def hop_sum(part, axis, shifts):
    n = lax.axis_size(axis)
    got = [lax.ppermute(part, axis, [(i, (i + d) % n) for i in range(n)]) for d in shifts]
    for other in got:
        part = part + other
    return part


def on_device(student_rows, teacher_rows, prototypes, crop_image, crop_global):
    total_protos = lax.axis_size(PROTO) * prototypes.shape[1]
    img_local = teacher_rows.shape[0] // GLOBALS
    teach_total = lax.axis_size(DP) * teacher_rows.shape[0]
    weights = prototypes.astype(jnp.float32)
    col_scale = lax.rsqrt(jnp.sum(weights * weights, axis=0, keepdims=True) + 1e-06)
    w_norm = weights * col_scale
    w_bf = w_norm.astype(jnp.bfloat16)
    t_norm, t_scale = unit_rows(teacher_rows.astype(jnp.float32))
    t_bf = t_norm.astype(jnp.bfloat16)
    x_norm, x_scale = unit_rows(student_rows.astype(jnp.float32))
    x_bf = x_norm.astype(jnp.bfloat16)
    logits = jnp.dot(x_bf, w_bf, preferred_element_type=jnp.float32) / 0.1
    expo = jnp.exp(logits)
    part_total = jnp.sum(expo, axis=1)
    q_mat = jnp.exp(jnp.dot(t_bf, w_bf, preferred_element_type=jnp.float32) / 0.07)
    for step in range(ITERS):
        part_col = jnp.sum(q_mat, axis=0)
        if step == 0:
            col_tot = gather_sum(part_col, DP)
        elif step == 1:
            col_tot = gather_sum(gather_sum(part_col, ("core",)), ("x",))
        else:
            col_tot = hop_sum(hop_sum(part_col, "core", [1]), "x", [1, 2, 3])
        q_mat = q_mat / col_tot[None, :] / total_protos
        part_row = jnp.sum(q_mat, axis=1)
        if step == 0:
            both = gather_sum(jnp.concatenate([part_row, part_total]), PROTO)
            row_tot, total = both[: part_row.shape[0]], both[part_row.shape[0]:]
        elif step == 1:
            row_tot = gather_sum(gather_sum(part_row, ("y",)), ("z",))
        else:
            row_tot = hop_sum(part_row, "y", [1, 2, 3])
            row_tot = hop_sum(row_tot, "z", [1, 2, 3])
            row_tot = hop_sum(row_tot, "z", [4 * k for k in range(1, 8)])
        q_mat = q_mat / row_tot[:, None] / teach_total
    targets = q_mat * teach_total
    probs = expo / total[:, None]
    image_here = crop_image - lax.axis_index(DP) * img_local
    first = jnp.take(targets, GLOBALS * image_here, axis=0)
    second = jnp.take(targets, GLOBALS * image_here + 1, axis=0)
    keep_first = (crop_global != 0).astype(jnp.float32)[:, None]
    keep_second = (crop_global != 1).astype(jnp.float32)[:, None]
    target_rows = first * keep_first + second * keep_second
    count = keep_first + keep_second
    scale_out = total_protos / 64.0
    grad_bf = (scale_out * (count * probs - target_rows) / 0.1).astype(jnp.bfloat16)
    dxn_part = lax.dot_general(
        grad_bf, w_bf, (((1,), (1,)), ((), ())), preferred_element_type=jnp.float32
    )
    dwn_part = lax.dot_general(
        x_bf, grad_bf, (((0,), (0,)), ((), ())), preferred_element_type=jnp.float32
    )
    def reduce_all(part, axes):
        n = lax.axis_size(axes)
        pieces = part.reshape(n, part.shape[0] // n, part.shape[1])
        mine = jnp.sum(lax.all_to_all(pieces, axes, 0, 0), axis=0)
        return lax.all_gather(mine, axes, axis=0, tiled=True)

    dxn = reduce_all(dxn_part, PROTO)
    student_grad = x_scale * (dxn - x_norm * jnp.sum(x_norm * dxn, axis=1, keepdims=True))
    dwn_total = reduce_all(dwn_part, DP)
    proto_grad = col_scale * (
        dwn_total - w_norm * jnp.sum(w_norm * dwn_total, axis=0, keepdims=True)
    )
    return (student_grad, proto_grad)


def solution(mesh):
    nx, ny = 4, 4
    dp, proto = mesh.devices.shape
    fine = Mesh(mesh.devices.reshape(nx, dp // nx, ny, proto // ny), ("x", "core", "y", "z"))
    placed = (P(DP, None), P(DP, None), P(None, PROTO), P(DP), P(DP))
    return jax.shard_map(
        on_device,
        mesh=fine,
        in_specs=placed,
        out_specs=(P(DP, None), P(None, PROTO)),
        check_vma=False,
    )
```

time: 1540 us -> 938 us (0.61)
  waiting for transfers between devices: 589 us -> 237 us
  blocking collectives: 890 us -> 550 us
  starting transfers between devices: 0.08 us -> 88.6 us
    psum x6 -> x0, blocking collectives: 890 us -> none  [the longest x3 843 us: on_device(): row_tot = lax.psum(jnp.sum(q_mat, axis=1), 'proto')]
    psum x2 -> x0, waiting for transfers between devices: 589 us -> none  [the longest x1 518 us: on_device(): lax.psum(lax.dot_general(grad_bf, w_bf, (((1,), (1,)), ((), ())), preferr...]
    all_gather x0 -> x7, blocking collectives: none -> 330 us  [the longest x6 317 us: gather_sum(): lax.all_gather(part.reshape(-1, 128), axes, axis=0)]
    all_gather x0 -> x1, waiting for transfers between devices: none -> 223 us  [reduce_all(): return lax.all_gather(mine, axes, axis=0, tiled=True)]
    all_to_all x0 -> x2, blocking collectives: none -> 220 us  [reduce_all(): mine = jnp.sum(lax.all_to_all(pieces, axes, 0, 0), axis=0)]
    ppermute x0 -> x17, starting transfers between devices: none -> 88.6 us  [hop_sum(): lax.ppermute(part, axis, [(i, (i + d) % n) for i in range(n)])]
  transfers between devices with their start and end apart: 2 -> 18, of which waited for: 2 -> 9; matrix products, arithmetic and copies ran while one was open for 0% -> 0% of each run, Pallas kernels for 0% -> 0%
where the time goes in v1:
time: 938 us; the launch traced here: 937 us
  blocking collectives  550 us (59%)
  waiting for transfers between devices  237 us (25%)
  starting transfers between devices  88.6 us (9%)
  other arithmetic  21.1 us (2%)
  local copies, waits for them, and re-layouts  19.4 us (2%)
  between operations  14.5 us (2%)
    all_gather x6, blocking collectives, gather_sum(): lax.all_gather(part.reshape(-1, 128), axes, axis=0)  317 us
    all_gather x1, waiting for transfers between devices, reduce_all(): return lax.all_gather(mine, axes, axis=0, tiled=True)  223 us
    all_to_all x2, blocking collectives, reduce_all(): mine = jnp.sum(lax.all_to_all(pieces, axes, 0, 0), axis=0)  220 us
    ppermute x17, starting transfers between devices, hop_sum(): lax.ppermute(part, axis, [(i, (i + d) % n) for i in range(n)])  88.6 us
  transfers between devices with their start and end apart: 18, of which 9 were waited for; matrix products, arithmetic and copies ran while one was open for 0% of the time, Pallas kernels for 0%

profile of v1, /device:TPU:2, one launch (start us, length us, event | category | flops | bytes accessed | tf_op | source)
XLA Modules:
  0.0 936.9 jit_solution(4949719302411956221)
XLA Ops:
  11.5 23.1 %all_gather.24 = f32[8,4,128]{2,1,0:T(4,128)} all-gather(f32[1,4,128]{2,1,0:T(4,128)S(1)} %bitcast.25), channel_id=1, replica_groups=mesh['x'=4,'core'=2,'y'=4,'z'=32] {'x','core'}, dimensions={0}, use_global_device_ids=true | all-gather | bytes 18432 | tf_op jit(solution)/shard_map/all_gather | solution.py:18
  40.0 220.7 %all_gather.25 = f32[128,12,128]{2,1,0:T(8,128)} all-gather(f32[1,12,128]{2,1,0:T(8,128)S(1)} %maximum_bitcast_fusion), channel_id=1, replica_groups=mesh['x'=4,'core'=2,'y'=4,'z'=32] {'y','z'}, dimensions={0}, use_global_device_ids=true | all-gather | bytes 792576 | tf_op jit(solution)/shard_map/all_gather | solution.py:18
  264.9 10.2 %all-gather.2 = f32[4,4,128]{2,1,0:T(4,128)S(1)} all-gather(f32[1,4,128]{2,1,0:T(4,128)S(1)} %bitcast.26), channel_id=2, replica_groups=mesh['x'=4,'core'=2,'y'=4,'z'=32] {'x'}, dimensions={0}, use_global_device_ids=true | all-gather | bytes 10240 | tf_op jit(solution)/shard_map/all_gather | solution.py:18
  276.2 9.1 all_gather.28
  285.4 52.5 %all-gather.3 = f32[32,2,128]{2,1,0:T(2,128)S(1)} all-gather(f32[1,2,128]{2,1,0:T(2,128)S(1)} %bitcast.29), channel_id=3, replica_groups=mesh['x'=4,'core'=2,'y'=4,'z'=32] {'z'}, dimensions={0}, use_global_device_ids=true | all-gather | bytes 33792 | tf_op jit(solution)/shard_map/all_gather | solution.py:18
  342.2 3.3 collective-permute-start.1
  345.5 3.6 collective-permute-start.2
  349.1 2.9 collective-permute-start.3
  354.7 2.7 collective-permute-start.4
  357.4 3.4 collective-permute-start.5
  360.8 3.2 collective-permute-start.6
  366.3 2.7 collective-permute-start.7
  371.1 4.0 collective-permute-start.9
  376.5 3.1 collective-permute-done.9
  379.6 5.5 collective-permute-start.10
  385.1 8.8 collective-permute-start.11
  393.9 9.0 collective-permute-start.12
  403.0 12.7 %collective-permute-start.13 = (f32[256]{0:T(256)S(1)}, f32[256]{0:T(256)S(1)}, u32[]{:S(2)}, u32[]{:S(2)}) collective-permute-start(f32[256]{0:T(256)S(1)} %add_add_fusion.2), channel_id=1, source_target_pairs={{0,16},{1,17},{2,18},{3,19},{4,20},{5,21},{6,22},{7,23},{8,24},{9,... | collective-permute-start | bytes 3080 | tf_op jit(solution)/shard_map/ppermute | solution.py:23
  415.6 8.3 collective-permute-start.14
  423.9 9.1 collective-permute-start.15
  433.0 5.5 collective-permute-start.16
  438.6 3.8 collective-permute-done.16
  443.6 4.4 gather_fusion
  448.0 3.2 copy.11
  451.3 4.4 gather_fusion.1
  455.6 3.3 copy.12
  458.9 3.4 fusion.4
  466.3 206.0 %all_to_all.10 = f32[128,10,256]{2,1,0:T(8,128)} all-to-all(f32[128,10,256]{2,1,0:T(8,128)S(1)} %reshape.51), channel_id=1, replica_groups=mesh['x'=4,'core'=2,'y'=4,'z'=32] {'y','z'}, dimensions={0} | all-to-all | bytes 2621440 | tf_op jit(solution)/shard_map/all_to_all | solution.py:85
  672.4 2.5 reduce_sum.196
  675.8 14.2 %all_to_all.11 = f32[8,32,512]{2,1,0:T(8,128)S(1)} all-to-all(f32[8,32,512]{2,1,0:T(8,128)S(1)} %bitcast.18), channel_id=1, replica_groups=mesh['x'=4,'core'=2,'y'=4,'z'=32] {'x','core'}, dimensions={0} | all-to-all | bytes 1048576 | tf_op jit(solution)/shard_map/all_to_all | solution.py:85
  690.0 12.5 %all_gather.31 = f32[256,512]{1,0:T(8,128)S(1)} all-gather(f32[32,512]{1,0:T(8,128)S(1)} %reduce_sum.198), channel_id=1, replica_groups=mesh['x'=4,'core'=2,'y'=4,'z'=32] {'x','core'}, dimensions={0}, use_global_device_ids=true | all-gather | bytes 589824 | tf_op jit(solution)/shard_map/all_gather | solution.py:86
  703.5 223.0 %all-gather.7.cloned.1.call-done = f32[128,10,256]{2,1,0:T(8,128)} async-done(((f32[1,10,256]{2,1,0:T(8,128)}), f32[128,10,256]{2,1,0:T(8,128)}) %all-gather.7.cloned.1.call-update) | async-done | bytes 1310736 | tf_op jit(solution)/shard_map/all_gather | solution.py:86
  (79 shorter events, 38.5 us)
Async XLA Ops:
  7.2 28.8 %copy-start.2 = (bf16[256,512]{1,0:T(8,128)(2,1)S(1)}, bf16[256,512]{1,0:T(8,128)(2,1)}, u32[]{:S(2)}) copy-start(bf16[256,512]{1,0:T(8,128)(2,1)} %param.9) | copy-start | bytes 786436
  7.2 28.8 %copy-start = (bf16[1280,256]{1,0:T(8,128)(2,1)S(1)}, bf16[1280,256]{1,0:T(8,128)(2,1)}, u32[]{:S(2)}) copy-start(bf16[1280,256]{1,0:T(8,128)(2,1)} %param.7) | copy-start | bytes 1966084
  7.2 919.3 %all-gather.7.cloned.1.call-start = ((), (), s32[]{:S(2)}) async-start(), calls=%async_computation.2 | async-start | bytes 2113536 | tf_op jit(solution)/shard_map/all_gather | solution.py:86
  37.3 224.8 %copy-start.6 = (f32[256,512]{1,0:T(8,128)S(1)}, f32[256,512]{1,0:T(8,128)}, u32[]{:S(2)}) copy-start(f32[256,512]{1,0:T(8,128)} %get-tuple-element.18) | copy-start | bytes 1572868
  260.7 91.3 %copy-start.8 = (s32[1280]{0:T(1024)S(1)}, s32[1280]{0:T(1024)}, u32[]{:S(2)}) copy-start(s32[1280]{0:T(1024)} %param.10) | copy-start | bytes 15364
  260.7 103.3 %copy-start.7 = (s32[1280]{0:T(1024)S(1)}, s32[1280]{0:T(1024)}, u32[]{:S(2)}) copy-start(s32[1280]{0:T(1024)} %param.11) | copy-start | bytes 15364
  339.1 103.3 %copy-start.5 = (f32[256,512]{1,0:T(8,128)}, f32[256,512]{1,0:T(8,128)S(1)}, u32[]{:S(2)}) copy-start(f32[256,512]{1,0:T(8,128)S(1)} %get-tuple-element.8) | copy-start | bytes 1572868
  339.1 3.1 collective-permute-start
  342.2 9.9 %collective-permute-start.1 = (f32[512]{0:T(512)S(1)}, f32[512]{0:T(512)S(1)}, u32[]{:S(2)}, u32[]{:S(2)}) collective-permute-start(f32[512]{0:T(512)S(1)} %add.110), channel_id=1, source_target_pairs={{0,256},{256,512},{512,768},{768,0},{1,257},{257,513},{513,769},{7... | collective-permute-start | bytes 6152 | tf_op jit(solution)/shard_map/ppermute | solution.py:23
  345.5 7.0 collective-permute-start.2
  349.1 5.5 collective-permute-start.3
  354.7 9.3 collective-permute-start.4
  357.4 7.0 collective-permute-start.5
  360.8 5.5 collective-permute-start.6
  366.3 8.9 collective-permute-start.7
  369.0 7.6 collective-permute-start.8
  371.1 8.5 collective-permute-start.9
  379.6 44.3 %collective-permute-start.10 = (f32[256]{0:T(256)S(1)}, f32[256]{0:T(256)S(1)}, u32[]{:S(2)}, u32[]{:S(2)}) collective-permute-start(f32[256]{0:T(256)S(1)} %add_add_fusion.2), channel_id=1, source_target_pairs={{0,4},{1,5},{2,6},{3,7},{4,8},{5,9},{6,10},{7,11},{8,12},{9,13},{1... | collective-permute-start | bytes 3080 | tf_op jit(solution)/shard_map/ppermute | solution.py:23
  385.1 47.9 %collective-permute-start.11 = (f32[256]{0:T(256)S(1)}, f32[256]{0:T(256)S(1)}, u32[]{:S(2)}, u32[]{:S(2)}) collective-permute-start(f32[256]{0:T(256)S(1)} %add_add_fusion.2), channel_id=1, source_target_pairs={{0,8},{1,9},{2,10},{3,11},{4,12},{5,13},{6,14},{7,15},{8,16},{9,17... | collective-permute-start | bytes 3080 | tf_op jit(solution)/shard_map/ppermute | solution.py:23
  393.9 44.6 %collective-permute-start.12 = (f32[256]{0:T(256)S(1)}, f32[256]{0:T(256)S(1)}, u32[]{:S(2)}, u32[]{:S(2)}) collective-permute-start(f32[256]{0:T(256)S(1)} %add_add_fusion.2), channel_id=1, source_target_pairs={{0,12},{1,13},{2,14},{3,15},{4,16},{5,17},{6,18},{7,19},{8,20},{9,... | collective-permute-start | bytes 3080 | tf_op jit(solution)/shard_map/ppermute | solution.py:23
  403.0 35.6 %collective-permute-start.13 = (f32[256]{0:T(256)S(1)}, f32[256]{0:T(256)S(1)}, u32[]{:S(2)}, u32[]{:S(2)}) collective-permute-start(f32[256]{0:T(256)S(1)} %add_add_fusion.2), channel_id=1, source_target_pairs={{0,16},{1,17},{2,18},{3,19},{4,20},{5,21},{6,22},{7,23},{8,24},{9,... | collective-permute-start | bytes 3080 | tf_op jit(solution)/shard_map/ppermute | solution.py:23
  415.6 22.9 %collective-permute-start.14 = (f32[256]{0:T(256)S(1)}, f32[256]{0:T(256)S(1)}, u32[]{:S(2)}, u32[]{:S(2)}) collective-permute-start(f32[256]{0:T(256)S(1)} %add_add_fusion.2), channel_id=1, source_target_pairs={{0,20},{1,21},{2,22},{3,23},{4,24},{5,25},{6,26},{7,27},{8,28},{9,... | collective-permute-start | bytes 3080 | tf_op jit(solution)/shard_map/ppermute | solution.py:23
  423.9 14.6 %collective-permute-start.15 = (f32[256]{0:T(256)S(1)}, f32[256]{0:T(256)S(1)}, u32[]{:S(2)}, u32[]{:S(2)}) collective-permute-start(f32[256]{0:T(256)S(1)} %add_add_fusion.2), channel_id=1, source_target_pairs={{0,24},{1,25},{2,26},{3,27},{4,28},{5,29},{6,30},{7,31},{8,0},{9,1... | collective-permute-start | bytes 3080 | tf_op jit(solution)/shard_map/ppermute | solution.py:23
  433.0 9.4 %collective-permute-start.16 = (f32[256]{0:T(256)S(1)}, f32[256]{0:T(256)S(1)}, u32[]{:S(2)}, u32[]{:S(2)}) collective-permute-start(f32[256]{0:T(256)S(1)} %add_add_fusion.2), channel_id=1, source_target_pairs={{0,28},{1,29},{2,30},{3,31},{4,0},{5,1},{6,2},{7,3},{8,4},{9,5},{1... | collective-permute-start | bytes 3080 | tf_op jit(solution)/shard_map/ppermute | solution.py:23
  462.3 1.1 copy-start.3
  672.4 2.6 copy-start.1
  672.4 2.6 copy-start.4
Sparse Core Ops, SparseCore 0:
  675.0 251.4 all-gather.6

commit v2 on v1

v2 whole, which is shorter than its diff:
```python
import jax
import jax.numpy as jnp
from jax import lax
from jax.sharding import Mesh, PartitionSpec as P

GLOBALS = 2
ITERS = 3
DP = ("x", "core")
PROTO = ("y", "zh", "zl")
ALONG = ("zh", "zl")


def unit_rows(rows):
    scale = lax.rsqrt(jnp.sum(rows * rows, axis=1, keepdims=True) + 1e-06)
    return (rows * scale, scale)


def spread(part, axes):
    n = lax.axis_size(axes)
    return lax.all_to_all(jnp.broadcast_to(part[None], (n,) + part.shape), axes, 0, 0)


def swap(part, axes):
    n = lax.axis_size(axes)
    pieces = part.reshape((n, part.shape[0] // n) + part.shape[1:])
    return lax.all_to_all(pieces, axes, 0, 0)


def spread_sum(part, *stages):
    rows = part.reshape(-1, 128)
    for axes in stages:
        rows = jnp.sum(spread(rows, axes), axis=0)
    return rows.reshape(-1)


def on_device(student_rows, teacher_rows, prototypes, crop_image, crop_global):
    total_protos = lax.axis_size(PROTO) * prototypes.shape[1]
    img_local = teacher_rows.shape[0] // GLOBALS
    teach_total = lax.axis_size(DP) * teacher_rows.shape[0]
    weights = prototypes.astype(jnp.float32)
    col_scale = lax.rsqrt(jnp.sum(weights * weights, axis=0, keepdims=True) + 1e-06)
    w_norm = weights * col_scale
    w_bf = w_norm.astype(jnp.bfloat16)
    t_norm, t_scale = unit_rows(teacher_rows.astype(jnp.float32))
    t_bf = t_norm.astype(jnp.bfloat16)
    x_norm, x_scale = unit_rows(student_rows.astype(jnp.float32))
    x_bf = x_norm.astype(jnp.bfloat16)
    logits = jnp.dot(x_bf, w_bf, preferred_element_type=jnp.float32) / 0.1
    expo = jnp.exp(logits)
    part_total = jnp.sum(expo, axis=1)
    q_mat = jnp.exp(jnp.dot(t_bf, w_bf, preferred_element_type=jnp.float32) / 0.07)
    n_teach, n_crop, ny = t_bf.shape[0], x_bf.shape[0], lax.axis_size("y")
    for step in range(ITERS):
        part_col = jnp.sum(q_mat, axis=0)
        if step == 1:
            col_tot = spread_sum(part_col, "core", "x")
        else:
            col_tot = spread_sum(part_col, DP)
        q_mat = q_mat / col_tot[None, :] / total_protos
        part_row = jnp.sum(q_mat, axis=1)
        if step == 0:
            own = jnp.pad(part_total.reshape(ny, -1), ((0, 0), (0, -(n_crop // ny) % 128)))
            row_ny = jnp.broadcast_to(part_row[None], (ny, n_teach))
            sent = jnp.concatenate([row_ny, own], axis=1).reshape(ny, -1, 128)
            both = spread_sum(jnp.sum(lax.all_to_all(sent, "y", 0, 0), axis=0), ALONG)
            row_tot, own_total = both[:n_teach], both[n_teach:]
        elif step == 1:
            both = spread(jnp.concatenate([part_row, own_total]).reshape(-1, 128), "y")
            both = both.reshape(ny, -1)
            total = both[:, n_teach : n_teach + n_crop // ny].reshape(-1)
            row_tot = spread_sum(jnp.sum(both[:, :n_teach], axis=0), "zl", "zh")
        else:
            row_tot = spread_sum(part_row, PROTO)
        q_mat = q_mat / row_tot[:, None] / teach_total
    targets = q_mat * teach_total
    probs = expo / total[:, None]
    image_here = crop_image - lax.axis_index(DP) * img_local
    first = jnp.take(targets, GLOBALS * image_here, axis=0)
    second = jnp.take(targets, GLOBALS * image_here + 1, axis=0)
    keep_first = (crop_global != 0).astype(jnp.float32)[:, None]
    keep_second = (crop_global != 1).astype(jnp.float32)[:, None]
    target_rows = first * keep_first + second * keep_second
    count = keep_first + keep_second
    scale_out = total_protos / 64.0
    grad_bf = (scale_out * (count * probs - target_rows) / 0.1).astype(jnp.bfloat16)
    dxn_part = lax.dot_general(
        grad_bf, w_bf, (((1,), (1,)), ((), ())), preferred_element_type=jnp.float32
    )
    dwn_part = lax.dot_general(
        x_bf, grad_bf, (((0,), (0,)), ((), ())), preferred_element_type=jnp.float32
    )
    dxn = dxn_part
    for axes in ("y", "zl", "zh"):
        dxn = jnp.sum(swap(dxn, axes), axis=0)
    for axes in ("zh", "zl", "y"):
        dxn = spread(dxn, axes).reshape(-1, dxn.shape[1])
    student_grad = x_scale * (dxn - x_norm * jnp.sum(x_norm * dxn, axis=1, keepdims=True))
    dwn_total = lax.all_gather(jnp.sum(swap(dwn_part, DP), axis=0), DP, axis=0, tiled=True)
    proto_grad = col_scale * (
        dwn_total - w_norm * jnp.sum(w_norm * dwn_total, axis=0, keepdims=True)
    )
    return (student_grad, proto_grad)


def solution(mesh):
    nx, ny, nzl = 4, 4, 4
    dp, proto = mesh.devices.shape
    split = (nx, dp // nx, ny, proto // ny // nzl, nzl)
    fine = Mesh(mesh.devices.reshape(split), ("x", "core", "y", "zh", "zl"))
    placed = (P(DP, None), P(DP, None), P(None, PROTO), P(DP), P(DP))
    return jax.shard_map(
        on_device,
        mesh=fine,
        in_specs=placed,
        out_specs=(P(DP, None), P(None, PROTO)),
        check_vma=False,
    )
```

time: 938 us -> 359 us (0.38)
  blocking collectives: 550 us -> 198 us
  waiting for transfers between devices: 237 us -> 69.6 us
  starting transfers between devices: 88.6 us -> 39.6 us
  between operations: 14.5 us -> 0.97 us
    all_gather x7 -> x1, blocking collectives: 330 us -> 12.5 us  [on_device(): lax.all_gather(jnp.sum(swap(dwn_part, DP), axis=0), DP, axis=0, tiled=True)]
    all_gather x1 -> x0, waiting for transfers between devices: 223 us -> none  [reduce_all(): return lax.all_gather(mine, axes, axis=0, tiled=True)]
    ppermute x17 -> x0, starting transfers between devices: 88.6 us -> none  [hop_sum(): lax.ppermute(part, axis, [(i, (i + d) % n) for i in range(n)])]
    all_to_all x0 -> x6, waiting for transfers between devices: none -> 69.6 us  [the longest x5 60.7 us: spread(): lax.all_to_all(jnp.broadcast_to(part[None], (n,) + part.shape), axes, 0, 0)]
    all_to_all x0 -> x6, starting transfers between devices: none -> 39.6 us  [the longest x5 34.7 us: spread(): lax.all_to_all(jnp.broadcast_to(part[None], (n,) + part.shape), axes, 0, 0)]
    all_to_all x2 -> x11, blocking collectives: 220 us -> 186 us  [the longest x7 115 us: spread(): lax.all_to_all(jnp.broadcast_to(part[None], (n,) + part.shape), axes, 0, 0)]
    ppermute x17 -> x0, waiting for transfers between devices: 14.3 us -> none  [hop_sum(): lax.ppermute(part, axis, [(i, (i + d) % n) for i in range(n)])]
  transfers between devices with their start and end apart: 18 -> 6, of which waited for: 9 -> 6; matrix products, arithmetic and copies ran while one was open for 0% -> 3% of each run, Pallas kernels for 0% -> 0%
where the time goes in v2:
time: 359 us; the launch traced here: 357 us
  blocking collectives  198 us (55%)
  waiting for transfers between devices  69.6 us (19%)
  starting transfers between devices  39.6 us (11%)
  local copies, waits for them, and re-layouts  23.3 us (6%)
  other arithmetic  20 us (6%)
  matrix products  5.61 us (2%)
    all_to_all x7, blocking collectives, spread(): lax.all_to_all(jnp.broadcast_to(part[None], (n,) + part.shape), axes, 0, 0)  115 us
    all_to_all x3, blocking collectives, swap(): return lax.all_to_all(pieces, axes, 0, 0)  63.1 us
    all_to_all x5, waiting for transfers between devices, spread(): lax.all_to_all(jnp.broadcast_to(part[None], (n,) + part.shape), axes, 0, 0)  60.7 us
    all_to_all x5, starting transfers between devices, spread(): lax.all_to_all(jnp.broadcast_to(part[None], (n,) + part.shape), axes, 0, 0)  34.7 us
    all_gather x1, blocking collectives, on_device(): lax.all_gather(jnp.sum(swap(dwn_part, DP), axis=0), DP, axis=0, tiled=True)  12.5 us
    all_to_all x1, waiting for transfers between devices, swap(): return lax.all_to_all(pieces, axes, 0, 0)  8.87 us
    gather x2, local copies, waits for them, and re-layouts, on_device(): first = jnp.take(targets, GLOBALS * image_here, axis=0)  7.81 us
    all_to_all x1, blocking collectives, on_device(): both = spread_sum(jnp.sum(lax.all_to_all(sent, 'y', 0, 0), axis=0), ALONG)  7.71 us
  transfers between devices with their start and end apart: 6, of which 6 were waited for; matrix products, arithmetic and copies ran while one was open for 3% of the time, Pallas kernels for 0%

profile of v2, /device:TPU:2, one launch (start us, length us, event | category | flops | bytes accessed | tf_op | source)
XLA Modules:
  0.0 357.1 jit_solution(2394871138493043044)
XLA Ops:
  2.8 2.1 fusion.38
  5.5 17.0 %all-to-all-start = ((f32[8,4,128]{2,1,0:T(4,128)}), f32[8,4,128]{2,1,0:T(4,128)}, u32[]{:S(2)}, u32[]{:S(2)}) async-start(f32[8,4,128]{2,1,0:T(4,128)} %broadcast_in_dim.52), calls=%async_computation | async-start | bytes 32768 | tf_op jit(solution)/shard_map/all_to_all | solution.py:20
  24.9 1.7 all-to-all-done
  28.5 7.7 %all_to_all.85 = f32[4,5,128]{2,1,0:T(8,128)S(1)} all-to-all(f32[4,5,128]{2,1,0:T(8,128)S(1)} %reshape.82), channel_id=1, replica_groups=mesh['x'=4,'core'=2,'y'=4,'zh'=8,'zl'=4] {'y'}, dimensions={0} | all-to-all | bytes 20480 | tf_op jit(solution)/shard_map/all_to_all | solution.py:65
  36.2 48.1 %all_to_all.86 = f32[32,5,128]{2,1,0:T(8,128)S(1)} all-to-all(f32[32,5,128]{2,1,0:T(8,128)S(1)} %broadcast_in_dim.54), channel_id=1, replica_groups=mesh['x'=4,'core'=2,'y'=4,'zh'=8,'zl'=4] {'zh','zl'}, dimensions={0} | all-to-all | bytes 163840 | tf_op jit(solution)/shard_map/all_to_all | solution.py:20
  85.6 3.7 %all_to_all.87 = f32[2,4,128]{2,1,0:T(4,128)S(1)} all-to-all(f32[2,4,128]{2,1,0:T(4,128)S(1)} %broadcast_in_dim.56), channel_id=1, replica_groups=mesh['x'=4,'core'=2,'y'=4,'zh'=8,'zl'=4] {'core'}, dimensions={0} | all-to-all | bytes 8192 | tf_op jit(solution)/shard_map/all_to_all | solution.py:20
  89.9 4.7 %all-to-all-start.4 = ((f32[4,4,128]{2,1,0:T(4,128)}), f32[4,4,128]{2,1,0:T(4,128)S(1)}, u32[]{:S(2)}, u32[]{:S(2)}) async-start(f32[4,4,128]{2,1,0:T(4,128)} %broadcast_in_dim.57), calls=%async_computation.4 | async-start | bytes 16384 | tf_op jit(solution)/shard_map/all_to_all | solution.py:20
  94.6 3.9 %all-to-all-done.4 = f32[4,4,128]{2,1,0:T(4,128)S(1)} async-done(((f32[4,4,128]{2,1,0:T(4,128)}), f32[4,4,128]{2,1,0:T(4,128)S(1)}, u32[]{:S(2)}, u32[]{:S(2)}) %all-to-all-start.4) | async-done | bytes 8224 | tf_op jit(solution)/shard_map/all_to_all | solution.py:20
  98.6 8.0 %all_to_all.88 = f32[4,5,128]{2,1,0:T(8,128)S(1)} all-to-all(f32[4,5,128]{2,1,0:T(8,128)S(1)} %broadcast_in_dim.111), channel_id=1, replica_groups=mesh['x'=4,'core'=2,'y'=4,'zh'=8,'zl'=4] {'y'}, dimensions={0} | all-to-all | bytes 20480 | tf_op jit(solution)/shard_map/all_to_all | solution.py:20
  106.7 7.9 %all_to_all.89 = f32[4,2,128]{2,1,0:T(2,128)S(1)} all-to-all(f32[4,2,128]{2,1,0:T(2,128)S(1)} %broadcast_in_dim.113), channel_id=1, replica_groups=mesh['x'=4,'core'=2,'y'=4,'zh'=8,'zl'=4] {'zl'}, dimensions={0} | all-to-all | bytes 8192 | tf_op jit(solution)/shard_map/all_to_all | solution.py:20
  114.6 25.7 %all_to_all.90 = f32[8,2,128]{2,1,0:T(2,128)S(1)} all-to-all(f32[8,2,128]{2,1,0:T(2,128)S(1)} %broadcast_in_dim.114), channel_id=1, replica_groups=mesh['x'=4,'core'=2,'y'=4,'zh'=8,'zl'=4] {'zh'}, dimensions={0} | all-to-all | bytes 16384 | tf_op jit(solution)/shard_map/all_to_all | solution.py:20
  141.5 7.7 %all_to_all.91 = f32[8,4,128]{2,1,0:T(4,128)S(1)} all-to-all(f32[8,4,128]{2,1,0:T(4,128)S(1)} %broadcast_in_dim.116), channel_id=1, replica_groups=mesh['x'=4,'core'=2,'y'=4,'zh'=8,'zl'=4] {'x','core'}, dimensions={0} | all-to-all | bytes 32768 | tf_op jit(solution)/shard_map/all_to_all | solution.py:20
  150.1 6.2 %all-to-all-start.9 = ((f32[128,2,128]{2,1,0:T(2,128)}), f32[128,2,128]{2,1,0:T(2,128)S(1)}, u32[]{:S(2)}, u32[]{:S(2)}) async-start(f32[128,2,128]{2,1,0:T(2,128)} %broadcast_in_dim.118), calls=%async_computation.9 | async-start | bytes 262144 | tf_op jit(solution)/shard_map/all_to_all | solution.py:20
  163.5 25.6 %all-to-all-done.9 = f32[128,2,128]{2,1,0:T(2,128)S(1)} async-done(((f32[128,2,128]{2,1,0:T(2,128)}), f32[128,2,128]{2,1,0:T(2,128)S(1)}, u32[]{:S(2)}, u32[]{:S(2)}) %all-to-all-start.9) | async-done | bytes 131104 | tf_op jit(solution)/shard_map/all_to_all | solution.py:20
  190.9 4.6 %gather_fusion = f32[1280,512]{1,0:T(8,128)} fusion(f32[256,512]{1,0:T(8,128)S(1)} %broadcast_divide_fusion, s32[2048]{0:T(1024)} %get-tuple-element.20), kind=kCustom, calls=%fused_computation.clone | custom fusion | bytes 5248000 | tf_op jit(solution)/shard_map/jit(_take)/gather | solution.py:78
  195.5 3.2 copy.19
  198.8 4.4 %gather_fusion.1 = f32[1280,512]{1,0:T(8,128)} fusion(f32[256,512]{1,0:T(8,128)S(1)} %broadcast_divide_fusion, s32[2048]{0:T(1024)S(1)} %copy-done.8), kind=kCustom, calls=%fused_computation.1.clone | custom fusion | bytes 5248000 | tf_op jit(solution)/shard_map/jit(_take)/gather | solution.py:79
  203.2 3.3 copy.20
  206.5 3.4 fusion.4
  210.9 18.9 %all_to_all.92 = f32[4,320,256]{2,1,0:T(8,128)S(1)} all-to-all(f32[4,320,256]{2,1,0:T(8,128)S(1)} %bitcast.29), channel_id=1, replica_groups=mesh['x'=4,'core'=2,'y'=4,'zh'=8,'zl'=4] {'y'}, dimensions={0} | all-to-all | bytes 2621440 | tf_op jit(solution)/shard_map/all_to_all | solution.py:26
  230.0 10.5 %all_to_all.93 = f32[4,80,256]{2,1,0:T(8,128)S(1)} all-to-all(f32[4,80,256]{2,1,0:T(8,128)S(1)} %bitcast.30), channel_id=1, replica_groups=mesh['x'=4,'core'=2,'y'=4,'zh'=8,'zl'=4] {'zl'}, dimensions={0} | all-to-all | bytes 655360 | tf_op jit(solution)/shard_map/all_to_all | solution.py:26
  240.6 33.6 %all_to_all.94 = f32[8,10,256]{2,1,0:T(8,128)S(1)} all-to-all(f32[8,10,256]{2,1,0:T(8,128)S(1)} %reshape.86), channel_id=1, replica_groups=mesh['x'=4,'core'=2,'y'=4,'zh'=8,'zl'=4] {'zh'}, dimensions={0} | all-to-all | bytes 163840 | tf_op jit(solution)/shard_map/all_to_all | solution.py:26
  274.9 3.4 all-to-all-start.13
  278.3 1.6 fusion.20
  279.9 26.6 %all-to-all-done.13 = f32[8,10,256]{2,1,0:T(8,128)S(1)} async-done(((f32[8,10,256]{2,1,0:T(8,128)}), f32[8,10,256]{2,1,0:T(8,128)S(1)}, u32[]{:S(2)}, u32[]{:S(2)}) %all-to-all-start.13) | async-done | bytes 81952 | tf_op jit(solution)/shard_map/all_to_all | solution.py:20
  306.5 4.9 %all-to-all-start.16 = ((f32[8,32,512]{2,1,0:T(8,128)}), f32[8,32,512]{2,1,0:T(8,128)S(1)}, u32[]{:S(2)}, u32[]{:S(2)}) async-start(f32[8,32,512]{2,1,0:T(8,128)} %bitcast.17), calls=%async_computation.16 | async-start | bytes 1048576 | tf_op jit(solution)/shard_map/all_to_all | solution.py:26
  311.4 8.9 %all-to-all-done.16 = f32[8,32,512]{2,1,0:T(8,128)S(1)} async-done(((f32[8,32,512]{2,1,0:T(8,128)}), f32[8,32,512]{2,1,0:T(8,128)S(1)}, u32[]{:S(2)}, u32[]{:S(2)}) %all-to-all-start.16) | async-done | bytes 524320 | tf_op jit(solution)/shard_map/all_to_all | solution.py:26
  320.3 13.7 %all_to_all.95 = f32[4,80,256]{2,1,0:T(8,128)S(1)} all-to-all(f32[4,80,256]{2,1,0:T(8,128)S(1)} %broadcast_in_dim.121), channel_id=1, replica_groups=mesh['x'=4,'core'=2,'y'=4,'zh'=8,'zl'=4] {'zl'}, dimensions={0} | all-to-all | bytes 655360 | tf_op jit(solution)/shard_map/all_to_all | solution.py:20
  335.1 3.5 all-to-all-start.15
  338.7 12.5 %all_gather.3 = f32[256,512]{1,0:T(8,128)S(1)} all-gather(f32[32,512]{1,0:T(8,128)S(1)} %reduce_sum.258), channel_id=1, replica_groups=mesh['x'=4,'core'=2,'y'=4,'zh'=8,'zl'=4] {'x','core'}, dimensions={0}, use_global_device_ids=true | all-gather | bytes 589824 | tf_op jit(solution)/shard_map/all_gather | solution.py:98
  352.2 3.0 all-to-all-done.15
  355.6 1.5 fusion.10
  (89 shorter events, 24.8 us)
Async XLA Ops:
  0.6 22.1 %copy-start.2 = (bf16[256,512]{1,0:T(8,128)(2,1)S(1)}, bf16[256,512]{1,0:T(8,128)(2,1)}, u32[]{:S(2)}) copy-start(bf16[256,512]{1,0:T(8,128)(2,1)} %param.9) | copy-start | bytes 786436
  0.6 21.9 %copy-start = (bf16[1280,256]{1,0:T(8,128)(2,1)S(1)}, bf16[1280,256]{1,0:T(8,128)(2,1)}, u32[]{:S(2)}) copy-start(bf16[1280,256]{1,0:T(8,128)(2,1)} %param.7) | copy-start | bytes 1966084
  5.5 21.0 %all-to-all-start = ((f32[8,4,128]{2,1,0:T(4,128)}), f32[8,4,128]{2,1,0:T(4,128)}, u32[]{:S(2)}, u32[]{:S(2)}) async-start(f32[8,4,128]{2,1,0:T(4,128)} %broadcast_in_dim.52), calls=%async_computation | async-start | bytes 32768 | tf_op jit(solution)/shard_map/all_to_all | solution.py:20
  85.6 54.7 %copy-start.6 = (f32[256,512]{1,0:T(8,128)}, f32[256,512]{1,0:T(8,128)S(1)}, u32[]{:S(2)}) copy-start(f32[256,512]{1,0:T(8,128)S(1)} %get-tuple-element.10) | copy-start | bytes 1572868
  89.9 8.5 %all-to-all-start.4 = ((f32[4,4,128]{2,1,0:T(4,128)}), f32[4,4,128]{2,1,0:T(4,128)S(1)}, u32[]{:S(2)}, u32[]{:S(2)}) async-start(f32[4,4,128]{2,1,0:T(4,128)} %broadcast_in_dim.57), calls=%async_computation.4 | async-start | bytes 16384 | tf_op jit(solution)/shard_map/all_to_all | solution.py:20
  106.6 34.9 %copy-start.7 = (f32[1,4,5,128]{3,1,2,0:T(4,128)}, f32[1,4,5,128]{3,1,2,0:T(4,128)S(1)}, u32[]{:S(2)}) copy-start(f32[1,4,5,128]{3,1,2,0:T(4,128)S(1)} %copy.31) | copy-start | bytes 30724
  141.5 48.3 %copy-start.5 = (f32[256,512]{1,0:T(8,128)}, f32[256,512]{1,0:T(8,128)S(1)}, u32[]{:S(2)}) copy-start(f32[256,512]{1,0:T(8,128)S(1)} %get-tuple-element.8) | copy-start | bytes 1572868
  150.1 38.9 %all-to-all-start.9 = ((f32[128,2,128]{2,1,0:T(2,128)}), f32[128,2,128]{2,1,0:T(2,128)S(1)}, u32[]{:S(2)}, u32[]{:S(2)}) async-start(f32[128,2,128]{2,1,0:T(2,128)} %broadcast_in_dim.118), calls=%async_computation.9 | async-start | bytes 262144 | tf_op jit(solution)/shard_map/all_to_all | solution.py:20
  195.5 3.2 copy-start.8
  203.1 3.3 copy-start.9
  203.2 3.3 copy-start.10
  203.2 3.3 copy-start.11
  203.2 3.3 copy-start.12
  203.2 3.3 copy-start.13
  203.2 3.3 copy-start.14
  209.9 1.1 copy-start.3
  230.0 48.3 %copy-start.1 = (bf16[1280,256]{1,0:T(8,128)(2,1)S(1)}, bf16[1280,256]{1,0:T(8,128)(2,1)}, u32[]{:S(2)}) copy-start(bf16[1280,256]{1,0:T(8,128)(2,1)} %param.7) | copy-start | bytes 1966084
  230.0 48.3 %copy-start.4 = (bf16[1280,512]{0,1:T(8,128)(2,1)S(1)}, bf16[1280,512]{0,1:T(8,128)(2,1)}, u32[]{:S(2)}) copy-start(bf16[1280,512]{0,1:T(8,128)(2,1)} %copy-done.3) | copy-start | bytes 3932164
  274.9 31.7 %all-to-all-start.13 = ((f32[8,10,256]{2,1,0:T(8,128)}), f32[8,10,256]{2,1,0:T(8,128)S(1)}, u32[]{:S(2)}, u32[]{:S(2)}) async-start(f32[8,10,256]{2,1,0:T(8,128)} %broadcast_in_dim.119), calls=%async_computation.13 | async-start | bytes 262144 | tf_op jit(solution)/shard_map/all_to_all | solution.py:20
  306.5 13.8 %all-to-all-start.16 = ((f32[8,32,512]{2,1,0:T(8,128)}), f32[8,32,512]{2,1,0:T(8,128)S(1)}, u32[]{:S(2)}, u32[]{:S(2)}) async-start(f32[8,32,512]{2,1,0:T(8,128)} %bitcast.17), calls=%async_computation.16 | async-start | bytes 1048576 | tf_op jit(solution)/shard_map/all_to_all | solution.py:26
  335.1 20.0 %all-to-all-start.15 = ((f32[4,320,256]{2,1,0:T(8,128)}), f32[4,320,256]{2,1,0:T(8,128)S(1)}, u32[]{:S(2)}, u32[]{:S(2)}) async-start(f32[4,320,256]{2,1,0:T(8,128)} %broadcast_in_dim.123), calls=%async_computation.15 | async-start | bytes 2621440 | tf_op jit(solution)/shard_map/all_to_all | solution.py:20

commit v3 on v2

--- a/solution.py
+++ b/solution.py
@@ -7,7 +7,7 @@
 ITERS = 3
 DP = ("x", "core")
 PROTO = ("y", "zh", "zl")
-ALONG = ("zh", "zl")
+NEAR = ("y", "zl")
 
 
 def unit_rows(rows):
@@ -49,53 +49,56 @@
     expo = jnp.exp(logits)
     part_total = jnp.sum(expo, axis=1)
     q_mat = jnp.exp(jnp.dot(t_bf, w_bf, preferred_element_type=jnp.float32) / 0.07)
-    n_teach, n_crop, ny = t_bf.shape[0], x_bf.shape[0], lax.axis_size("y")
+    n_teach, n_crop, near = t_bf.shape[0], x_bf.shape[0], lax.axis_size(NEAR)
+    own_crops = n_crop // near
+    image_here = crop_image - lax.axis_index(DP) * img_local
+    keep_first = (crop_global != 0).astype(jnp.float32)[:, None]
+    keep_second = (crop_global != 1).astype(jnp.float32)[:, None]
     for step in range(ITERS):
         part_col = jnp.sum(q_mat, axis=0)
-        if step == 1:
-            col_tot = spread_sum(part_col, "core", "x")
-        else:
-            col_tot = spread_sum(part_col, DP)
-        q_mat = q_mat / col_tot[None, :] / total_protos
+        q_mat = q_mat / spread_sum(part_col, DP)[None, :] / total_protos
         part_row = jnp.sum(q_mat, axis=1)
         if step == 0:
-            own = jnp.pad(part_total.reshape(ny, -1), ((0, 0), (0, -(n_crop // ny) % 128)))
-            row_ny = jnp.broadcast_to(part_row[None], (ny, n_teach))
-            sent = jnp.concatenate([row_ny, own], axis=1).reshape(ny, -1, 128)
-            both = spread_sum(jnp.sum(lax.all_to_all(sent, "y", 0, 0), axis=0), ALONG)
+            own = jnp.pad(part_total.reshape(near, -1), ((0, 0), (0, -own_crops % 128)))
+            rows = jnp.broadcast_to(part_row[None], (near, n_teach))
+            sent = jnp.concatenate([rows, own], axis=1).reshape(near, -1, 128)
+            both = spread_sum(jnp.sum(lax.all_to_all(sent, NEAR, 0, 0), axis=0), "zh")
             row_tot, own_total = both[:n_teach], both[n_teach:]
         elif step == 1:
-            both = spread(jnp.concatenate([part_row, own_total]).reshape(-1, 128), "y")
-            both = both.reshape(ny, -1)
-            total = both[:, n_teach : n_teach + n_crop // ny].reshape(-1)
-            row_tot = spread_sum(jnp.sum(both[:, :n_teach], axis=0), "zl", "zh")
+            both = spread(jnp.concatenate([part_row, own_total]).reshape(-1, 128), NEAR)
+            both = both.reshape(near, -1)
+            total = both[:, n_teach : n_teach + own_crops].reshape(-1)
+            row_tot = spread_sum(jnp.sum(both[:, :n_teach], axis=0), "zh")
         else:
-            row_tot = spread_sum(part_row, PROTO)
-        q_mat = q_mat / row_tot[:, None] / teach_total
-    targets = q_mat * teach_total
+            first = jnp.take(q_mat, GLOBALS * image_here, axis=0)
+            second = jnp.take(q_mat, GLOBALS * image_here + 1, axis=0)
+            row_tot = spread_sum(part_row, NEAR, "zh")
+        if step + 1 < ITERS:
+            q_mat = q_mat / row_tot[:, None] / teach_total
+    teach_ids = lax.broadcasted_iota(jnp.int32, (1, n_teach), 1)
+
+    def of_crop(index):
+        return jnp.sum(jnp.where(index[:, None] == teach_ids, row_tot[None], 0.0), axis=1)
+
+    first = first / of_crop(GLOBALS * image_here)[:, None] / teach_total * teach_total
+    second = second / of_crop(GLOBALS * image_here + 1)[:, None] / teach_total * teach_total
     probs = expo / total[:, None]
-    image_here = crop_image - lax.axis_index(DP) * img_local
-    first = jnp.take(targets, GLOBALS * image_here, axis=0)
-    second = jnp.take(targets, GLOBALS * image_here + 1, axis=0)
-    keep_first = (crop_global != 0).astype(jnp.float32)[:, None]
-    keep_second = (crop_global != 1).astype(jnp.float32)[:, None]
     target_rows = first * keep_first + second * keep_second
     count = keep_first + keep_second
     scale_out = total_protos / 64.0
     grad_bf = (scale_out * (count * probs - target_rows) / 0.1).astype(jnp.bfloat16)
-    dxn_part = lax.dot_general(
-        grad_bf, w_bf, (((1,), (1,)), ((), ())), preferred_element_type=jnp.float32
-    )
     dwn_part = lax.dot_general(
         x_bf, grad_bf, (((0,), (0,)), ((), ())), preferred_element_type=jnp.float32
     )
-    dxn = dxn_part
-    for axes in ("y", "zl", "zh"):
+    dxn = lax.dot_general(
+        grad_bf, w_bf, (((1,), (1,)), ((), ())), preferred_element_type=jnp.float32
+    )
+    dwn_total = spread(jnp.sum(swap(dwn_part, DP), axis=0), DP).reshape(dwn_part.shape)
+    for axes in (NEAR, "zh"):
         dxn = jnp.sum(swap(dxn, axes), axis=0)
-    for axes in ("zh", "zl", "y"):
+    for axes in ("zh", NEAR):
         dxn = spread(dxn, axes).reshape(-1, dxn.shape[1])
     student_grad = x_scale * (dxn - x_norm * jnp.sum(x_norm * dxn, axis=1, keepdims=True))
-    dwn_total = lax.all_gather(jnp.sum(swap(dwn_part, DP), axis=0), DP, axis=0, tiled=True)
     proto_grad = col_scale * (
         dwn_total - w_norm * jnp.sum(w_norm * dwn_total, axis=0, keepdims=True)
     )

time: 359 us -> 368 us (1.025)
  the two profiles are of different devices: /device:TPU:2 before, /device:TPU:1 now
where the time goes in v3:
time: 368 us; the launch traced here: 367 us
  waiting for transfers between devices  169 us (46%)
  starting transfers between devices  105 us (29%)
  blocking collectives  44.3 us (12%)
  local copies, waits for them, and re-layouts  25 us (7%)
  other arithmetic  16.3 us (4%)
  matrix products  6.91 us (2%)
    all_to_all x11, waiting for transfers between devices, spread(): lax.all_to_all(jnp.broadcast_to(part[None], (n,) + part.shape), axes, 0, 0)  138 us
    all_to_all x11, starting transfers between devices, spread(): lax.all_to_all(jnp.broadcast_to(part[None], (n,) + part.shape), axes, 0, 0)  80.5 us
    all_to_all x1, blocking collectives, swap(): return lax.all_to_all(pieces, axes, 0, 0)  34.9 us
    all_to_all x2, waiting for transfers between devices, swap(): return lax.all_to_all(pieces, axes, 0, 0)  31.1 us
    all_to_all x2, starting transfers between devices, swap(): return lax.all_to_all(pieces, axes, 0, 0)  24.2 us
    all_to_all x1, blocking collectives, on_device(): both = spread_sum(jnp.sum(lax.all_to_all(sent, NEAR, 0, 0), axis=0), 'zh')  9.41 us
    gather x2, local copies, waits for them, and re-layouts, on_device(): first = jnp.take(q_mat, GLOBALS * image_here, axis=0)  7.66 us
    gather x2, local copies, waits for them, and re-layouts, on_device(): second = jnp.take(q_mat, GLOBALS * image_here + 1, axis=0)  7.64 us
  transfers between devices with their start and end apart: 13, of which 13 were waited for; matrix products, arithmetic and copies ran while one was open for 6% of the time, Pallas kernels for 0%

profile of v3, /device:TPU:1, one launch (start us, length us, event | category | flops | bytes accessed | tf_op | source)
XLA Modules:
  0.0 366.7 jit_solution(7681738856098179871)
XLA Ops:
  5.5 17.9 %all-to-all-start = ((f32[8,4,128]{2,1,0:T(4,128)}), f32[8,4,128]{2,1,0:T(4,128)}, u32[]{:S(2)}, u32[]{:S(2)}) async-start(f32[8,4,128]{2,1,0:T(4,128)} %broadcast_in_dim.66), calls=%async_computation | async-start | bytes 32768 | tf_op jit(solution)/shard_map/all_to_all | solution.py:20
  30.2 9.4 %all_to_all.75 = f32[16,3,128]{2,1,0:T(4,128)S(1)} all-to-all(f32[16,3,128]{2,1,0:T(4,128)S(1)} %reshape.85), channel_id=1, replica_groups=mesh['x'=4,'core'=2,'y'=4,'zh'=8,'zl'=4] {'y','zl'}, dimensions={0} | all-to-all | bytes 49152 | tf_op jit(solution)/shard_map/all_to_all | solution.py:65
  40.3 18.8 %all-to-all-start.2 = ((f32[8,3,128]{2,1,0:T(4,128)}), f32[8,3,128]{2,1,0:T(4,128)S(1)}, u32[]{:S(2)}, u32[]{:S(2)}) async-start(f32[8,3,128]{2,1,0:T(4,128)} %broadcast_in_dim.121), calls=%async_computation.2 | async-start | bytes 32768 | tf_op jit(solution)/shard_map/all_to_all | solution.py:20
  59.1 21.0 %all-to-all-done.2 = f32[8,3,128]{2,1,0:T(4,128)S(1)} async-done(((f32[8,3,128]{2,1,0:T(4,128)}), f32[8,3,128]{2,1,0:T(4,128)S(1)}, u32[]{:S(2)}, u32[]{:S(2)}) %all-to-all-start.2) | async-done | bytes 12320 | tf_op jit(solution)/shard_map/all_to_all | solution.py:20
  81.9 6.8 %all-to-all-start.3 = ((f32[8,4,128]{2,1,0:T(4,128)}), f32[8,4,128]{2,1,0:T(4,128)S(1)}, u32[]{:S(2)}, u32[]{:S(2)}) async-start(f32[8,4,128]{2,1,0:T(4,128)} %broadcast_in_dim.123), calls=%async_computation.3 | async-start | bytes 32768 | tf_op jit(solution)/shard_map/all_to_all | solution.py:20
  88.7 4.7 %all-to-all-done.3 = f32[8,4,128]{2,1,0:T(4,128)S(1)} async-done(((f32[8,4,128]{2,1,0:T(4,128)}), f32[8,4,128]{2,1,0:T(4,128)S(1)}, u32[]{:S(2)}, u32[]{:S(2)}) %all-to-all-start.3) | async-done | bytes 16416 | tf_op jit(solution)/shard_map/all_to_all | solution.py:20
  94.2 3.5 all-to-all-start.4
  97.7 6.8 %all-to-all-done.4 = f32[16,3,128]{2,1,0:T(4,128)S(1)} async-done(((f32[16,3,128]{2,1,0:T(4,128)}), f32[16,3,128]{2,1,0:T(4,128)S(1)}, u32[]{:S(2)}, u32[]{:S(2)}) %all-to-all-start.4) | async-done | bytes 24608 | tf_op jit(solution)/shard_map/all_to_all | solution.py:20
  105.1 3.3 all-to-all-start.5
  109.1 20.4 %all-to-all-done.5 = f32[8,2,128]{2,1,0:T(2,128)S(1)} async-done(((f32[8,2,128]{2,1,0:T(2,128)}), f32[8,2,128]{2,1,0:T(2,128)S(1)}, u32[]{:S(2)}, u32[]{:S(2)}) %all-to-all-start.5) | async-done | bytes 8224 | tf_op jit(solution)/shard_map/all_to_all | solution.py:20
  131.0 6.2 %all-to-all-start.6 = ((f32[8,4,128]{2,1,0:T(4,128)}), f32[8,4,128]{2,1,0:T(4,128)S(1)}, u32[]{:S(2)}, u32[]{:S(2)}) async-start(f32[8,4,128]{2,1,0:T(4,128)} %broadcast_in_dim.129), calls=%async_computation.6 | async-start | bytes 32768 | tf_op jit(solution)/shard_map/all_to_all | solution.py:20
  137.3 4.7 %all-to-all-done.6 = f32[8,4,128]{2,1,0:T(4,128)S(1)} async-done(((f32[8,4,128]{2,1,0:T(4,128)}), f32[8,4,128]{2,1,0:T(4,128)S(1)}, u32[]{:S(2)}, u32[]{:S(2)}) %all-to-all-start.6) | async-done | bytes 16416 | tf_op jit(solution)/shard_map/all_to_all | solution.py:20
  143.8 3.5 all-to-all-start.7
  147.3 6.7 %all-to-all-done.7 = f32[16,2,128]{2,1,0:T(2,128)S(1)} async-done(((f32[16,2,128]{2,1,0:T(2,128)}), f32[16,2,128]{2,1,0:T(2,128)S(1)}, u32[]{:S(2)}, u32[]{:S(2)}) %all-to-all-start.7) | async-done | bytes 16416 | tf_op jit(solution)/shard_map/all_to_all | solution.py:20
  154.6 3.3 all-to-all-start.8
  158.1 4.4 %gather_fusion = f32[1280,512]{1,0:T(8,128)} fusion(f32[256,512]{1,0:T(8,128)S(1)} %get-tuple-element.8, s32[2048]{0:T(1024)S(1)} %get-tuple-element.23), kind=kCustom, calls=%fused_computation.clone | custom fusion | bytes 5248000 | tf_op jit(solution)/shard_map/jit(_take)/gather | solution.py:73
  162.5 3.2 copy.18
  165.7 4.4 %gather_fusion.1 = f32[1280,512]{1,0:T(8,128)} fusion(f32[256,512]{1,0:T(8,128)S(1)} %get-tuple-element.8, s32[2048]{0:T(1024)S(1)} %get-tuple-element.22), kind=kCustom, calls=%fused_computation.1.clone | custom fusion | bytes 5248000 | tf_op jit(solution)/shard_map/jit(_take)/gather | solution.py:74
  170.1 3.3 copy.21
  173.4 5.6 %all-to-all-done.8 = f32[8,2,128]{2,1,0:T(2,128)S(1)} async-done(((f32[8,2,128]{2,1,0:T(2,128)}), f32[8,2,128]{2,1,0:T(2,128)S(1)}, u32[]{:S(2)}, u32[]{:S(2)}) %all-to-all-start.8) | async-done | bytes 8224 | tf_op jit(solution)/shard_map/all_to_all | solution.py:20
  180.1 3.5 fusion.6
  184.7 34.9 %all_to_all.76 = f32[16,80,256]{2,1,0:T(8,128)S(1)} all-to-all(f32[16,80,256]{2,1,0:T(8,128)S(1)} %bitcast.30), channel_id=1, replica_groups=mesh['x'=4,'core'=2,'y'=4,'zh'=8,'zl'=4] {'y','zl'}, dimensions={0} | all-to-all | bytes 2621440 | tf_op jit(solution)/shard_map/all_to_all | solution.py:26
  220.3 15.9 %all-to-all-start.10 = ((f32[8,10,256]{2,1,0:T(8,128)}), f32[8,10,256]{2,1,0:T(8,128)S(1)}, u32[]{:S(2)}, u32[]{:S(2)}) async-start(f32[8,10,256]{2,1,0:T(8,128)} %reshape.88), calls=%async_computation.10 | async-start | bytes 262144 | tf_op jit(solution)/shard_map/all_to_all | solution.py:26
  239.1 21.7 %all-to-all-done.10 = f32[8,10,256]{2,1,0:T(8,128)S(1)} async-done(((f32[8,10,256]{2,1,0:T(8,128)}), f32[8,10,256]{2,1,0:T(8,128)S(1)}, u32[]{:S(2)}, u32[]{:S(2)}) %all-to-all-start.10) | async-done | bytes 81952 | tf_op jit(solution)/shard_map/all_to_all | solution.py:26
  260.8 8.3 %all-to-all-start.13 = ((f32[8,32,512]{2,1,0:T(8,128)}), f32[8,32,512]{2,1,0:T(8,128)S(1)}, u32[]{:S(2)}, u32[]{:S(2)}) async-start(f32[8,32,512]{2,1,0:T(8,128)} %bitcast.15), calls=%async_computation.13 | async-start | bytes 1048576 | tf_op jit(solution)/shard_map/all_to_all | solution.py:26
  269.1 9.4 %all-to-all-done.13 = f32[8,32,512]{2,1,0:T(8,128)S(1)} async-done(((f32[8,32,512]{2,1,0:T(8,128)}), f32[8,32,512]{2,1,0:T(8,128)S(1)}, u32[]{:S(2)}, u32[]{:S(2)}) %all-to-all-start.13) | async-done | bytes 524320 | tf_op jit(solution)/shard_map/all_to_all | solution.py:26
  279.2 3.8 %all-to-all-start.11 = ((f32[8,10,256]{2,1,0:T(8,128)}), f32[8,10,256]{2,1,0:T(8,128)S(1)}, u32[]{:S(2)}, u32[]{:S(2)}) async-start(f32[8,10,256]{2,1,0:T(8,128)} %broadcast_in_dim.136), calls=%async_computation.11 | async-start | bytes 262144 | tf_op jit(solution)/shard_map/all_to_all | solution.py:20
  283.0 24.4 %all-to-all-done.11 = f32[8,10,256]{2,1,0:T(8,128)S(1)} async-done(((f32[8,10,256]{2,1,0:T(8,128)}), f32[8,10,256]{2,1,0:T(8,128)S(1)}, u32[]{:S(2)}, u32[]{:S(2)}) %all-to-all-start.11) | async-done | bytes 81952 | tf_op jit(solution)/shard_map/all_to_all | solution.py:20
  308.3 7.5 %all-to-all-start.14 = ((f32[8,32,512]{2,1,0:T(8,128)}), f32[8,32,512]{2,1,0:T(8,128)S(1)}, u32[]{:S(2)}, u32[]{:S(2)}) async-start(f32[8,32,512]{2,1,0:T(8,128)} %broadcast_in_dim.139), calls=%async_computation.14 | async-start | bytes 1048576 | tf_op jit(solution)/shard_map/all_to_all | solution.py:20
  315.8 9.4 %all-to-all-done.14 = f32[8,32,512]{2,1,0:T(8,128)S(1)} async-done(((f32[8,32,512]{2,1,0:T(8,128)}), f32[8,32,512]{2,1,0:T(8,128)S(1)}, u32[]{:S(2)}, u32[]{:S(2)}) %all-to-all-start.14) | async-done | bytes 524320 | tf_op jit(solution)/shard_map/all_to_all | solution.py:20
  326.4 5.8 %all-to-all-start.12 = ((f32[16,80,256]{2,1,0:T(8,128)}), f32[16,80,256]{2,1,0:T(8,128)S(1)}, u32[]{:S(2)}, u32[]{:S(2)}) async-start(f32[16,80,256]{2,1,0:T(8,128)} %broadcast_in_dim.138), calls=%async_computation.12 | async-start | bytes 2621440 | tf_op jit(solution)/shard_map/all_to_all | solution.py:20
  333.1 31.7 %all-to-all-done.12 = f32[16,80,256]{2,1,0:T(8,128)S(1)} async-done(((f32[16,80,256]{2,1,0:T(8,128)}), f32[16,80,256]{2,1,0:T(8,128)S(1)}, u32[]{:S(2)}, u32[]{:S(2)}) %all-to-all-start.12) | async-done | bytes 1310752 | tf_op jit(solution)/shard_map/all_to_all | solution.py:20
  (75 shorter events, 31.7 us)
Async XLA Ops:
  0.6 23.1 %copy-start.2 = (bf16[256,512]{1,0:T(8,128)(2,1)S(1)}, bf16[256,512]{1,0:T(8,128)(2,1)}, u32[]{:S(2)}) copy-start(bf16[256,512]{1,0:T(8,128)(2,1)} %param.9) | copy-start | bytes 786436
  0.6 22.8 %copy-start = (bf16[1280,256]{1,0:T(8,128)(2,1)S(1)}, bf16[1280,256]{1,0:T(8,128)(2,1)}, u32[]{:S(2)}) copy-start(bf16[1280,256]{1,0:T(8,128)(2,1)} %param.7) | copy-start | bytes 1966084
  5.5 22.7 %all-to-all-start = ((f32[8,4,128]{2,1,0:T(4,128)}), f32[8,4,128]{2,1,0:T(4,128)}, u32[]{:S(2)}, u32[]{:S(2)}) async-start(f32[8,4,128]{2,1,0:T(4,128)} %broadcast_in_dim.66), calls=%async_computation | async-start | bytes 32768 | tf_op jit(solution)/shard_map/all_to_all | solution.py:20
  25.0 72.7 %copy-start.5 = (s32[1280]{0:T(1024)S(1)}, s32[1280]{0:T(1024)}, u32[]{:S(2)}) copy-start(s32[1280]{0:T(1024)} %param.10) | copy-start | bytes 15364
  29.0 79.5 %copy-start.4 = (s32[1280]{0:T(1024)S(1)}, s32[1280]{0:T(1024)}, u32[]{:S(2)}) copy-start(s32[1280]{0:T(1024)} %param.11) | copy-start | bytes 15364
  40.3 39.8 %all-to-all-start.2 = ((f32[8,3,128]{2,1,0:T(4,128)}), f32[8,3,128]{2,1,0:T(4,128)S(1)}, u32[]{:S(2)}, u32[]{:S(2)}) async-start(f32[8,3,128]{2,1,0:T(4,128)} %broadcast_in_dim.121), calls=%async_computation.2 | async-start | bytes 32768 | tf_op jit(solution)/shard_map/all_to_all | solution.py:20
  81.9 11.5 %all-to-all-start.3 = ((f32[8,4,128]{2,1,0:T(4,128)}), f32[8,4,128]{2,1,0:T(4,128)S(1)}, u32[]{:S(2)}, u32[]{:S(2)}) async-start(f32[8,4,128]{2,1,0:T(4,128)} %broadcast_in_dim.123), calls=%async_computation.3 | async-start | bytes 32768 | tf_op jit(solution)/shard_map/all_to_all | solution.py:20
  94.2 10.3 %all-to-all-start.4 = ((f32[16,3,128]{2,1,0:T(4,128)}), f32[16,3,128]{2,1,0:T(4,128)S(1)}, u32[]{:S(2)}, u32[]{:S(2)}) async-start(f32[16,3,128]{2,1,0:T(4,128)} %broadcast_in_dim.125), calls=%async_computation.4 | async-start | bytes 65536 | tf_op jit(solution)/shard_map/all_to_all | solution.py:20
  105.1 24.3 %all-to-all-start.5 = ((f32[8,2,128]{2,1,0:T(2,128)}), f32[8,2,128]{2,1,0:T(2,128)S(1)}, u32[]{:S(2)}, u32[]{:S(2)}) async-start(f32[8,2,128]{2,1,0:T(2,128)} %broadcast_in_dim.127), calls=%async_computation.5 | async-start | bytes 16384 | tf_op jit(solution)/shard_map/all_to_all | solution.py:20
  131.0 10.9 %all-to-all-start.6 = ((f32[8,4,128]{2,1,0:T(4,128)}), f32[8,4,128]{2,1,0:T(4,128)S(1)}, u32[]{:S(2)}, u32[]{:S(2)}) async-start(f32[8,4,128]{2,1,0:T(4,128)} %broadcast_in_dim.129), calls=%async_computation.6 | async-start | bytes 32768 | tf_op jit(solution)/shard_map/all_to_all | solution.py:20
  143.8 10.2 %all-to-all-start.7 = ((f32[16,2,128]{2,1,0:T(2,128)}), f32[16,2,128]{2,1,0:T(2,128)S(1)}, u32[]{:S(2)}, u32[]{:S(2)}) async-start(f32[16,2,128]{2,1,0:T(2,128)} %broadcast_in_dim.131), calls=%async_computation.7 | async-start | bytes 32768 | tf_op jit(solution)/shard_map/all_to_all | solution.py:20
  154.6 24.3 %all-to-all-start.8 = ((f32[8,2,128]{2,1,0:T(2,128)}), f32[8,2,128]{2,1,0:T(2,128)S(1)}, u32[]{:S(2)}, u32[]{:S(2)}) async-start(f32[8,2,128]{2,1,0:T(2,128)} %broadcast_in_dim.132), calls=%async_computation.8 | async-start | bytes 16384 | tf_op jit(solution)/shard_map/all_to_all | solution.py:20
  170.1 10.0 %copy-start.6 = (pred[1280]{0:T(1024)(128)(4,1)S(1)}, pred[1280]{0:T(1024)(128)(4,1)}, u32[]{:S(2)}) copy-start(pred[1280]{0:T(1024)(128)(4,1)} %get-tuple-element.24) | copy-start | bytes 3844
  183.7 1.1 copy-start.3
  219.6 16.6 %copy-start.1 = (bf16[1280,256]{1,0:T(8,128)(2,1)S(1)}, bf16[1280,256]{1,0:T(8,128)(2,1)}, u32[]{:S(2)}) copy-start(bf16[1280,256]{1,0:T(8,128)(2,1)} %param.7) | copy-start | bytes 1966084
  220.3 40.5 %all-to-all-start.10 = ((f32[8,10,256]{2,1,0:T(8,128)}), f32[8,10,256]{2,1,0:T(8,128)S(1)}, u32[]{:S(2)}, u32[]{:S(2)}) async-start(f32[8,10,256]{2,1,0:T(8,128)} %reshape.88), calls=%async_computation.10 | async-start | bytes 262144 | tf_op jit(solution)/shard_map/all_to_all | solution.py:26
  260.8 17.7 %all-to-all-start.13 = ((f32[8,32,512]{2,1,0:T(8,128)}), f32[8,32,512]{2,1,0:T(8,128)S(1)}, u32[]{:S(2)}, u32[]{:S(2)}) async-start(f32[8,32,512]{2,1,0:T(8,128)} %bitcast.15), calls=%async_computation.13 | async-start | bytes 1048576 | tf_op jit(solution)/shard_map/all_to_all | solution.py:26
  279.2 28.2 %all-to-all-start.11 = ((f32[8,10,256]{2,1,0:T(8,128)}), f32[8,10,256]{2,1,0:T(8,128)S(1)}, u32[]{:S(2)}, u32[]{:S(2)}) async-start(f32[8,10,256]{2,1,0:T(8,128)} %broadcast_in_dim.136), calls=%async_computation.11 | async-start | bytes 262144 | tf_op jit(solution)/shard_map/all_to_all | solution.py:20
  308.3 16.9 %all-to-all-start.14 = ((f32[8,32,512]{2,1,0:T(8,128)}), f32[8,32,512]{2,1,0:T(8,128)S(1)}, u32[]{:S(2)}, u32[]{:S(2)}) async-start(f32[8,32,512]{2,1,0:T(8,128)} %broadcast_in_dim.139), calls=%async_computation.14 | async-start | bytes 1048576 | tf_op jit(solution)/shard_map/all_to_all | solution.py:20
  326.4 38.4 %all-to-all-start.12 = ((f32[16,80,256]{2,1,0:T(8,128)}), f32[16,80,256]{2,1,0:T(8,128)S(1)}, u32[]{:S(2)}, u32[]{:S(2)}) async-start(f32[16,80,256]{2,1,0:T(8,128)} %broadcast_in_dim.138), calls=%async_computation.12 | async-start | bytes 2621440 | tf_op jit(solution)/shard_map/all_to_all | solution.py:20

commit v4 on v3

--- a/solution.py
+++ b/solution.py
@@ -2,6 +2,7 @@
 import jax.numpy as jnp
 from jax import lax
 from jax.sharding import Mesh, PartitionSpec as P
+
 
 GLOBALS = 2
 ITERS = 3
@@ -33,6 +34,32 @@
     return rows.reshape(-1)
 
 
+def shifted(part, axis, step):
+    n = lax.axis_size(axis)
+    return lax.ppermute(part, axis, [(i, (i + step) % n) for i in range(n)])
+
+
+def dwn_reduce(part):
+    core, x, nx = lax.axis_index("core"), lax.axis_index("x"), lax.axis_size("x")
+    half = part.shape[0] // 2
+    piece = half // nx
+
+    def rows(arr, start, size):
+        return lax.dynamic_slice_in_dim(arr, start * size, size, 0)
+
+    mine = rows(part, core, half) + shifted(rows(part, 1 - core, half), "core", 1)
+    own = rows(mine, x, piece)
+    for step in range(1, nx):
+        own = own + shifted(rows(mine, (x + step) % nx, piece), "x", step)
+    got = [own] + [shifted(own, "x", step) for step in range(1, nx)]
+    back = got[:1] + got[:0:-1]
+    start = (nx - x) % nx * piece
+    mine = lax.dynamic_slice_in_dim(jnp.concatenate(back + back, axis=0), start, half, 0)
+    other = shifted(mine, "core", 1)
+    low, high = jnp.where(core == 0, mine, other), jnp.where(core == 0, other, mine)
+    return jnp.concatenate([low, high], axis=0)
+
+
 def on_device(student_rows, teacher_rows, prototypes, crop_image, crop_global):
     total_protos = lax.axis_size(PROTO) * prototypes.shape[1]
     img_local = teacher_rows.shape[0] // GLOBALS
@@ -41,7 +68,7 @@
     col_scale = lax.rsqrt(jnp.sum(weights * weights, axis=0, keepdims=True) + 1e-06)
     w_norm = weights * col_scale
     w_bf = w_norm.astype(jnp.bfloat16)
-    t_norm, t_scale = unit_rows(teacher_rows.astype(jnp.float32))
+    t_norm, _ = unit_rows(teacher_rows.astype(jnp.float32))
     t_bf = t_norm.astype(jnp.bfloat16)
     x_norm, x_scale = unit_rows(student_rows.astype(jnp.float32))
     x_bf = x_norm.astype(jnp.bfloat16)
@@ -93,11 +120,20 @@
     dxn = lax.dot_general(
         grad_bf, w_bf, (((1,), (1,)), ((), ())), preferred_element_type=jnp.float32
     )
-    dwn_total = spread(jnp.sum(swap(dwn_part, DP), axis=0), DP).reshape(dwn_part.shape)
-    for axes in (NEAR, "zh"):
-        dxn = jnp.sum(swap(dxn, axes), axis=0)
-    for axes in ("zh", NEAR):
-        dxn = spread(dxn, axes).reshape(-1, dxn.shape[1])
+    dwn_total = dwn_reduce(dwn_part)
+    for axes in ("y", "zl"):
+        got = swap(dxn, axes)
+        dxn = jnp.sum(got, axis=0)
+    rows, lanes = dxn.shape[0], dxn.shape[1] // 2
+    dxn = jnp.concatenate([dxn[:, :lanes], dxn[:, lanes:]], axis=0)
+    got = swap(dxn, "zh")
+    dxn = jnp.sum(got, axis=0)
+    got = spread(dxn, "zh")
+    dxn = got.reshape(-1, lanes)
+    dxn = jnp.concatenate([dxn[:rows], dxn[rows:]], axis=1)
+    for axes in ("zl", "y"):
+        got = spread(dxn, axes)
+        dxn = got.reshape(-1, dxn.shape[1])
     student_grad = x_scale * (dxn - x_norm * jnp.sum(x_norm * dxn, axis=1, keepdims=True))
     proto_grad = col_scale * (
         dwn_total - w_norm * jnp.sum(w_norm * dwn_total, axis=0, keepdims=True)
@@ -111,6 +147,7 @@
     split = (nx, dp // nx, ny, proto // ny // nzl, nzl)
     fine = Mesh(mesh.devices.reshape(split), ("x", "core", "y", "zh", "zl"))
     placed = (P(DP, None), P(DP, None), P(None, PROTO), P(DP), P(DP))
+
     return jax.shard_map(
         on_device,
         mesh=fine,

time: 368 us -> 344 us (0.935)
  the two profiles are of different devices: /device:TPU:1 before, /device:TPU:32 now
where the time goes in v4:
time: 344 us; the launch traced here: 342 us
  waiting for transfers between devices  123 us (36%)
  blocking collectives  91.1 us (26%)
  starting transfers between devices  80.4 us (23%)
  local copies, waits for them, and re-layouts  24.3 us (7%)
  other arithmetic  17.4 us (5%)
  matrix products  4.8 us (1%)
    all_to_all x11, waiting for transfers between devices, spread(): lax.all_to_all(jnp.broadcast_to(part[None], (n,) + part.shape), axes, 0, 0)  112 us
    all_to_all x3, blocking collectives, swap(): return lax.all_to_all(pieces, axes, 0, 0)  69.8 us
    all_to_all x11, starting transfers between devices, spread(): lax.all_to_all(jnp.broadcast_to(part[None], (n,) + part.shape), axes, 0, 0)  57.8 us
    ppermute x8, starting transfers between devices, shifted(): return lax.ppermute(part, axis, [(i, (i + step) % n) for i in range(n)])  22.6 us
    all_to_all x1, blocking collectives, on_device(): both = spread_sum(jnp.sum(lax.all_to_all(sent, NEAR, 0, 0), axis=0), 'zh')  21.3 us
    ppermute x8, waiting for transfers between devices, shifted(): return lax.ppermute(part, axis, [(i, (i + step) % n) for i in range(n)])  11.6 us
    gather x2, local copies, waits for them, and re-layouts, on_device(): first = jnp.take(q_mat, GLOBALS * image_here, axis=0)  7.66 us
    gather x2, local copies, waits for them, and re-layouts, on_device(): second = jnp.take(q_mat, GLOBALS * image_here + 1, axis=0)  7.64 us
  transfers between devices with their start and end apart: 19, of which 16 were waited for; matrix products, arithmetic and copies ran while one was open for 6% of the time, Pallas kernels for 0%

profile of v4, /device:TPU:32, one launch (start us, length us, event | category | flops | bytes accessed | tf_op | source)
XLA Modules:
  0.0 342.4 jit_solution(15571150157362851615)
XLA Ops:
  5.5 4.3 %all-to-all-start = ((f32[8,4,128]{2,1,0:T(4,128)}), f32[8,4,128]{2,1,0:T(4,128)}, u32[]{:S(2)}, u32[]{:S(2)}) async-start(f32[8,4,128]{2,1,0:T(4,128)} %broadcast_in_dim.66), calls=%async_computation | async-start | bytes 32768 | tf_op jit(solution)/shard_map/all_to_all | solution.py:21
  17.3 21.3 %all_to_all.75 = f32[16,3,128]{2,1,0:T(4,128)S(1)} all-to-all(f32[16,3,128]{2,1,0:T(4,128)S(1)} %reshape.85), channel_id=1, replica_groups=mesh['x'=4,'core'=2,'y'=4,'zh'=8,'zl'=4] {'y','zl'}, dimensions={0} | all-to-all | bytes 49152 | tf_op jit(solution)/shard_map/all_to_all | solution.py:92
  39.2 19.4 %all-to-all-start.2 = ((f32[8,3,128]{2,1,0:T(4,128)}), f32[8,3,128]{2,1,0:T(4,128)S(1)}, u32[]{:S(2)}, u32[]{:S(2)}) async-start(f32[8,3,128]{2,1,0:T(4,128)} %broadcast_in_dim.121), calls=%async_computation.2 | async-start | bytes 32768 | tf_op jit(solution)/shard_map/all_to_all | solution.py:21
  58.5 22.2 %all-to-all-done.2 = f32[8,3,128]{2,1,0:T(4,128)S(1)} async-done(((f32[8,3,128]{2,1,0:T(4,128)}), f32[8,3,128]{2,1,0:T(4,128)S(1)}, u32[]{:S(2)}, u32[]{:S(2)}) %all-to-all-start.2) | async-done | bytes 12320 | tf_op jit(solution)/shard_map/all_to_all | solution.py:21
  82.6 3.3 all-to-all-start.3
  85.9 5.3 %all-to-all-done.3 = f32[8,4,128]{2,1,0:T(4,128)S(1)} async-done(((f32[8,4,128]{2,1,0:T(4,128)}), f32[8,4,128]{2,1,0:T(4,128)S(1)}, u32[]{:S(2)}, u32[]{:S(2)}) %all-to-all-start.3) | async-done | bytes 16416 | tf_op jit(solution)/shard_map/all_to_all | solution.py:21
  92.0 4.9 %all-to-all-start.4 = ((f32[16,3,128]{2,1,0:T(4,128)}), f32[16,3,128]{2,1,0:T(4,128)S(1)}, u32[]{:S(2)}, u32[]{:S(2)}) async-start(f32[16,3,128]{2,1,0:T(4,128)} %broadcast_in_dim.125), calls=%async_computation.4 | async-start | bytes 65536 | tf_op jit(solution)/shard_map/all_to_all | solution.py:21
  96.8 6.6 %all-to-all-done.4 = f32[16,3,128]{2,1,0:T(4,128)S(1)} async-done(((f32[16,3,128]{2,1,0:T(4,128)}), f32[16,3,128]{2,1,0:T(4,128)S(1)}, u32[]{:S(2)}, u32[]{:S(2)}) %all-to-all-start.4) | async-done | bytes 24608 | tf_op jit(solution)/shard_map/all_to_all | solution.py:21
  104.0 3.3 all-to-all-start.5
  108.0 21.5 %all-to-all-done.5 = f32[8,2,128]{2,1,0:T(2,128)S(1)} async-done(((f32[8,2,128]{2,1,0:T(2,128)}), f32[8,2,128]{2,1,0:T(2,128)S(1)}, u32[]{:S(2)}, u32[]{:S(2)}) %all-to-all-start.5) | async-done | bytes 8224 | tf_op jit(solution)/shard_map/all_to_all | solution.py:21
  131.0 3.3 all-to-all-start.6
  134.4 5.3 %all-to-all-done.6 = f32[8,4,128]{2,1,0:T(4,128)S(1)} async-done(((f32[8,4,128]{2,1,0:T(4,128)}), f32[8,4,128]{2,1,0:T(4,128)S(1)}, u32[]{:S(2)}, u32[]{:S(2)}) %all-to-all-start.6) | async-done | bytes 16416 | tf_op jit(solution)/shard_map/all_to_all | solution.py:21
  141.5 4.9 %all-to-all-start.7 = ((f32[16,2,128]{2,1,0:T(2,128)}), f32[16,2,128]{2,1,0:T(2,128)S(1)}, u32[]{:S(2)}, u32[]{:S(2)}) async-start(f32[16,2,128]{2,1,0:T(2,128)} %broadcast_in_dim.131), calls=%async_computation.7 | async-start | bytes 32768 | tf_op jit(solution)/shard_map/all_to_all | solution.py:21
  146.4 6.6 %all-to-all-done.7 = f32[16,2,128]{2,1,0:T(2,128)S(1)} async-done(((f32[16,2,128]{2,1,0:T(2,128)}), f32[16,2,128]{2,1,0:T(2,128)S(1)}, u32[]{:S(2)}, u32[]{:S(2)}) %all-to-all-start.7) | async-done | bytes 16416 | tf_op jit(solution)/shard_map/all_to_all | solution.py:21
  153.6 3.3 all-to-all-start.8
  157.0 4.4 %gather_fusion = f32[1280,512]{1,0:T(8,128)} fusion(f32[256,512]{1,0:T(8,128)S(1)} %get-tuple-element.10, s32[2048]{0:T(1024)S(1)} %get-tuple-element.34), kind=kCustom, calls=%fused_computation.clone | custom fusion | bytes 5248000 | tf_op jit(solution)/shard_map/jit(_take)/gather | solution.py:100
  161.5 3.2 copy.18
  164.7 4.4 %gather_fusion.1 = f32[1280,512]{1,0:T(8,128)} fusion(f32[256,512]{1,0:T(8,128)S(1)} %get-tuple-element.10, s32[2048]{0:T(1024)S(1)} %get-tuple-element.33), kind=kCustom, calls=%fused_computation.1.clone | custom fusion | bytes 5248000 | tf_op jit(solution)/shard_map/jit(_take)/gather | solution.py:101
  169.1 3.3 copy.21
  172.3 6.7 %all-to-all-done.8 = f32[8,2,128]{2,1,0:T(2,128)S(1)} async-done(((f32[8,2,128]{2,1,0:T(2,128)}), f32[8,2,128]{2,1,0:T(2,128)S(1)}, u32[]{:S(2)}, u32[]{:S(2)}) %all-to-all-start.8) | async-done | bytes 8224 | tf_op jit(solution)/shard_map/all_to_all | solution.py:21
  180.2 3.5 %fusion.6 = bf16[1280,512]{0,1:T(8,128)(2,1)S(1)} fusion(f32[1280,512]{0,1:T(8,128)} %copy.21, f32[1280,512]{0,1:T(8,128)} %copy.18, f32[1280,512]{0,1:T(8,128)S(1)} %get-tuple-element.30, f32[1280]{0:T(1024)S(1)} %get-tuple-element.25, f32[1280]{0:T(1024)S(1)} %get-tuple-element.4, f32[1280]{0:T(1024)S(1)} %get-tuple-element.24, ...), kind=kLoop, calls=%fused_computation.11 | loop fusion | flops 7864320 | bytes 9208320 | tf_op jit(solution)/shard_map/convert_element_type | solution.py:116
  184.8 18.3 %all_to_all.76 = f32[4,320,256]{2,1,0:T(8,128)S(1)} all-to-all(f32[4,320,256]{2,1,0:T(8,128)S(1)} %bitcast.28), channel_id=1, replica_groups=mesh['x'=4,'core'=2,'y'=4,'zh'=8,'zl'=4] {'y'}, dimensions={0} | all-to-all | bytes 2621440 | tf_op jit(solution)/shard_map/all_to_all | solution.py:27
  203.2 10.7 %all_to_all.77 = f32[4,80,256]{2,1,0:T(8,128)S(1)} all-to-all(f32[4,80,256]{2,1,0:T(8,128)S(1)} %bitcast.30), channel_id=1, replica_groups=mesh['x'=4,'core'=2,'y'=4,'zh'=8,'zl'=4] {'zl'}, dimensions={0} | all-to-all | bytes 655360 | tf_op jit(solution)/shard_map/all_to_all | solution.py:27
  213.9 40.9 %all_to_all.78 = f32[8,20,128]{2,1,0:T(8,128)S(1)} all-to-all(f32[8,20,128]{2,1,0:T(8,128)S(1)} %reshape.89), channel_id=1, replica_groups=mesh['x'=4,'core'=2,'y'=4,'zh'=8,'zl'=4] {'zh'}, dimensions={0} | all-to-all | bytes 163840 | tf_op jit(solution)/shard_map/all_to_all | solution.py:27
  255.5 3.4 all-to-all-start.12
  258.9 24.4 %all-to-all-done.12 = f32[8,20,128]{2,1,0:T(8,128)S(1)} async-done(((f32[8,20,128]{2,1,0:T(8,128)}), f32[8,20,128]{2,1,0:T(8,128)S(1)}, u32[]{:S(2)}, u32[]{:S(2)}) %all-to-all-start.12) | async-done | bytes 81952 | tf_op jit(solution)/shard_map/all_to_all | solution.py:21
  284.1 4.1 %all-to-all-start.13 = ((f32[4,80,256]{2,1,0:T(8,128)}), f32[4,80,256]{2,1,0:T(8,128)S(1)}, u32[]{:S(2)}, u32[]{:S(2)}) async-start(f32[4,80,256]{2,1,0:T(8,128)} %broadcast_in_dim.137), calls=%async_computation.13 | async-start | bytes 655360 | tf_op jit(solution)/shard_map/all_to_all | solution.py:21
  295.1 4.0 %collective-permute-start.2 = (f32[32,512]{1,0:T(8,128)S(1)}, f32[32,512]{1,0:T(8,128)S(1)}, u32[]{:S(2)}, u32[]{:S(2)}) collective-permute-start(f32[32,512]{1,0:T(8,128)S(1)} %get-tuple-element.19), channel_id=1, source_target_pairs={{0,512},{256,768},{512,0},{768,256},{1,513},{257,769},{513,1},{769... | collective-permute-start | bytes 196616 | tf_op jit(solution)/shard_map/ppermute | solution.py:39
  305.2 4.3 %collective-permute-start.4 = (f32[32,512]{1,0:T(8,128)S(1)}, f32[32,512]{1,0:T(8,128)S(1)}, u32[]{:S(2)}, u32[]{:S(2)}) collective-permute-start(f32[32,512]{1,0:T(8,128)S(1)} %get-tuple-element.6), channel_id=1, source_target_pairs={{0,768},{256,0},{512,256},{768,512},{1,769},{257,1},{513,257},{769... | collective-permute-start | bytes 196616 | tf_op jit(solution)/shard_map/ppermute | solution.py:39
  309.5 3.1 collective-permute-start.5
  321.2 3.5 %all-to-all-start.14 = ((f32[4,320,256]{2,1,0:T(8,128)}), f32[4,320,256]{2,1,0:T(8,128)S(1)}, u32[]{:S(2)}, u32[]{:S(2)}) async-start(f32[4,320,256]{2,1,0:T(8,128)} %broadcast_in_dim.139), calls=%async_computation.14 | async-start | bytes 2621440 | tf_op jit(solution)/shard_map/all_to_all | solution.py:21
  330.4 10.1 %all-to-all-done.14 = f32[4,320,256]{2,1,0:T(8,128)S(1)} async-done(((f32[4,320,256]{2,1,0:T(8,128)}), f32[4,320,256]{2,1,0:T(8,128)S(1)}, u32[]{:S(2)}, u32[]{:S(2)}) %all-to-all-start.14) | async-done | bytes 1310752 | tf_op jit(solution)/shard_map/all_to_all | solution.py:21
  (109 shorter events, 53.6 us)
Async XLA Ops:
  0.6 9.5 %copy-start.2 = (bf16[256,512]{1,0:T(8,128)(2,1)S(1)}, bf16[256,512]{1,0:T(8,128)(2,1)}, u32[]{:S(2)}) copy-start(bf16[256,512]{1,0:T(8,128)(2,1)} %param.9) | copy-start | bytes 786436
  0.6 9.2 %copy-start = (bf16[1280,256]{1,0:T(8,128)(2,1)S(1)}, bf16[1280,256]{1,0:T(8,128)(2,1)}, u32[]{:S(2)}) copy-start(bf16[1280,256]{1,0:T(8,128)(2,1)} %param.7) | copy-start | bytes 1966084
  5.5 9.8 %all-to-all-start = ((f32[8,4,128]{2,1,0:T(4,128)}), f32[8,4,128]{2,1,0:T(4,128)}, u32[]{:S(2)}, u32[]{:S(2)}) async-start(f32[8,4,128]{2,1,0:T(4,128)} %broadcast_in_dim.66), calls=%async_computation | async-start | bytes 32768 | tf_op jit(solution)/shard_map/all_to_all | solution.py:21
  11.4 85.4 %copy-start.6 = (s32[1280]{0:T(1024)S(1)}, s32[1280]{0:T(1024)}, u32[]{:S(2)}) copy-start(s32[1280]{0:T(1024)} %param.10) | copy-start | bytes 15364
  16.0 91.4 %copy-start.5 = (s32[1280]{0:T(1024)S(1)}, s32[1280]{0:T(1024)}, u32[]{:S(2)}) copy-start(s32[1280]{0:T(1024)} %param.11) | copy-start | bytes 15364
  39.2 41.6 %all-to-all-start.2 = ((f32[8,3,128]{2,1,0:T(4,128)}), f32[8,3,128]{2,1,0:T(4,128)S(1)}, u32[]{:S(2)}, u32[]{:S(2)}) async-start(f32[8,3,128]{2,1,0:T(4,128)} %broadcast_in_dim.121), calls=%async_computation.2 | async-start | bytes 32768 | tf_op jit(solution)/shard_map/all_to_all | solution.py:21
  82.6 8.6 %all-to-all-start.3 = ((f32[8,4,128]{2,1,0:T(4,128)}), f32[8,4,128]{2,1,0:T(4,128)S(1)}, u32[]{:S(2)}, u32[]{:S(2)}) async-start(f32[8,4,128]{2,1,0:T(4,128)} %broadcast_in_dim.123), calls=%async_computation.3 | async-start | bytes 32768 | tf_op jit(solution)/shard_map/all_to_all | solution.py:21
  92.0 11.4 %all-to-all-start.4 = ((f32[16,3,128]{2,1,0:T(4,128)}), f32[16,3,128]{2,1,0:T(4,128)S(1)}, u32[]{:S(2)}, u32[]{:S(2)}) async-start(f32[16,3,128]{2,1,0:T(4,128)} %broadcast_in_dim.125), calls=%async_computation.4 | async-start | bytes 65536 | tf_op jit(solution)/shard_map/all_to_all | solution.py:21
  104.0 25.4 %all-to-all-start.5 = ((f32[8,2,128]{2,1,0:T(2,128)}), f32[8,2,128]{2,1,0:T(2,128)S(1)}, u32[]{:S(2)}, u32[]{:S(2)}) async-start(f32[8,2,128]{2,1,0:T(2,128)} %broadcast_in_dim.127), calls=%async_computation.5 | async-start | bytes 16384 | tf_op jit(solution)/shard_map/all_to_all | solution.py:21
  131.0 8.6 %all-to-all-start.6 = ((f32[8,4,128]{2,1,0:T(4,128)}), f32[8,4,128]{2,1,0:T(4,128)S(1)}, u32[]{:S(2)}, u32[]{:S(2)}) async-start(f32[8,4,128]{2,1,0:T(4,128)} %broadcast_in_dim.129), calls=%async_computation.6 | async-start | bytes 32768 | tf_op jit(solution)/shard_map/all_to_all | solution.py:21
  141.5 11.5 %all-to-all-start.7 = ((f32[16,2,128]{2,1,0:T(2,128)}), f32[16,2,128]{2,1,0:T(2,128)S(1)}, u32[]{:S(2)}, u32[]{:S(2)}) async-start(f32[16,2,128]{2,1,0:T(2,128)} %broadcast_in_dim.131), calls=%async_computation.7 | async-start | bytes 32768 | tf_op jit(solution)/shard_map/all_to_all | solution.py:21
  153.6 25.4 %all-to-all-start.8 = ((f32[8,2,128]{2,1,0:T(2,128)}), f32[8,2,128]{2,1,0:T(2,128)S(1)}, u32[]{:S(2)}, u32[]{:S(2)}) async-start(f32[8,2,128]{2,1,0:T(2,128)} %broadcast_in_dim.132), calls=%async_computation.8 | async-start | bytes 16384 | tf_op jit(solution)/shard_map/all_to_all | solution.py:21
  169.1 11.1 %copy-start.7 = (pred[1280]{0:T(1024)(128)(4,1)S(1)}, pred[1280]{0:T(1024)(128)(4,1)}, u32[]{:S(2)}) copy-start(pred[1280]{0:T(1024)(128)(4,1)} %get-tuple-element.35) | copy-start | bytes 3844
  183.7 1.1 copy-start.3
  213.9 74.3 %copy-start.1 = (bf16[1280,256]{1,0:T(8,128)(2,1)S(1)}, bf16[1280,256]{1,0:T(8,128)(2,1)}, u32[]{:S(2)}) copy-start(bf16[1280,256]{1,0:T(8,128)(2,1)} %param.7) | copy-start | bytes 1966084
  213.9 74.3 %copy-start.4 = (bf16[1280,512]{0,1:T(8,128)(2,1)S(1)}, bf16[1280,512]{0,1:T(8,128)(2,1)}, u32[]{:S(2)}) copy-start(bf16[1280,512]{0,1:T(8,128)(2,1)} %copy-done.3) | copy-start | bytes 3932164
  255.5 27.8 %all-to-all-start.12 = ((f32[8,20,128]{2,1,0:T(8,128)}), f32[8,20,128]{2,1,0:T(8,128)S(1)}, u32[]{:S(2)}, u32[]{:S(2)}) async-start(f32[8,20,128]{2,1,0:T(8,128)} %broadcast_in_dim.136), calls=%async_computation.12 | async-start | bytes 196608 | tf_op jit(solution)/shard_map/all_to_all | solution.py:21
  284.1 36.0 %all-to-all-start.13 = ((f32[4,80,256]{2,1,0:T(8,128)}), f32[4,80,256]{2,1,0:T(8,128)S(1)}, u32[]{:S(2)}, u32[]{:S(2)}) async-start(f32[4,80,256]{2,1,0:T(8,128)} %broadcast_in_dim.137), calls=%async_computation.13 | async-start | bytes 655360 | tf_op jit(solution)/shard_map/all_to_all | solution.py:21
  289.1 3.4 %collective-permute-start = (f32[128,512]{1,0:T(8,128)S(1)}, f32[128,512]{1,0:T(8,128)S(1)}, u32[]{:S(2)}, u32[]{:S(2)}) collective-permute-start(f32[128,512]{1,0:T(8,128)S(1)} %constant_dynamic-slice_fusion.4), channel_id=1, source_target_pairs={{0,128},{128,0},{1,129},{129,1},{2,130},{130,2},{3,131},{131,3},{4... | collective-permute-start | bytes 786440 | tf_op jit(solution)/shard_map/ppermute | solution.py:39
  292.6 9.5 %collective-permute-start.1 = (f32[32,512]{1,0:T(8,128)S(1)}, f32[32,512]{1,0:T(8,128)S(1)}, u32[]{:S(2)}, u32[]{:S(2)}) collective-permute-start(f32[32,512]{1,0:T(8,128)S(1)} %get-tuple-element.17), channel_id=1, source_target_pairs={{0,256},{256,512},{512,768},{768,0},{1,257},{257,513},{513,769},{7... | collective-permute-start | bytes 196616 | tf_op jit(solution)/shard_map/ppermute | solution.py:39
  295.1 7.7 %collective-permute-start.2 = (f32[32,512]{1,0:T(8,128)S(1)}, f32[32,512]{1,0:T(8,128)S(1)}, u32[]{:S(2)}, u32[]{:S(2)}) collective-permute-start(f32[32,512]{1,0:T(8,128)S(1)} %get-tuple-element.19), channel_id=1, source_target_pairs={{0,512},{256,768},{512,0},{768,256},{1,513},{257,769},{513,1},{769... | collective-permute-start | bytes 196616 | tf_op jit(solution)/shard_map/ppermute | solution.py:39
  299.0 6.2 %collective-permute-start.3 = (f32[32,512]{1,0:T(8,128)S(1)}, f32[32,512]{1,0:T(8,128)S(1)}, u32[]{:S(2)}, u32[]{:S(2)}) collective-permute-start(f32[32,512]{1,0:T(8,128)S(1)} %get-tuple-element.18), channel_id=1, source_target_pairs={{0,768},{256,0},{512,256},{768,512},{1,769},{257,1},{513,257},{769... | collective-permute-start | bytes 196616 | tf_op jit(solution)/shard_map/ppermute | solution.py:39
  305.2 9.3 %collective-permute-start.4 = (f32[32,512]{1,0:T(8,128)S(1)}, f32[32,512]{1,0:T(8,128)S(1)}, u32[]{:S(2)}, u32[]{:S(2)}) collective-permute-start(f32[32,512]{1,0:T(8,128)S(1)} %get-tuple-element.6), channel_id=1, source_target_pairs={{0,768},{256,0},{512,256},{768,512},{1,769},{257,1},{513,257},{769... | collective-permute-start | bytes 196616 | tf_op jit(solution)/shard_map/ppermute | solution.py:39
  309.5 7.8 %collective-permute-start.5 = (f32[32,512]{1,0:T(8,128)S(1)}, f32[32,512]{1,0:T(8,128)S(1)}, u32[]{:S(2)}, u32[]{:S(2)}) collective-permute-start(f32[32,512]{1,0:T(8,128)S(1)} %get-tuple-element.6), channel_id=1, source_target_pairs={{0,512},{256,768},{512,0},{768,256},{1,513},{257,769},{513,1},{769... | collective-permute-start | bytes 196616 | tf_op jit(solution)/shard_map/ppermute | solution.py:39
  312.6 7.4 %collective-permute-start.6 = (f32[32,512]{1,0:T(8,128)S(1)}, f32[32,512]{1,0:T(8,128)S(1)}, u32[]{:S(2)}, u32[]{:S(2)}) collective-permute-start(f32[32,512]{1,0:T(8,128)S(1)} %get-tuple-element.6), channel_id=1, source_target_pairs={{0,256},{256,512},{512,768},{768,0},{1,257},{257,513},{513,769},{7... | collective-permute-start | bytes 196616 | tf_op jit(solution)/shard_map/ppermute | solution.py:39
  321.2 19.3 %all-to-all-start.14 = ((f32[4,320,256]{2,1,0:T(8,128)}), f32[4,320,256]{2,1,0:T(8,128)S(1)}, u32[]{:S(2)}, u32[]{:S(2)}) async-start(f32[4,320,256]{2,1,0:T(8,128)} %broadcast_in_dim.139), calls=%async_computation.14 | async-start | bytes 2621440 | tf_op jit(solution)/shard_map/all_to_all | solution.py:21
  324.8 3.6 %collective-permute-start.7 = (f32[128,512]{1,0:T(8,128)S(1)}, f32[128,512]{1,0:T(8,128)}, u32[]{:S(2)}, u32[]{:S(2)}) collective-permute-start(f32[128,512]{1,0:T(8,128)S(1)} %constant_dynamic-slice_fusion), channel_id=1, source_target_pairs={{0,128},{128,0},{1,129},{129,1},{2,130},{130,2},{3,131},{131,3},{4... | collective-permute-start | bytes 786440 | tf_op jit(solution)/shard_map/ppermute | solution.py:39

commit v5 on v4

--- a/solution.py
+++ b/solution.py
@@ -48,9 +48,10 @@
         return lax.dynamic_slice_in_dim(arr, start * size, size, 0)
 
     mine = rows(part, core, half) + shifted(rows(part, 1 - core, half), "core", 1)
-    own = rows(mine, x, piece)
+    sums = [rows(mine, x, piece)]
     for step in range(1, nx):
-        own = own + shifted(rows(mine, (x + step) % nx, piece), "x", step)
+        sums.append(shifted(rows(mine, (x + step) % nx, piece), "x", step))
+    own = lax.optimization_barrier(sum(sums[1:], sums[0]))
     got = [own] + [shifted(own, "x", step) for step in range(1, nx)]
     back = got[:1] + got[:0:-1]
     start = (nx - x) % nx * piece
@@ -121,20 +122,22 @@
         grad_bf, w_bf, (((1,), (1,)), ((), ())), preferred_element_type=jnp.float32
     )
     dwn_total = dwn_reduce(dwn_part)
-    for axes in ("y", "zl"):
-        got = swap(dxn, axes)
-        dxn = jnp.sum(got, axis=0)
+    dxn = dxn - x_norm * jnp.sum(x_norm * dxn, axis=1, keepdims=True)
+    got = swap(dxn.astype(jnp.float16), "y")
+    dxn = jnp.sum(got.astype(jnp.float32), axis=0)
+    got = swap(dxn, "zl")
+    dxn = jnp.sum(got, axis=0)
     rows, lanes = dxn.shape[0], dxn.shape[1] // 2
     dxn = jnp.concatenate([dxn[:, :lanes], dxn[:, lanes:]], axis=0)
     got = swap(dxn, "zh")
-    dxn = jnp.sum(got, axis=0)
+    dxn = jnp.sum(got, axis=0).astype(jnp.float16)
     got = spread(dxn, "zh")
     dxn = got.reshape(-1, lanes)
     dxn = jnp.concatenate([dxn[:rows], dxn[rows:]], axis=1)
     for axes in ("zl", "y"):
         got = spread(dxn, axes)
         dxn = got.reshape(-1, dxn.shape[1])
-    student_grad = x_scale * (dxn - x_norm * jnp.sum(x_norm * dxn, axis=1, keepdims=True))
+    student_grad = x_scale * dxn.astype(jnp.float32)
     proto_grad = col_scale * (
         dwn_total - w_norm * jnp.sum(w_norm * dwn_total, axis=0, keepdims=True)
     )

time: 344 us -> 307 us (0.89)
  blocking collectives: 91.1 us -> 32.6 us
  starting transfers between devices: 80.4 us -> 105 us
  waiting for transfers between devices: 123 us -> 119 us
    all_to_all x3 -> x1, blocking collectives: 69.8 us -> 11.4 us  [swap(): return lax.all_to_all(pieces, axes, 0, 0)]
    all_to_all x0 -> x2, starting transfers between devices: none -> 21.3 us  [swap(): return lax.all_to_all(pieces, axes, 0, 0)]
    all_to_all x0 -> x2, waiting for transfers between devices: none -> 19.1 us  [swap(): return lax.all_to_all(pieces, axes, 0, 0)]
    all_to_all x11, waiting for transfers between devices: 112 us -> 99.9 us  [spread(): lax.all_to_all(jnp.broadcast_to(part[None], (n,) + part.shape), axes, 0, 0)]
    ppermute x8, waiting for transfers between devices: 11.6 us -> 0.02 us  [shifted(): return lax.ppermute(part, axis, [(i, (i + step) % n) for i in range(n)])]
  transfers between devices with their start and end apart: 19 -> 21, of which waited for: 16 -> 13; matrix products, arithmetic and copies ran while one was open for 6% -> 8% of each run, Pallas kernels for 0% -> 0%
where the time goes in v5:
time: 307 us; the launch traced here: 306 us
  waiting for transfers between devices  119 us (39%)
  starting transfers between devices  105 us (34%)
  blocking collectives  32.6 us (11%)
  local copies, waits for them, and re-layouts  25 us (8%)
  other arithmetic  17.7 us (6%)
  matrix products  5.07 us (2%)
    all_to_all x11, waiting for transfers between devices, spread(): lax.all_to_all(jnp.broadcast_to(part[None], (n,) + part.shape), axes, 0, 0)  99.9 us
    all_to_all x11, starting transfers between devices, spread(): lax.all_to_all(jnp.broadcast_to(part[None], (n,) + part.shape), axes, 0, 0)  61.1 us
    ppermute x8, starting transfers between devices, shifted(): return lax.ppermute(part, axis, [(i, (i + step) % n) for i in range(n)])  22.9 us
    all_to_all x2, starting transfers between devices, swap(): return lax.all_to_all(pieces, axes, 0, 0)  21.3 us
    all_to_all x1, blocking collectives, on_device(): both = spread_sum(jnp.sum(lax.all_to_all(sent, NEAR, 0, 0), axis=0), 'zh')  21.3 us
    all_to_all x2, waiting for transfers between devices, swap(): return lax.all_to_all(pieces, axes, 0, 0)  19.1 us
    all_to_all x1, blocking collectives, swap(): return lax.all_to_all(pieces, axes, 0, 0)  11.4 us
    gather x2, local copies, waits for them, and re-layouts, on_device(): first = jnp.take(q_mat, GLOBALS * image_here, axis=0)  7.65 us
  transfers between devices with their start and end apart: 21, of which 13 were waited for; matrix products, arithmetic and copies ran while one was open for 8% of the time, Pallas kernels for 0%

profile of v5, /device:TPU:32, one launch (start us, length us, event | category | flops | bytes accessed | tf_op | source)
XLA Modules:
  0.0 305.9 jit_solution(16312213995154077839)
XLA Ops:
  5.5 4.3 %all-to-all-start = ((f32[8,4,128]{2,1,0:T(4,128)}), f32[8,4,128]{2,1,0:T(4,128)}, u32[]{:S(2)}, u32[]{:S(2)}) async-start(f32[8,4,128]{2,1,0:T(4,128)} %broadcast_in_dim.66), calls=%async_computation | async-start | bytes 32768 | tf_op jit(solution)/shard_map/all_to_all | solution.py:21
  17.3 21.3 %all_to_all.75 = f32[16,3,128]{2,1,0:T(4,128)S(1)} all-to-all(f32[16,3,128]{2,1,0:T(4,128)S(1)} %reshape.87), channel_id=1, replica_groups=mesh['x'=4,'core'=2,'y'=4,'zh'=8,'zl'=4] {'y','zl'}, dimensions={0} | all-to-all | bytes 49152 | tf_op jit(solution)/shard_map/all_to_all | solution.py:93
  39.2 19.4 %all-to-all-start.2 = ((f32[8,3,128]{2,1,0:T(4,128)}), f32[8,3,128]{2,1,0:T(4,128)S(1)}, u32[]{:S(2)}, u32[]{:S(2)}) async-start(f32[8,3,128]{2,1,0:T(4,128)} %broadcast_in_dim.121), calls=%async_computation.2 | async-start | bytes 32768 | tf_op jit(solution)/shard_map/all_to_all | solution.py:21
  58.5 22.2 %all-to-all-done.2 = f32[8,3,128]{2,1,0:T(4,128)S(1)} async-done(((f32[8,3,128]{2,1,0:T(4,128)}), f32[8,3,128]{2,1,0:T(4,128)S(1)}, u32[]{:S(2)}, u32[]{:S(2)}) %all-to-all-start.2) | async-done | bytes 12320 | tf_op jit(solution)/shard_map/all_to_all | solution.py:21
  82.6 3.3 %all-to-all-start.3 = ((f32[8,4,128]{2,1,0:T(4,128)}), f32[8,4,128]{2,1,0:T(4,128)S(1)}, u32[]{:S(2)}, u32[]{:S(2)}) async-start(f32[8,4,128]{2,1,0:T(4,128)} %broadcast_in_dim.123), calls=%async_computation.3 | async-start | bytes 32768 | tf_op jit(solution)/shard_map/all_to_all | solution.py:21
  85.9 5.3 %all-to-all-done.3 = f32[8,4,128]{2,1,0:T(4,128)S(1)} async-done(((f32[8,4,128]{2,1,0:T(4,128)}), f32[8,4,128]{2,1,0:T(4,128)S(1)}, u32[]{:S(2)}, u32[]{:S(2)}) %all-to-all-start.3) | async-done | bytes 16416 | tf_op jit(solution)/shard_map/all_to_all | solution.py:21
  92.0 4.9 %all-to-all-start.4 = ((f32[16,3,128]{2,1,0:T(4,128)}), f32[16,3,128]{2,1,0:T(4,128)S(1)}, u32[]{:S(2)}, u32[]{:S(2)}) async-start(f32[16,3,128]{2,1,0:T(4,128)} %broadcast_in_dim.125), calls=%async_computation.4 | async-start | bytes 65536 | tf_op jit(solution)/shard_map/all_to_all | solution.py:21
  96.8 6.6 %all-to-all-done.4 = f32[16,3,128]{2,1,0:T(4,128)S(1)} async-done(((f32[16,3,128]{2,1,0:T(4,128)}), f32[16,3,128]{2,1,0:T(4,128)S(1)}, u32[]{:S(2)}, u32[]{:S(2)}) %all-to-all-start.4) | async-done | bytes 24608 | tf_op jit(solution)/shard_map/all_to_all | solution.py:21
  104.0 3.3 %all-to-all-start.5 = ((f32[8,2,128]{2,1,0:T(2,128)}), f32[8,2,128]{2,1,0:T(2,128)S(1)}, u32[]{:S(2)}, u32[]{:S(2)}) async-start(f32[8,2,128]{2,1,0:T(2,128)} %broadcast_in_dim.127), calls=%async_computation.5 | async-start | bytes 16384 | tf_op jit(solution)/shard_map/all_to_all | solution.py:21
  108.0 21.5 %all-to-all-done.5 = f32[8,2,128]{2,1,0:T(2,128)S(1)} async-done(((f32[8,2,128]{2,1,0:T(2,128)}), f32[8,2,128]{2,1,0:T(2,128)S(1)}, u32[]{:S(2)}, u32[]{:S(2)}) %all-to-all-start.5) | async-done | bytes 8224 | tf_op jit(solution)/shard_map/all_to_all | solution.py:21
  131.0 3.3 %all-to-all-start.6 = ((f32[8,4,128]{2,1,0:T(4,128)}), f32[8,4,128]{2,1,0:T(4,128)S(1)}, u32[]{:S(2)}, u32[]{:S(2)}) async-start(f32[8,4,128]{2,1,0:T(4,128)} %broadcast_in_dim.129), calls=%async_computation.6 | async-start | bytes 32768 | tf_op jit(solution)/shard_map/all_to_all | solution.py:21
  134.4 5.3 %all-to-all-done.6 = f32[8,4,128]{2,1,0:T(4,128)S(1)} async-done(((f32[8,4,128]{2,1,0:T(4,128)}), f32[8,4,128]{2,1,0:T(4,128)S(1)}, u32[]{:S(2)}, u32[]{:S(2)}) %all-to-all-start.6) | async-done | bytes 16416 | tf_op jit(solution)/shard_map/all_to_all | solution.py:21
  141.5 4.9 %all-to-all-start.7 = ((f32[16,2,128]{2,1,0:T(2,128)}), f32[16,2,128]{2,1,0:T(2,128)S(1)}, u32[]{:S(2)}, u32[]{:S(2)}) async-start(f32[16,2,128]{2,1,0:T(2,128)} %broadcast_in_dim.131), calls=%async_computation.7 | async-start | bytes 32768 | tf_op jit(solution)/shard_map/all_to_all | solution.py:21
  147.0 6.0 %all-to-all-done.7 = f32[16,2,128]{2,1,0:T(2,128)S(1)} async-done(((f32[16,2,128]{2,1,0:T(2,128)}), f32[16,2,128]{2,1,0:T(2,128)S(1)}, u32[]{:S(2)}, u32[]{:S(2)}) %all-to-all-start.7) | async-done | bytes 16416 | tf_op jit(solution)/shard_map/all_to_all | solution.py:21
  153.6 3.3 %all-to-all-start.8 = ((f32[8,2,128]{2,1,0:T(2,128)}), f32[8,2,128]{2,1,0:T(2,128)S(1)}, u32[]{:S(2)}, u32[]{:S(2)}) async-start(f32[8,2,128]{2,1,0:T(2,128)} %broadcast_in_dim.132), calls=%async_computation.8 | async-start | bytes 16384 | tf_op jit(solution)/shard_map/all_to_all | solution.py:21
  157.6 4.4 %gather_fusion = f32[1280,512]{1,0:T(8,128)} fusion(f32[256,512]{1,0:T(8,128)S(1)} %get-tuple-element.8, s32[2048]{0:T(1024)S(1)} %get-tuple-element.34), kind=kCustom, calls=%fused_computation.clone | custom fusion | bytes 5248000 | tf_op jit(solution)/shard_map/jit(_take)/gather | solution.py:101
  165.3 4.4 %gather_fusion.1 = f32[1280,512]{1,0:T(8,128)} fusion(f32[256,512]{1,0:T(8,128)S(1)} %get-tuple-element.8, s32[2048]{0:T(1024)S(1)} %get-tuple-element.33), kind=kCustom, calls=%fused_computation.1.clone | custom fusion | bytes 5248000 | tf_op jit(solution)/shard_map/jit(_take)/gather | solution.py:102
  172.9 6.1 %all-to-all-done.8 = f32[8,2,128]{2,1,0:T(2,128)S(1)} async-done(((f32[8,2,128]{2,1,0:T(2,128)}), f32[8,2,128]{2,1,0:T(2,128)S(1)}, u32[]{:S(2)}, u32[]{:S(2)}) %all-to-all-start.8) | async-done | bytes 8224 | tf_op jit(solution)/shard_map/all_to_all | solution.py:21
  180.2 3.6 %fusion.6 = bf16[1280,512]{0,1:T(8,128)(2,1)S(1)} fusion(f32[1280,512]{0,1:T(8,128)} %copy.21, f32[1280,512]{0,1:T(8,128)} %copy.18, f32[1280,512]{0,1:T(8,128)S(1)} %get-tuple-element.28, f32[1280]{0:T(1024)} %get-tuple-element.23, f32[1280]{0:T(1024)S(1)} %get-tuple-element.4, f32[1280]{0:T(1024)} %get-tuple-element.22, f32[1280]{0:T(1024)S(1)} %get-tuple-element.3, ...), kind=kLoop, calls=%fused_computation.11 | loop fusion | flops 7864320 | bytes 9208320 | tf_op jit(solution)/shard_map/convert_element_type | solution.py:117
  185.3 11.4 %all_to_all.76 = f16[4,320,256]{2,1,0:T(8,128)(2,1)S(1)} all-to-all(f16[4,320,256]{2,1,0:T(8,128)(2,1)S(1)} %bitcast.28), channel_id=1, replica_groups=mesh['x'=4,'core'=2,'y'=4,'zh'=8,'zl'=4] {'y'}, dimensions={0} | all-to-all | bytes 1310720 | tf_op jit(solution)/shard_map/all_to_all | solution.py:27
  197.5 5.0 %all-to-all-start.10 = ((f32[4,80,256]{2,1,0:T(8,128)}), f32[4,80,256]{2,1,0:T(8,128)S(1)}, u32[]{:S(2)}, u32[]{:S(2)}) async-start(f32[4,80,256]{2,1,0:T(8,128)} %bitcast.14), calls=%async_computation.10 | async-start | bytes 655360 | tf_op jit(solution)/shard_map/all_to_all | solution.py:27
  205.3 3.9 %all-to-all-done.10 = f32[4,80,256]{2,1,0:T(8,128)S(1)} async-done(((f32[4,80,256]{2,1,0:T(8,128)}), f32[4,80,256]{2,1,0:T(8,128)S(1)}, u32[]{:S(2)}, u32[]{:S(2)}) %all-to-all-start.10) | async-done | bytes 327712 | tf_op jit(solution)/shard_map/all_to_all | solution.py:27
  209.9 16.3 %all-to-all-start.11 = ((f32[8,20,128]{2,1,0:T(8,128)}), f32[8,20,128]{2,1,0:T(8,128)S(1)}, u32[]{:S(2)}, u32[]{:S(2)}) async-start(f32[8,20,128]{2,1,0:T(8,128)} %reshape.91), calls=%async_computation.11 | async-start | bytes 196608 | tf_op jit(solution)/shard_map/all_to_all | solution.py:27
  228.8 3.9 %collective-permute-start.2 = (f32[32,512]{1,0:T(8,128)S(1)}, f32[32,512]{1,0:T(8,128)S(1)}, u32[]{:S(2)}, u32[]{:S(2)}) collective-permute-start(f32[32,512]{1,0:T(8,128)S(1)} %get-tuple-element.17), channel_id=1, source_target_pairs={{0,512},{256,768},{512,0},{768,256},{1,513},{257,769},{513,1},{769... | collective-permute-start | bytes 196616 | tf_op jit(solution)/shard_map/ppermute | solution.py:39
  235.8 15.2 %all-to-all-done.11 = f32[8,20,128]{2,1,0:T(8,128)S(1)} async-done(((f32[8,20,128]{2,1,0:T(8,128)}), f32[8,20,128]{2,1,0:T(8,128)S(1)}, u32[]{:S(2)}, u32[]{:S(2)}) %all-to-all-start.11) | async-done | bytes 81952 | tf_op jit(solution)/shard_map/all_to_all | solution.py:27
  251.7 6.5 %all-to-all-start.12 = ((f16[8,20,128]{2,1,0:T(8,128)(2,1)}), f16[8,20,128]{2,1,0:T(8,128)(2,1)S(1)}, u32[]{:S(2)}, u32[]{:S(2)}) async-start(f16[8,20,128]{2,1,0:T(8,128)(2,1)} %broadcast_in_dim.136), calls=%async_computation.12 | async-start | bytes 98304 | tf_op jit(solution)/shard_map/all_to_all | solution.py:21
  261.0 3.9 %collective-permute-start.5 = (f32[32,512]{1,0:T(8,128)S(1)}, f32[32,512]{1,0:T(8,128)S(1)}, u32[]{:S(2)}, u32[]{:S(2)}) collective-permute-start(f32[32,512]{1,0:T(8,128)S(1)} %add_add_fusion), channel_id=1, source_target_pairs={{0,512},{256,768},{512,0},{768,256},{1,513},{257,769},{513,1},{769... | collective-permute-start | bytes 196616 | tf_op jit(solution)/shard_map/ppermute | solution.py:39
  267.8 13.0 %all-to-all-done.12 = f16[8,20,128]{2,1,0:T(8,128)(2,1)S(1)} async-done(((f16[8,20,128]{2,1,0:T(8,128)(2,1)}), f16[8,20,128]{2,1,0:T(8,128)(2,1)S(1)}, u32[]{:S(2)}, u32[]{:S(2)}) %all-to-all-start.12) | async-done | bytes 40992 | tf_op jit(solution)/shard_map/all_to_all | solution.py:21
  281.6 4.4 %all-to-all-start.13 = ((f16[4,80,256]{2,1,0:T(8,128)(2,1)}), f16[4,80,256]{2,1,0:T(8,128)(2,1)S(1)}, u32[]{:S(2)}, u32[]{:S(2)}) async-start(f16[4,80,256]{2,1,0:T(8,128)(2,1)} %broadcast_in_dim.137), calls=%async_computation.13 | async-start | bytes 327680 | tf_op jit(solution)/shard_map/all_to_all | solution.py:21
  288.1 3.4 %all-to-all-done.13 = f16[4,80,256]{2,1,0:T(8,128)(2,1)S(1)} async-done(((f16[4,80,256]{2,1,0:T(8,128)(2,1)}), f16[4,80,256]{2,1,0:T(8,128)(2,1)S(1)}, u32[]{:S(2)}, u32[]{:S(2)}) %all-to-all-start.13) | async-done | bytes 163872 | tf_op jit(solution)/shard_map/all_to_all | solution.py:21
  292.3 3.5 %all-to-all-start.14 = ((f16[4,320,256]{2,1,0:T(8,128)(2,1)}), f16[4,320,256]{2,1,0:T(8,128)(2,1)S(1)}, u32[]{:S(2)}, u32[]{:S(2)}) async-start(f16[4,320,256]{2,1,0:T(8,128)(2,1)} %broadcast_in_dim.139), calls=%async_computation.14 | async-start | bytes 1310720 | tf_op jit(solution)/shard_map/all_to_all | solution.py:21
  296.9 7.7 %all-to-all-done.14 = f16[4,320,256]{2,1,0:T(8,128)(2,1)S(1)} async-done(((f16[4,320,256]{2,1,0:T(8,128)(2,1)}), f16[4,320,256]{2,1,0:T(8,128)(2,1)S(1)}, u32[]{:S(2)}, u32[]{:S(2)}) %all-to-all-start.14) | async-done | bytes 655392 | tf_op jit(solution)/shard_map/all_to_all | solution.py:21
  (111 shorter events, 53.3 us)
Async XLA Ops:
  0.6 9.5 %copy-start.2 = (bf16[256,512]{1,0:T(8,128)(2,1)S(1)}, bf16[256,512]{1,0:T(8,128)(2,1)}, u32[]{:S(2)}) copy-start(bf16[256,512]{1,0:T(8,128)(2,1)} %param.9) | copy-start | bytes 786436
  0.6 9.2 %copy-start = (bf16[1280,256]{1,0:T(8,128)(2,1)S(1)}, bf16[1280,256]{1,0:T(8,128)(2,1)}, u32[]{:S(2)}) copy-start(bf16[1280,256]{1,0:T(8,128)(2,1)} %param.7) | copy-start | bytes 1966084
  5.5 9.8 %all-to-all-start = ((f32[8,4,128]{2,1,0:T(4,128)}), f32[8,4,128]{2,1,0:T(4,128)}, u32[]{:S(2)}, u32[]{:S(2)}) async-start(f32[8,4,128]{2,1,0:T(4,128)} %broadcast_in_dim.66), calls=%async_computation | async-start | bytes 32768 | tf_op jit(solution)/shard_map/all_to_all | solution.py:21
  11.4 85.4 %copy-start.6 = (s32[1280]{0:T(1024)S(1)}, s32[1280]{0:T(1024)}, u32[]{:S(2)}) copy-start(s32[1280]{0:T(1024)} %param.10) | copy-start | bytes 15364
  16.0 91.4 %copy-start.5 = (s32[1280]{0:T(1024)S(1)}, s32[1280]{0:T(1024)}, u32[]{:S(2)}) copy-start(s32[1280]{0:T(1024)} %param.11) | copy-start | bytes 15364
  39.2 41.6 %all-to-all-start.2 = ((f32[8,3,128]{2,1,0:T(4,128)}), f32[8,3,128]{2,1,0:T(4,128)S(1)}, u32[]{:S(2)}, u32[]{:S(2)}) async-start(f32[8,3,128]{2,1,0:T(4,128)} %broadcast_in_dim.121), calls=%async_computation.2 | async-start | bytes 32768 | tf_op jit(solution)/shard_map/all_to_all | solution.py:21
  82.6 8.6 %all-to-all-start.3 = ((f32[8,4,128]{2,1,0:T(4,128)}), f32[8,4,128]{2,1,0:T(4,128)S(1)}, u32[]{:S(2)}, u32[]{:S(2)}) async-start(f32[8,4,128]{2,1,0:T(4,128)} %broadcast_in_dim.123), calls=%async_computation.3 | async-start | bytes 32768 | tf_op jit(solution)/shard_map/all_to_all | solution.py:21
  92.0 11.4 %all-to-all-start.4 = ((f32[16,3,128]{2,1,0:T(4,128)}), f32[16,3,128]{2,1,0:T(4,128)S(1)}, u32[]{:S(2)}, u32[]{:S(2)}) async-start(f32[16,3,128]{2,1,0:T(4,128)} %broadcast_in_dim.125), calls=%async_computation.4 | async-start | bytes 65536 | tf_op jit(solution)/shard_map/all_to_all | solution.py:21
  104.0 25.4 %all-to-all-start.5 = ((f32[8,2,128]{2,1,0:T(2,128)}), f32[8,2,128]{2,1,0:T(2,128)S(1)}, u32[]{:S(2)}, u32[]{:S(2)}) async-start(f32[8,2,128]{2,1,0:T(2,128)} %broadcast_in_dim.127), calls=%async_computation.5 | async-start | bytes 16384 | tf_op jit(solution)/shard_map/all_to_all | solution.py:21
  131.0 8.6 %all-to-all-start.6 = ((f32[8,4,128]{2,1,0:T(4,128)}), f32[8,4,128]{2,1,0:T(4,128)S(1)}, u32[]{:S(2)}, u32[]{:S(2)}) async-start(f32[8,4,128]{2,1,0:T(4,128)} %broadcast_in_dim.129), calls=%async_computation.6 | async-start | bytes 32768 | tf_op jit(solution)/shard_map/all_to_all | solution.py:21
  141.5 11.5 %all-to-all-start.7 = ((f32[16,2,128]{2,1,0:T(2,128)}), f32[16,2,128]{2,1,0:T(2,128)S(1)}, u32[]{:S(2)}, u32[]{:S(2)}) async-start(f32[16,2,128]{2,1,0:T(2,128)} %broadcast_in_dim.131), calls=%async_computation.7 | async-start | bytes 32768 | tf_op jit(solution)/shard_map/all_to_all | solution.py:21
  153.6 25.4 %all-to-all-start.8 = ((f32[8,2,128]{2,1,0:T(2,128)}), f32[8,2,128]{2,1,0:T(2,128)S(1)}, u32[]{:S(2)}, u32[]{:S(2)}) async-start(f32[8,2,128]{2,1,0:T(2,128)} %broadcast_in_dim.132), calls=%async_computation.8 | async-start | bytes 16384 | tf_op jit(solution)/shard_map/all_to_all | solution.py:21
  180.2 3.6 %copy-start.1 = (bf16[1280,256]{1,0:T(8,128)(2,1)S(1)}, bf16[1280,256]{1,0:T(8,128)(2,1)}, u32[]{:S(2)}) copy-start(bf16[1280,256]{1,0:T(8,128)(2,1)} %param.7) | copy-start | bytes 1966084
  183.8 1.1 copy-start.3
  185.3 17.2 %copy-start.4 = (bf16[1280,512]{0,1:T(8,128)(2,1)S(1)}, bf16[1280,512]{0,1:T(8,128)(2,1)}, u32[]{:S(2)}) copy-start(bf16[1280,512]{0,1:T(8,128)(2,1)} %copy-done.3) | copy-start | bytes 3932164
  197.5 11.7 %all-to-all-start.10 = ((f32[4,80,256]{2,1,0:T(8,128)}), f32[4,80,256]{2,1,0:T(8,128)S(1)}, u32[]{:S(2)}, u32[]{:S(2)}) async-start(f32[4,80,256]{2,1,0:T(8,128)} %bitcast.14), calls=%async_computation.10 | async-start | bytes 655360 | tf_op jit(solution)/shard_map/all_to_all | solution.py:27
  203.4 22.9 %collective-permute-start = (f32[128,512]{1,0:T(8,128)S(1)}, f32[128,512]{1,0:T(8,128)S(1)}, u32[]{:S(2)}, u32[]{:S(2)}) collective-permute-start(f32[128,512]{1,0:T(8,128)S(1)} %constant_dynamic-slice_fusion.4), channel_id=1, source_target_pairs={{0,128},{128,0},{1,129},{129,1},{2,130},{130,2},{3,131},{131,3},{4... | collective-permute-start | bytes 786440 | tf_op jit(solution)/shard_map/ppermute | solution.py:39
  209.9 41.1 %all-to-all-start.11 = ((f32[8,20,128]{2,1,0:T(8,128)}), f32[8,20,128]{2,1,0:T(8,128)S(1)}, u32[]{:S(2)}, u32[]{:S(2)}) async-start(f32[8,20,128]{2,1,0:T(8,128)} %reshape.91), calls=%async_computation.11 | async-start | bytes 196608 | tf_op jit(solution)/shard_map/all_to_all | solution.py:27
  226.3 31.8 %collective-permute-start.1 = (f32[32,512]{1,0:T(8,128)S(1)}, f32[32,512]{1,0:T(8,128)S(1)}, u32[]{:S(2)}, u32[]{:S(2)}) collective-permute-start(f32[32,512]{1,0:T(8,128)S(1)} %get-tuple-element.15), channel_id=1, source_target_pairs={{0,256},{256,512},{512,768},{768,0},{1,257},{257,513},{513,769},{7... | collective-permute-start | bytes 196616 | tf_op jit(solution)/shard_map/ppermute | solution.py:39
  228.8 29.3 %collective-permute-start.2 = (f32[32,512]{1,0:T(8,128)S(1)}, f32[32,512]{1,0:T(8,128)S(1)}, u32[]{:S(2)}, u32[]{:S(2)}) collective-permute-start(f32[32,512]{1,0:T(8,128)S(1)} %get-tuple-element.17), channel_id=1, source_target_pairs={{0,512},{256,768},{512,0},{768,256},{1,513},{257,769},{513,1},{769... | collective-permute-start | bytes 196616 | tf_op jit(solution)/shard_map/ppermute | solution.py:39
  232.8 25.4 %collective-permute-start.3 = (f32[32,512]{1,0:T(8,128)S(1)}, f32[32,512]{1,0:T(8,128)S(1)}, u32[]{:S(2)}, u32[]{:S(2)}) collective-permute-start(f32[32,512]{1,0:T(8,128)S(1)} %get-tuple-element.16), channel_id=1, source_target_pairs={{0,768},{256,0},{512,256},{768,512},{1,769},{257,1},{513,257},{769... | collective-permute-start | bytes 196616 | tf_op jit(solution)/shard_map/ppermute | solution.py:39
  251.7 29.1 %all-to-all-start.12 = ((f16[8,20,128]{2,1,0:T(8,128)(2,1)}), f16[8,20,128]{2,1,0:T(8,128)(2,1)S(1)}, u32[]{:S(2)}, u32[]{:S(2)}) async-start(f16[8,20,128]{2,1,0:T(8,128)(2,1)} %broadcast_in_dim.136), calls=%async_computation.12 | async-start | bytes 98304 | tf_op jit(solution)/shard_map/all_to_all | solution.py:21
  258.2 9.6 %collective-permute-start.4 = (f32[32,512]{1,0:T(8,128)S(1)}, f32[32,512]{1,0:T(8,128)S(1)}, u32[]{:S(2)}, u32[]{:S(2)}) collective-permute-start(f32[32,512]{1,0:T(8,128)S(1)} %add_add_fusion), channel_id=1, source_target_pairs={{0,768},{256,0},{512,256},{768,512},{1,769},{257,1},{513,257},{769... | collective-permute-start | bytes 196616 | tf_op jit(solution)/shard_map/ppermute | solution.py:39
  261.0 25.0 %collective-permute-start.5 = (f32[32,512]{1,0:T(8,128)S(1)}, f32[32,512]{1,0:T(8,128)S(1)}, u32[]{:S(2)}, u32[]{:S(2)}) collective-permute-start(f32[32,512]{1,0:T(8,128)S(1)} %add_add_fusion), channel_id=1, source_target_pairs={{0,512},{256,768},{512,0},{768,256},{1,513},{257,769},{513,1},{769... | collective-permute-start | bytes 196616 | tf_op jit(solution)/shard_map/ppermute | solution.py:39
  265.0 21.1 %collective-permute-start.6 = (f32[32,512]{1,0:T(8,128)S(1)}, f32[32,512]{1,0:T(8,128)S(1)}, u32[]{:S(2)}, u32[]{:S(2)}) collective-permute-start(f32[32,512]{1,0:T(8,128)S(1)} %add_add_fusion), channel_id=1, source_target_pairs={{0,256},{256,512},{512,768},{768,0},{1,257},{257,513},{513,769},{7... | collective-permute-start | bytes 196616 | tf_op jit(solution)/shard_map/ppermute | solution.py:39
  281.6 9.9 %all-to-all-start.13 = ((f16[4,80,256]{2,1,0:T(8,128)(2,1)}), f16[4,80,256]{2,1,0:T(8,128)(2,1)S(1)}, u32[]{:S(2)}, u32[]{:S(2)}) async-start(f16[4,80,256]{2,1,0:T(8,128)(2,1)} %broadcast_in_dim.137), calls=%async_computation.13 | async-start | bytes 327680 | tf_op jit(solution)/shard_map/all_to_all | solution.py:21
  286.2 9.7 %collective-permute-start.7 = (f32[128,512]{1,0:T(8,128)S(1)}, f32[128,512]{1,0:T(8,128)S(1)}, u32[]{:S(2)}, u32[]{:S(2)}) collective-permute-start(f32[128,512]{1,0:T(8,128)S(1)} %constant_dynamic-slice_fusion), channel_id=1, source_target_pairs={{0,128},{128,0},{1,129},{129,1},{2,130},{130,2},{3,131},{131,3},{4... | collective-permute-start | bytes 786440 | tf_op jit(solution)/shard_map/ppermute | solution.py:39
  292.3 12.2 %all-to-all-start.14 = ((f16[4,320,256]{2,1,0:T(8,128)(2,1)}), f16[4,320,256]{2,1,0:T(8,128)(2,1)S(1)}, u32[]{:S(2)}, u32[]{:S(2)}) async-start(f16[4,320,256]{2,1,0:T(8,128)(2,1)} %broadcast_in_dim.139), calls=%async_computation.14 | async-start | bytes 1310720 | tf_op jit(solution)/shard_map/all_to_all | solution.py:21

commit v6 on v5

--- a/solution.py
+++ b/solution.py
@@ -125,15 +125,10 @@
     dxn = dxn - x_norm * jnp.sum(x_norm * dxn, axis=1, keepdims=True)
     got = swap(dxn.astype(jnp.float16), "y")
     dxn = jnp.sum(got.astype(jnp.float32), axis=0)
-    got = swap(dxn, "zl")
-    dxn = jnp.sum(got, axis=0)
-    rows, lanes = dxn.shape[0], dxn.shape[1] // 2
-    dxn = jnp.concatenate([dxn[:, :lanes], dxn[:, lanes:]], axis=0)
-    got = swap(dxn, "zh")
-    dxn = jnp.sum(got, axis=0).astype(jnp.float16)
-    got = spread(dxn, "zh")
-    dxn = got.reshape(-1, lanes)
-    dxn = jnp.concatenate([dxn[:rows], dxn[rows:]], axis=1)
+    got = swap(dxn.astype(jnp.float16), "zl")
+    dxn = jnp.sum(got.astype(jnp.float32), axis=0)
+    got = spread(dxn.astype(jnp.float16), "zh")
+    dxn = jnp.sum(got.astype(jnp.float32), axis=0).astype(jnp.float16)
     for axes in ("zl", "y"):
         got = spread(dxn, axes)
         dxn = got.reshape(-1, dxn.shape[1])

time: 307 us -> 290 us (0.945)
  waiting for transfers between devices: 119 us -> 105 us
  starting transfers between devices: 105 us -> 93.2 us
  blocking collectives: 32.6 us -> 42 us
    all_to_all x2 -> x0, starting transfers between devices: 21.3 us -> none  [swap(): return lax.all_to_all(pieces, axes, 0, 0)]
    all_to_all x2 -> x0, waiting for transfers between devices: 19.1 us -> none  [swap(): return lax.all_to_all(pieces, axes, 0, 0)]
    all_to_all x11, starting transfers between devices: 61.1 us -> 70.6 us  [spread(): lax.all_to_all(jnp.broadcast_to(part[None], (n,) + part.shape), axes, 0, 0)]
    all_to_all x1 -> x2, blocking collectives: 11.4 us -> 20.7 us  [swap(): return lax.all_to_all(pieces, axes, 0, 0)]
    ppermute x8, waiting for transfers between devices: 0.02 us -> 4.52 us  [shifted(): return lax.ppermute(part, axis, [(i, (i + step) % n) for i in range(n)])]
  transfers between devices with their start and end apart: 21 -> 19, of which waited for: 13 -> 14; matrix products, arithmetic and copies ran while one was open for 8% -> 8% of each run, Pallas kernels for 0% -> 0%
where the time goes in v6:
time: 290 us; the launch traced here: 288 us
  waiting for transfers between devices  105 us (36%)
  starting transfers between devices  93.2 us (32%)
  blocking collectives  42 us (14%)
  local copies, waits for them, and re-layouts  24.4 us (8%)
  other arithmetic  17 us (6%)
  matrix products  5.07 us (2%)
    all_to_all x11, waiting for transfers between devices, spread(): lax.all_to_all(jnp.broadcast_to(part[None], (n,) + part.shape), axes, 0, 0)  101 us
    all_to_all x11, starting transfers between devices, spread(): lax.all_to_all(jnp.broadcast_to(part[None], (n,) + part.shape), axes, 0, 0)  70.6 us
    ppermute x8, starting transfers between devices, shifted(): return lax.ppermute(part, axis, [(i, (i + step) % n) for i in range(n)])  22.6 us
    all_to_all x1, blocking collectives, on_device(): both = spread_sum(jnp.sum(lax.all_to_all(sent, NEAR, 0, 0), axis=0), 'zh')  21.3 us
    all_to_all x2, blocking collectives, swap(): return lax.all_to_all(pieces, axes, 0, 0)  20.7 us
    gather x2, local copies, waits for them, and re-layouts, on_device(): first = jnp.take(q_mat, GLOBALS * image_here, axis=0)  7.65 us
    gather x2, local copies, waits for them, and re-layouts, on_device(): second = jnp.take(q_mat, GLOBALS * image_here + 1, axis=0)  7.64 us
    broadcast_in_dim x11, local copies, waits for them, and re-layouts, spread(): jnp.broadcast_to(part[None], (n,) + part.shape)  7.21 us
  transfers between devices with their start and end apart: 19, of which 14 were waited for; matrix products, arithmetic and copies ran while one was open for 8% of the time, Pallas kernels for 0%

profile of v6, /device:TPU:32, one launch (start us, length us, event | category | flops | bytes accessed | tf_op | source)
XLA Modules:
  0.0 288.1 jit_solution(9388499595793997088)
XLA Ops:
  5.5 4.3 %all-to-all-start = ((f32[8,4,128]{2,1,0:T(4,128)}), f32[8,4,128]{2,1,0:T(4,128)}, u32[]{:S(2)}, u32[]{:S(2)}) async-start(f32[8,4,128]{2,1,0:T(4,128)} %broadcast_in_dim.66), calls=%async_computation | async-start | bytes 32768 | tf_op jit(solution)/shard_map/all_to_all | solution.py:21
  17.3 21.3 %all_to_all.70 = f32[16,3,128]{2,1,0:T(4,128)S(1)} all-to-all(f32[16,3,128]{2,1,0:T(4,128)S(1)} %reshape.83), channel_id=1, replica_groups=mesh['x'=4,'core'=2,'y'=4,'zh'=8,'zl'=4] {'y','zl'}, dimensions={0} | all-to-all | bytes 49152 | tf_op jit(solution)/shard_map/all_to_all | solution.py:93
  39.2 19.4 %all-to-all-start.2 = ((f32[8,3,128]{2,1,0:T(4,128)}), f32[8,3,128]{2,1,0:T(4,128)S(1)}, u32[]{:S(2)}, u32[]{:S(2)}) async-start(f32[8,3,128]{2,1,0:T(4,128)} %broadcast_in_dim.121), calls=%async_computation.2 | async-start | bytes 32768 | tf_op jit(solution)/shard_map/all_to_all | solution.py:21
  58.5 22.2 %all-to-all-done.2 = f32[8,3,128]{2,1,0:T(4,128)S(1)} async-done(((f32[8,3,128]{2,1,0:T(4,128)}), f32[8,3,128]{2,1,0:T(4,128)S(1)}, u32[]{:S(2)}, u32[]{:S(2)}) %all-to-all-start.2) | async-done | bytes 12320 | tf_op jit(solution)/shard_map/all_to_all | solution.py:21
  82.6 3.3 %all-to-all-start.3 = ((f32[8,4,128]{2,1,0:T(4,128)}), f32[8,4,128]{2,1,0:T(4,128)S(1)}, u32[]{:S(2)}, u32[]{:S(2)}) async-start(f32[8,4,128]{2,1,0:T(4,128)} %broadcast_in_dim.123), calls=%async_computation.3 | async-start | bytes 32768 | tf_op jit(solution)/shard_map/all_to_all | solution.py:21
  85.9 5.3 %all-to-all-done.3 = f32[8,4,128]{2,1,0:T(4,128)S(1)} async-done(((f32[8,4,128]{2,1,0:T(4,128)}), f32[8,4,128]{2,1,0:T(4,128)S(1)}, u32[]{:S(2)}, u32[]{:S(2)}) %all-to-all-start.3) | async-done | bytes 16416 | tf_op jit(solution)/shard_map/all_to_all | solution.py:21
  92.0 4.9 %all-to-all-start.4 = ((f32[16,3,128]{2,1,0:T(4,128)}), f32[16,3,128]{2,1,0:T(4,128)S(1)}, u32[]{:S(2)}, u32[]{:S(2)}) async-start(f32[16,3,128]{2,1,0:T(4,128)} %broadcast_in_dim.125), calls=%async_computation.4 | async-start | bytes 65536 | tf_op jit(solution)/shard_map/all_to_all | solution.py:21
  96.8 6.6 %all-to-all-done.4 = f32[16,3,128]{2,1,0:T(4,128)S(1)} async-done(((f32[16,3,128]{2,1,0:T(4,128)}), f32[16,3,128]{2,1,0:T(4,128)S(1)}, u32[]{:S(2)}, u32[]{:S(2)}) %all-to-all-start.4) | async-done | bytes 24608 | tf_op jit(solution)/shard_map/all_to_all | solution.py:21
  104.0 3.3 %all-to-all-start.5 = ((f32[8,2,128]{2,1,0:T(2,128)}), f32[8,2,128]{2,1,0:T(2,128)S(1)}, u32[]{:S(2)}, u32[]{:S(2)}) async-start(f32[8,2,128]{2,1,0:T(2,128)} %broadcast_in_dim.127), calls=%async_computation.5 | async-start | bytes 16384 | tf_op jit(solution)/shard_map/all_to_all | solution.py:21
  108.0 21.5 %all-to-all-done.5 = f32[8,2,128]{2,1,0:T(2,128)S(1)} async-done(((f32[8,2,128]{2,1,0:T(2,128)}), f32[8,2,128]{2,1,0:T(2,128)S(1)}, u32[]{:S(2)}, u32[]{:S(2)}) %all-to-all-start.5) | async-done | bytes 8224 | tf_op jit(solution)/shard_map/all_to_all | solution.py:21
  131.0 3.3 %all-to-all-start.6 = ((f32[8,4,128]{2,1,0:T(4,128)}), f32[8,4,128]{2,1,0:T(4,128)S(1)}, u32[]{:S(2)}, u32[]{:S(2)}) async-start(f32[8,4,128]{2,1,0:T(4,128)} %broadcast_in_dim.129), calls=%async_computation.6 | async-start | bytes 32768 | tf_op jit(solution)/shard_map/all_to_all | solution.py:21
  134.4 5.3 %all-to-all-done.6 = f32[8,4,128]{2,1,0:T(4,128)S(1)} async-done(((f32[8,4,128]{2,1,0:T(4,128)}), f32[8,4,128]{2,1,0:T(4,128)S(1)}, u32[]{:S(2)}, u32[]{:S(2)}) %all-to-all-start.6) | async-done | bytes 16416 | tf_op jit(solution)/shard_map/all_to_all | solution.py:21
  141.5 4.9 %all-to-all-start.7 = ((f32[16,2,128]{2,1,0:T(2,128)}), f32[16,2,128]{2,1,0:T(2,128)S(1)}, u32[]{:S(2)}, u32[]{:S(2)}) async-start(f32[16,2,128]{2,1,0:T(2,128)} %broadcast_in_dim.131), calls=%async_computation.7 | async-start | bytes 32768 | tf_op jit(solution)/shard_map/all_to_all | solution.py:21
  147.0 6.0 %all-to-all-done.7 = f32[16,2,128]{2,1,0:T(2,128)S(1)} async-done(((f32[16,2,128]{2,1,0:T(2,128)}), f32[16,2,128]{2,1,0:T(2,128)S(1)}, u32[]{:S(2)}, u32[]{:S(2)}) %all-to-all-start.7) | async-done | bytes 16416 | tf_op jit(solution)/shard_map/all_to_all | solution.py:21
  153.6 3.3 %all-to-all-start.8 = ((f32[8,2,128]{2,1,0:T(2,128)}), f32[8,2,128]{2,1,0:T(2,128)S(1)}, u32[]{:S(2)}, u32[]{:S(2)}) async-start(f32[8,2,128]{2,1,0:T(2,128)} %broadcast_in_dim.132), calls=%async_computation.8 | async-start | bytes 16384 | tf_op jit(solution)/shard_map/all_to_all | solution.py:21
  157.6 4.4 %gather_fusion = f32[1280,512]{1,0:T(8,128)} fusion(f32[256,512]{1,0:T(8,128)S(1)} %get-tuple-element.8, s32[2048]{0:T(1024)S(1)} %get-tuple-element.30), kind=kCustom, calls=%fused_computation.clone | custom fusion | bytes 5248000 | tf_op jit(solution)/shard_map/jit(_take)/gather | solution.py:101
  162.1 3.2 %copy.18 = f32[1280,512]{0,1:T(8,128)} copy(f32[1280,512]{1,0:T(8,128)} %gather_fusion) | data formatting | bytes 5242880 | tf_op jit(solution)/shard_map/jit(_take)/gather | solution.py:101
  165.3 4.4 %gather_fusion.1 = f32[1280,512]{1,0:T(8,128)} fusion(f32[256,512]{1,0:T(8,128)S(1)} %get-tuple-element.8, s32[2048]{0:T(1024)S(1)} %get-tuple-element.29), kind=kCustom, calls=%fused_computation.1.clone | custom fusion | bytes 5248000 | tf_op jit(solution)/shard_map/jit(_take)/gather | solution.py:102
  169.7 3.3 %copy.21 = f32[1280,512]{0,1:T(8,128)} copy(f32[1280,512]{1,0:T(8,128)} %gather_fusion.1) | data formatting | bytes 5242880 | tf_op jit(solution)/shard_map/jit(_take)/gather | solution.py:102
  172.9 6.1 %all-to-all-done.8 = f32[8,2,128]{2,1,0:T(2,128)S(1)} async-done(((f32[8,2,128]{2,1,0:T(2,128)}), f32[8,2,128]{2,1,0:T(2,128)S(1)}, u32[]{:S(2)}, u32[]{:S(2)}) %all-to-all-start.8) | async-done | bytes 8224 | tf_op jit(solution)/shard_map/all_to_all | solution.py:21
  180.2 3.6 %fusion.6 = bf16[1280,512]{0,1:T(8,128)(2,1)S(1)} fusion(f32[1280,512]{0,1:T(8,128)} %copy.21, f32[1280,512]{0,1:T(8,128)} %copy.18, f32[1280,512]{0,1:T(8,128)S(1)} %get-tuple-element.24, f32[1280]{0:T(1024)} %get-tuple-element.19, f32[1280]{0:T(1024)S(1)} %get-tuple-element.4, f32[1280]{0:T(1024)} %get-tuple-element.18, f32[1280]{0:T(1024)S(1)} %get-tuple-element.3, ...), kind=kLoop, calls=%fused_computation.11 | loop fusion | flops 7864320 | bytes 9208320 | tf_op jit(solution)/shard_map/convert_element_type | solution.py:117
  185.3 11.2 %all_to_all.71 = f16[4,320,256]{2,1,0:T(8,128)(2,1)S(1)} all-to-all(f16[4,320,256]{2,1,0:T(8,128)(2,1)S(1)} %bitcast.28), channel_id=1, replica_groups=mesh['x'=4,'core'=2,'y'=4,'zh'=8,'zl'=4] {'y'}, dimensions={0} | all-to-all | bytes 1310720 | tf_op jit(solution)/shard_map/all_to_all | solution.py:27
  196.7 9.5 %all_to_all.72 = f16[4,80,256]{2,1,0:T(8,128)(2,1)S(1)} all-to-all(f16[4,80,256]{2,1,0:T(8,128)(2,1)S(1)} %bitcast.30), channel_id=1, replica_groups=mesh['x'=4,'core'=2,'y'=4,'zh'=8,'zl'=4] {'zl'}, dimensions={0} | all-to-all | bytes 327680 | tf_op jit(solution)/shard_map/all_to_all | solution.py:27
  207.0 16.3 %all-to-all-start.11 = ((f16[8,80,256]{2,1,0:T(8,128)(2,1)}), f16[8,80,256]{2,1,0:T(8,128)(2,1)S(1)}, u32[]{:S(2)}, u32[]{:S(2)}) async-start(f16[8,80,256]{2,1,0:T(8,128)(2,1)} %broadcast_in_dim.136), calls=%async_computation.11 | async-start | bytes 655360 | tf_op jit(solution)/shard_map/all_to_all | solution.py:21
  230.1 3.9 %collective-permute-start.2 = (f32[32,512]{1,0:T(8,128)S(1)}, f32[32,512]{1,0:T(8,128)S(1)}, u32[]{:S(2)}, u32[]{:S(2)}) collective-permute-start(f32[32,512]{1,0:T(8,128)S(1)} %get-tuple-element.17), channel_id=1, source_target_pairs={{0,512},{256,768},{512,0},{768,256},{1,513},{257,769},{513,1},{769... | collective-permute-start | bytes 196616 | tf_op jit(solution)/shard_map/ppermute | solution.py:39
  240.3 4.3 %collective-permute-start.4 = (f32[32,512]{1,0:T(8,128)S(1)}, f32[32,512]{1,0:T(8,128)S(1)}, u32[]{:S(2)}, u32[]{:S(2)}) collective-permute-start(f32[32,512]{1,0:T(8,128)S(1)} %add_add_fusion), channel_id=1, source_target_pairs={{0,768},{256,0},{512,256},{768,512},{1,769},{257,1},{513,257},{769... | collective-permute-start | bytes 196616 | tf_op jit(solution)/shard_map/ppermute | solution.py:39
  244.5 3.1 %collective-permute-start.5 = (f32[32,512]{1,0:T(8,128)S(1)}, f32[32,512]{1,0:T(8,128)S(1)}, u32[]{:S(2)}, u32[]{:S(2)}) collective-permute-start(f32[32,512]{1,0:T(8,128)S(1)} %add_add_fusion), channel_id=1, source_target_pairs={{0,512},{256,768},{512,0},{768,256},{1,513},{257,769},{513,1},{769... | collective-permute-start | bytes 196616 | tf_op jit(solution)/shard_map/ppermute | solution.py:39
  249.6 13.9 %all-to-all-done.11 = f16[8,80,256]{2,1,0:T(8,128)(2,1)S(1)} async-done(((f16[8,80,256]{2,1,0:T(8,128)(2,1)}), f16[8,80,256]{2,1,0:T(8,128)(2,1)S(1)}, u32[]{:S(2)}, u32[]{:S(2)}) %all-to-all-start.11) | async-done | bytes 327712 | tf_op jit(solution)/shard_map/all_to_all | solution.py:21
  264.2 4.0 %all-to-all-start.12 = ((f16[4,80,256]{2,1,0:T(8,128)(2,1)}), f16[4,80,256]{2,1,0:T(8,128)(2,1)S(1)}, u32[]{:S(2)}, u32[]{:S(2)}) async-start(f16[4,80,256]{2,1,0:T(8,128)(2,1)} %broadcast_in_dim.137), calls=%async_computation.12 | async-start | bytes 327680 | tf_op jit(solution)/shard_map/all_to_all | solution.py:21
  270.3 3.4 %all-to-all-done.12 = f16[4,80,256]{2,1,0:T(8,128)(2,1)S(1)} async-done(((f16[4,80,256]{2,1,0:T(8,128)(2,1)}), f16[4,80,256]{2,1,0:T(8,128)(2,1)S(1)}, u32[]{:S(2)}, u32[]{:S(2)}) %all-to-all-start.12) | async-done | bytes 163872 | tf_op jit(solution)/shard_map/all_to_all | solution.py:21
  274.6 3.5 %all-to-all-start.13 = ((f16[4,320,256]{2,1,0:T(8,128)(2,1)}), f16[4,320,256]{2,1,0:T(8,128)(2,1)S(1)}, u32[]{:S(2)}, u32[]{:S(2)}) async-start(f16[4,320,256]{2,1,0:T(8,128)(2,1)} %broadcast_in_dim.139), calls=%async_computation.13 | async-start | bytes 1310720 | tf_op jit(solution)/shard_map/all_to_all | solution.py:21
  279.1 7.7 %all-to-all-done.13 = f16[4,320,256]{2,1,0:T(8,128)(2,1)S(1)} async-done(((f16[4,320,256]{2,1,0:T(8,128)(2,1)}), f16[4,320,256]{2,1,0:T(8,128)(2,1)S(1)}, u32[]{:S(2)}, u32[]{:S(2)}) %all-to-all-start.13) | async-done | bytes 655392 | tf_op jit(solution)/shard_map/all_to_all | solution.py:21
  (103 shorter events, 46.4 us)
Async XLA Ops:
  0.6 9.5 %copy-start.2 = (bf16[256,512]{1,0:T(8,128)(2,1)S(1)}, bf16[256,512]{1,0:T(8,128)(2,1)}, u32[]{:S(2)}) copy-start(bf16[256,512]{1,0:T(8,128)(2,1)} %param.9) | copy-start | bytes 786436
  0.6 9.2 %copy-start = (bf16[1280,256]{1,0:T(8,128)(2,1)S(1)}, bf16[1280,256]{1,0:T(8,128)(2,1)}, u32[]{:S(2)}) copy-start(bf16[1280,256]{1,0:T(8,128)(2,1)} %param.7) | copy-start | bytes 1966084
  5.5 9.8 %all-to-all-start = ((f32[8,4,128]{2,1,0:T(4,128)}), f32[8,4,128]{2,1,0:T(4,128)}, u32[]{:S(2)}, u32[]{:S(2)}) async-start(f32[8,4,128]{2,1,0:T(4,128)} %broadcast_in_dim.66), calls=%async_computation | async-start | bytes 32768 | tf_op jit(solution)/shard_map/all_to_all | solution.py:21
  11.4 85.4 %copy-start.6 = (s32[1280]{0:T(1024)S(1)}, s32[1280]{0:T(1024)}, u32[]{:S(2)}) copy-start(s32[1280]{0:T(1024)} %param.10) | copy-start | bytes 15364
  16.0 91.4 %copy-start.5 = (s32[1280]{0:T(1024)S(1)}, s32[1280]{0:T(1024)}, u32[]{:S(2)}) copy-start(s32[1280]{0:T(1024)} %param.11) | copy-start | bytes 15364
  39.2 41.6 %all-to-all-start.2 = ((f32[8,3,128]{2,1,0:T(4,128)}), f32[8,3,128]{2,1,0:T(4,128)S(1)}, u32[]{:S(2)}, u32[]{:S(2)}) async-start(f32[8,3,128]{2,1,0:T(4,128)} %broadcast_in_dim.121), calls=%async_computation.2 | async-start | bytes 32768 | tf_op jit(solution)/shard_map/all_to_all | solution.py:21
  82.6 8.6 %all-to-all-start.3 = ((f32[8,4,128]{2,1,0:T(4,128)}), f32[8,4,128]{2,1,0:T(4,128)S(1)}, u32[]{:S(2)}, u32[]{:S(2)}) async-start(f32[8,4,128]{2,1,0:T(4,128)} %broadcast_in_dim.123), calls=%async_computation.3 | async-start | bytes 32768 | tf_op jit(solution)/shard_map/all_to_all | solution.py:21
  92.0 11.4 %all-to-all-start.4 = ((f32[16,3,128]{2,1,0:T(4,128)}), f32[16,3,128]{2,1,0:T(4,128)S(1)}, u32[]{:S(2)}, u32[]{:S(2)}) async-start(f32[16,3,128]{2,1,0:T(4,128)} %broadcast_in_dim.125), calls=%async_computation.4 | async-start | bytes 65536 | tf_op jit(solution)/shard_map/all_to_all | solution.py:21
  104.0 25.4 %all-to-all-start.5 = ((f32[8,2,128]{2,1,0:T(2,128)}), f32[8,2,128]{2,1,0:T(2,128)S(1)}, u32[]{:S(2)}, u32[]{:S(2)}) async-start(f32[8,2,128]{2,1,0:T(2,128)} %broadcast_in_dim.127), calls=%async_computation.5 | async-start | bytes 16384 | tf_op jit(solution)/shard_map/all_to_all | solution.py:21
  131.0 8.6 %all-to-all-start.6 = ((f32[8,4,128]{2,1,0:T(4,128)}), f32[8,4,128]{2,1,0:T(4,128)S(1)}, u32[]{:S(2)}, u32[]{:S(2)}) async-start(f32[8,4,128]{2,1,0:T(4,128)} %broadcast_in_dim.129), calls=%async_computation.6 | async-start | bytes 32768 | tf_op jit(solution)/shard_map/all_to_all | solution.py:21
  141.5 11.5 %all-to-all-start.7 = ((f32[16,2,128]{2,1,0:T(2,128)}), f32[16,2,128]{2,1,0:T(2,128)S(1)}, u32[]{:S(2)}, u32[]{:S(2)}) async-start(f32[16,2,128]{2,1,0:T(2,128)} %broadcast_in_dim.131), calls=%async_computation.7 | async-start | bytes 32768 | tf_op jit(solution)/shard_map/all_to_all | solution.py:21
  153.6 25.4 %all-to-all-start.8 = ((f32[8,2,128]{2,1,0:T(2,128)}), f32[8,2,128]{2,1,0:T(2,128)S(1)}, u32[]{:S(2)}, u32[]{:S(2)}) async-start(f32[8,2,128]{2,1,0:T(2,128)} %broadcast_in_dim.132), calls=%async_computation.8 | async-start | bytes 16384 | tf_op jit(solution)/shard_map/all_to_all | solution.py:21
  180.2 3.6 %copy-start.1 = (bf16[1280,256]{1,0:T(8,128)(2,1)S(1)}, bf16[1280,256]{1,0:T(8,128)(2,1)}, u32[]{:S(2)}) copy-start(bf16[1280,256]{1,0:T(8,128)(2,1)} %param.7) | copy-start | bytes 1966084
  183.8 1.1 copy-start.3
  196.6 26.6 %copy-start.4 = (bf16[1280,512]{0,1:T(8,128)(2,1)S(1)}, bf16[1280,512]{0,1:T(8,128)(2,1)}, u32[]{:S(2)}) copy-start(bf16[1280,512]{0,1:T(8,128)(2,1)} %copy-done.3) | copy-start | bytes 3932164
  207.0 56.5 %all-to-all-start.11 = ((f16[8,80,256]{2,1,0:T(8,128)(2,1)}), f16[8,80,256]{2,1,0:T(8,128)(2,1)S(1)}, u32[]{:S(2)}, u32[]{:S(2)}) async-start(f16[8,80,256]{2,1,0:T(8,128)(2,1)} %broadcast_in_dim.136), calls=%async_computation.11 | async-start | bytes 655360 | tf_op jit(solution)/shard_map/all_to_all | solution.py:21
  224.1 3.4 %collective-permute-start = (f32[128,512]{1,0:T(8,128)S(1)}, f32[128,512]{1,0:T(8,128)S(1)}, u32[]{:S(2)}, u32[]{:S(2)}) collective-permute-start(f32[128,512]{1,0:T(8,128)S(1)} %constant_dynamic-slice_fusion.4), channel_id=1, source_target_pairs={{0,128},{128,0},{1,129},{129,1},{2,130},{130,2},{3,131},{131,3},{4... | collective-permute-start | bytes 786440 | tf_op jit(solution)/shard_map/ppermute | solution.py:39
  227.6 9.5 %collective-permute-start.1 = (f32[32,512]{1,0:T(8,128)S(1)}, f32[32,512]{1,0:T(8,128)S(1)}, u32[]{:S(2)}, u32[]{:S(2)}) collective-permute-start(f32[32,512]{1,0:T(8,128)S(1)} %get-tuple-element.15), channel_id=1, source_target_pairs={{0,256},{256,512},{512,768},{768,0},{1,257},{257,513},{513,769},{7... | collective-permute-start | bytes 196616 | tf_op jit(solution)/shard_map/ppermute | solution.py:39
  230.1 7.7 %collective-permute-start.2 = (f32[32,512]{1,0:T(8,128)S(1)}, f32[32,512]{1,0:T(8,128)S(1)}, u32[]{:S(2)}, u32[]{:S(2)}) collective-permute-start(f32[32,512]{1,0:T(8,128)S(1)} %get-tuple-element.17), channel_id=1, source_target_pairs={{0,512},{256,768},{512,0},{768,256},{1,513},{257,769},{513,1},{769... | collective-permute-start | bytes 196616 | tf_op jit(solution)/shard_map/ppermute | solution.py:39
  234.1 6.2 %collective-permute-start.3 = (f32[32,512]{1,0:T(8,128)S(1)}, f32[32,512]{1,0:T(8,128)S(1)}, u32[]{:S(2)}, u32[]{:S(2)}) collective-permute-start(f32[32,512]{1,0:T(8,128)S(1)} %get-tuple-element.16), channel_id=1, source_target_pairs={{0,768},{256,0},{512,256},{768,512},{1,769},{257,1},{513,257},{769... | collective-permute-start | bytes 196616 | tf_op jit(solution)/shard_map/ppermute | solution.py:39
  240.3 9.3 %collective-permute-start.4 = (f32[32,512]{1,0:T(8,128)S(1)}, f32[32,512]{1,0:T(8,128)S(1)}, u32[]{:S(2)}, u32[]{:S(2)}) collective-permute-start(f32[32,512]{1,0:T(8,128)S(1)} %add_add_fusion), channel_id=1, source_target_pairs={{0,768},{256,0},{512,256},{768,512},{1,769},{257,1},{513,257},{769... | collective-permute-start | bytes 196616 | tf_op jit(solution)/shard_map/ppermute | solution.py:39
  244.5 23.7 %collective-permute-start.5 = (f32[32,512]{1,0:T(8,128)S(1)}, f32[32,512]{1,0:T(8,128)S(1)}, u32[]{:S(2)}, u32[]{:S(2)}) collective-permute-start(f32[32,512]{1,0:T(8,128)S(1)} %add_add_fusion), channel_id=1, source_target_pairs={{0,512},{256,768},{512,0},{768,256},{1,513},{257,769},{513,1},{769... | collective-permute-start | bytes 196616 | tf_op jit(solution)/shard_map/ppermute | solution.py:39
  247.6 20.6 %collective-permute-start.6 = (f32[32,512]{1,0:T(8,128)S(1)}, f32[32,512]{1,0:T(8,128)S(1)}, u32[]{:S(2)}, u32[]{:S(2)}) collective-permute-start(f32[32,512]{1,0:T(8,128)S(1)} %add_add_fusion), channel_id=1, source_target_pairs={{0,256},{256,512},{512,768},{768,0},{1,257},{257,513},{513,769},{7... | collective-permute-start | bytes 196616 | tf_op jit(solution)/shard_map/ppermute | solution.py:39
  264.2 9.5 %all-to-all-start.12 = ((f16[4,80,256]{2,1,0:T(8,128)(2,1)}), f16[4,80,256]{2,1,0:T(8,128)(2,1)S(1)}, u32[]{:S(2)}, u32[]{:S(2)}) async-start(f16[4,80,256]{2,1,0:T(8,128)(2,1)} %broadcast_in_dim.137), calls=%async_computation.12 | async-start | bytes 327680 | tf_op jit(solution)/shard_map/all_to_all | solution.py:21
  268.4 9.7 %collective-permute-start.7 = (f32[128,512]{1,0:T(8,128)S(1)}, f32[128,512]{1,0:T(8,128)S(1)}, u32[]{:S(2)}, u32[]{:S(2)}) collective-permute-start(f32[128,512]{1,0:T(8,128)S(1)} %constant_dynamic-slice_fusion), channel_id=1, source_target_pairs={{0,128},{128,0},{1,129},{129,1},{2,130},{130,2},{3,131},{131,3},{4... | collective-permute-start | bytes 786440 | tf_op jit(solution)/shard_map/ppermute | solution.py:39
  274.6 12.2 %all-to-all-start.13 = ((f16[4,320,256]{2,1,0:T(8,128)(2,1)}), f16[4,320,256]{2,1,0:T(8,128)(2,1)S(1)}, u32[]{:S(2)}, u32[]{:S(2)}) async-start(f16[4,320,256]{2,1,0:T(8,128)(2,1)} %broadcast_in_dim.139), calls=%async_computation.13 | async-start | bytes 1310720 | tf_op jit(solution)/shard_map/all_to_all | solution.py:21

commit v7 on v6

--- a/solution.py
+++ b/solution.py
@@ -80,27 +80,37 @@
     n_teach, n_crop, near = t_bf.shape[0], x_bf.shape[0], lax.axis_size(NEAR)
     own_crops = n_crop // near
     image_here = crop_image - lax.axis_index(DP) * img_local
-    keep_first = (crop_global != 0).astype(jnp.float32)[:, None]
-    keep_second = (crop_global != 1).astype(jnp.float32)[:, None]
+    first_at, second_at = GLOBALS * image_here, GLOBALS * image_here + 1
+    keep_first = (crop_global != 0).astype(jnp.float32)
+    keep_second = (crop_global != 1).astype(jnp.float32)
+    prep = (first_at, second_at, keep_first, keep_second)
+    first_at, second_at, keep_first, keep_second = lax.optimization_barrier(prep)
+    keep_first, keep_second = keep_first[:, None], keep_second[:, None]
     for step in range(ITERS):
         part_col = jnp.sum(q_mat, axis=0)
-        q_mat = q_mat / spread_sum(part_col, DP)[None, :] / total_protos
+        col_tot = spread_sum(part_col, DP)
+        q_mat = q_mat / col_tot[None, :] / total_protos
         part_row = jnp.sum(q_mat, axis=1)
         if step == 0:
             own = jnp.pad(part_total.reshape(near, -1), ((0, 0), (0, -own_crops % 128)))
             rows = jnp.broadcast_to(part_row[None], (near, n_teach))
             sent = jnp.concatenate([rows, own], axis=1).reshape(near, -1, 128)
             both = spread_sum(jnp.sum(lax.all_to_all(sent, NEAR, 0, 0), axis=0), "zh")
-            row_tot, own_total = both[:n_teach], both[n_teach:]
+            row_tot = both[:n_teach]
         elif step == 1:
-            both = spread(jnp.concatenate([part_row, own_total]).reshape(-1, 128), NEAR)
-            both = both.reshape(near, -1)
-            total = both[:, n_teach : n_teach + own_crops].reshape(-1)
-            row_tot = spread_sum(jnp.sum(both[:, :n_teach], axis=0), "zh")
+            both, part_row = lax.optimization_barrier((both, part_row))
+            sent = jnp.concatenate([part_row, both[n_teach:]])
+            both = spread(sent.reshape(-1, 128), NEAR)
+            near_row = jnp.sum(both.reshape(near, -1)[:, :n_teach], axis=0)
+            row_tot = spread_sum(near_row, "zh")
         else:
-            first = jnp.take(q_mat, GLOBALS * image_here, axis=0)
-            second = jnp.take(q_mat, GLOBALS * image_here + 1, axis=0)
-            row_tot = spread_sum(part_row, NEAR, "zh")
+            near_row = spread_sum(part_row, NEAR)
+            late = (near_row, both, first_at, second_at)
+            near_row, both, first_at, second_at = lax.optimization_barrier(late)
+            total = both.reshape(near, -1)[:, n_teach : n_teach + own_crops].reshape(-1)
+            first = q_mat.at[first_at].get(mode="promise_in_bounds")
+            second = q_mat.at[second_at].get(mode="promise_in_bounds")
+            row_tot = spread_sum(near_row, "zh")
         if step + 1 < ITERS:
             q_mat = q_mat / row_tot[:, None] / teach_total
     teach_ids = lax.broadcasted_iota(jnp.int32, (1, n_teach), 1)
@@ -108,25 +118,26 @@
     def of_crop(index):
         return jnp.sum(jnp.where(index[:, None] == teach_ids, row_tot[None], 0.0), axis=1)
 
-    first = first / of_crop(GLOBALS * image_here)[:, None] / teach_total * teach_total
-    second = second / of_crop(GLOBALS * image_here + 1)[:, None] / teach_total * teach_total
+    first = first / of_crop(first_at)[:, None] / teach_total * teach_total
+    second = second / of_crop(second_at)[:, None] / teach_total * teach_total
     probs = expo / total[:, None]
     target_rows = first * keep_first + second * keep_second
     count = keep_first + keep_second
     scale_out = total_protos / 64.0
     grad_bf = (scale_out * (count * probs - target_rows) / 0.1).astype(jnp.bfloat16)
-    dwn_part = lax.dot_general(
-        x_bf, grad_bf, (((0,), (0,)), ((), ())), preferred_element_type=jnp.float32
-    )
     dxn = lax.dot_general(
         grad_bf, w_bf, (((1,), (1,)), ((), ())), preferred_element_type=jnp.float32
     )
-    dwn_total = dwn_reduce(dwn_part)
     dxn = dxn - x_norm * jnp.sum(x_norm * dxn, axis=1, keepdims=True)
     got = swap(dxn.astype(jnp.float16), "y")
     dxn = jnp.sum(got.astype(jnp.float32), axis=0)
     got = swap(dxn.astype(jnp.float16), "zl")
     dxn = jnp.sum(got.astype(jnp.float32), axis=0)
+    dxn, grad_bf = lax.optimization_barrier((dxn, grad_bf))
+    dwn_part = lax.dot_general(
+        x_bf, grad_bf, (((0,), (0,)), ((), ())), preferred_element_type=jnp.float32
+    )
+    dwn_total = dwn_reduce(dwn_part)
     got = spread(dxn.astype(jnp.float16), "zh")
     dxn = jnp.sum(got.astype(jnp.float32), axis=0).astype(jnp.float16)
     for axes in ("zl", "y"):

time: 290 us -> 284 us (0.979)
  blocking collectives: 42 us -> 126 us
  waiting for transfers between devices: 105 us -> 51.3 us
  starting transfers between devices: 93.2 us -> 60.8 us
    all_to_all x0 -> x4, blocking collectives: none -> 84.4 us  [spread(): lax.all_to_all(jnp.broadcast_to(part[None], (n,) + part.shape), axes, 0, 0)]
    all_to_all x11 -> x7, waiting for transfers between devices: 101 us -> 41 us  [spread(): lax.all_to_all(jnp.broadcast_to(part[None], (n,) + part.shape), axes, 0, 0)]
    all_to_all x11 -> x7, starting transfers between devices: 70.6 us -> 39 us  [spread(): lax.all_to_all(jnp.broadcast_to(part[None], (n,) + part.shape), axes, 0, 0)]
    ppermute x8, waiting for transfers between devices: 4.52 us -> 10.2 us  [shifted(): return lax.ppermute(part, axis, [(i, (i + step) % n) for i in range(n)])]
  transfers between devices with their start and end apart: 19 -> 15, of which waited for: 14 -> 10; matrix products, arithmetic and copies ran while one was open for 8% -> 8% of each run, Pallas kernels for 0% -> 0%
where the time goes in v7:
time: 284 us; the launch traced here: 283 us
  blocking collectives  126 us (44%)
  starting transfers between devices  60.8 us (21%)
  waiting for transfers between devices  51.3 us (18%)
  local copies, waits for them, and re-layouts  22 us (8%)
  other arithmetic  16.2 us (6%)
  matrix products  5.08 us (2%)
    all_to_all x4, blocking collectives, spread(): lax.all_to_all(jnp.broadcast_to(part[None], (n,) + part.shape), axes, 0, 0)  84.4 us
    all_to_all x7, waiting for transfers between devices, spread(): lax.all_to_all(jnp.broadcast_to(part[None], (n,) + part.shape), axes, 0, 0)  41 us
    all_to_all x7, starting transfers between devices, spread(): lax.all_to_all(jnp.broadcast_to(part[None], (n,) + part.shape), axes, 0, 0)  39 us
    ppermute x8, starting transfers between devices, shifted(): return lax.ppermute(part, axis, [(i, (i + step) % n) for i in range(n)])  21.8 us
    all_to_all x1, blocking collectives, on_device(): both = spread_sum(jnp.sum(lax.all_to_all(sent, NEAR, 0, 0), axis=0), 'zh')  21.3 us
    all_to_all x2, blocking collectives, swap(): return lax.all_to_all(pieces, axes, 0, 0)  20.7 us
    ppermute x8, waiting for transfers between devices, shifted(): return lax.ppermute(part, axis, [(i, (i + step) % n) for i in range(n)])  10.2 us
    gather x2, local copies, waits for them, and re-layouts, on_device(): first = q_mat.at[first_at].get(mode='promise_in_bounds')  7.66 us
  transfers between devices with their start and end apart: 15, of which 10 were waited for; matrix products, arithmetic and copies ran while one was open for 8% of the time, Pallas kernels for 0%

profile of v7, /device:TPU:32, one launch (start us, length us, event | category | flops | bytes accessed | tf_op | source)
XLA Modules:
  0.0 282.9 jit_solution(13545320163520943252)
XLA Ops:
  5.5 4.3 %all-to-all-start = ((f32[8,4,128]{2,1,0:T(4,128)}), f32[8,4,128]{2,1,0:T(4,128)}, u32[]{:S(2)}, u32[]{:S(2)}) async-start(f32[8,4,128]{2,1,0:T(4,128)} %broadcast_in_dim.117), calls=%async_computation | async-start | bytes 32768 | tf_op jit(solution)/shard_map/all_to_all | solution.py:21
  12.2 3.1 %all-to-all-done = f32[8,4,128]{2,1,0:T(4,128)} async-done(((f32[8,4,128]{2,1,0:T(4,128)}), f32[8,4,128]{2,1,0:T(4,128)}, u32[]{:S(2)}, u32[]{:S(2)}) %all-to-all-start) | async-done | bytes 16416 | tf_op jit(solution)/shard_map/all_to_all | solution.py:21
  17.2 21.3 %all_to_all.70 = f32[16,3,128]{2,1,0:T(4,128)S(1)} all-to-all(f32[16,3,128]{2,1,0:T(4,128)S(1)} %reshape.83), channel_id=1, replica_groups=mesh['x'=4,'core'=2,'y'=4,'zh'=8,'zl'=4] {'y','zl'}, dimensions={0} | all-to-all | bytes 49152 | tf_op jit(solution)/shard_map/all_to_all | solution.py:98
  38.5 41.3 %all_to_all.71 = f32[8,3,128]{2,1,0:T(4,128)S(1)} all-to-all(f32[8,3,128]{2,1,0:T(4,128)S(1)} %broadcast_in_dim.119), channel_id=1, replica_groups=mesh['x'=4,'core'=2,'y'=4,'zh'=8,'zl'=4] {'zh'}, dimensions={0} | all-to-all | bytes 24576 | tf_op jit(solution)/shard_map/all_to_all | solution.py:21
  81.1 7.7 %all_to_all.72 = f32[8,4,128]{2,1,0:T(4,128)S(1)} all-to-all(f32[8,4,128]{2,1,0:T(4,128)S(1)} %broadcast_in_dim.121), channel_id=1, replica_groups=mesh['x'=4,'core'=2,'y'=4,'zh'=8,'zl'=4] {'x','core'}, dimensions={0} | all-to-all | bytes 32768 | tf_op jit(solution)/shard_map/all_to_all | solution.py:21
  89.1 10.9 %all_to_all.73 = f32[16,3,128]{2,1,0:T(4,128)S(1)} all-to-all(f32[16,3,128]{2,1,0:T(4,128)S(1)} %broadcast_in_dim.123), channel_id=1, replica_groups=mesh['x'=4,'core'=2,'y'=4,'zh'=8,'zl'=4] {'y','zl'}, dimensions={0} | all-to-all | bytes 49152 | tf_op jit(solution)/shard_map/all_to_all | solution.py:21
  100.0 24.5 %all_to_all.74 = f32[8,2,128]{2,1,0:T(2,128)S(1)} all-to-all(f32[8,2,128]{2,1,0:T(2,128)S(1)} %broadcast_in_dim.125), channel_id=1, replica_groups=mesh['x'=4,'core'=2,'y'=4,'zh'=8,'zl'=4] {'zh'}, dimensions={0} | all-to-all | bytes 16384 | tf_op jit(solution)/shard_map/all_to_all | solution.py:21
  126.1 3.3 %all-to-all-start.6 = ((f32[8,4,128]{2,1,0:T(4,128)}), f32[8,4,128]{2,1,0:T(4,128)S(1)}, u32[]{:S(2)}, u32[]{:S(2)}) async-start(f32[8,4,128]{2,1,0:T(4,128)} %broadcast_in_dim.127), calls=%async_computation.6 | async-start | bytes 32768 | tf_op jit(solution)/shard_map/all_to_all | solution.py:21
  129.5 5.2 %all-to-all-done.6 = f32[8,4,128]{2,1,0:T(4,128)S(1)} async-done(((f32[8,4,128]{2,1,0:T(4,128)}), f32[8,4,128]{2,1,0:T(4,128)S(1)}, u32[]{:S(2)}, u32[]{:S(2)}) %all-to-all-start.6) | async-done | bytes 16416 | tf_op jit(solution)/shard_map/all_to_all | solution.py:21
  136.5 4.8 %all-to-all-start.7 = ((f32[16,2,128]{2,1,0:T(2,128)}), f32[16,2,128]{2,1,0:T(2,128)S(1)}, u32[]{:S(2)}, u32[]{:S(2)}) async-start(f32[16,2,128]{2,1,0:T(2,128)} %broadcast_in_dim.129), calls=%async_computation.7 | async-start | bytes 32768 | tf_op jit(solution)/shard_map/all_to_all | solution.py:21
  142.0 6.0 %all-to-all-done.7 = f32[16,2,128]{2,1,0:T(2,128)S(1)} async-done(((f32[16,2,128]{2,1,0:T(2,128)}), f32[16,2,128]{2,1,0:T(2,128)S(1)}, u32[]{:S(2)}, u32[]{:S(2)}) %all-to-all-start.7) | async-done | bytes 16416 | tf_op jit(solution)/shard_map/all_to_all | solution.py:21
  149.2 3.3 %all-to-all-start.8 = ((f32[8,2,128]{2,1,0:T(2,128)}), f32[8,2,128]{2,1,0:T(2,128)S(1)}, u32[]{:S(2)}, u32[]{:S(2)}) async-start(f32[8,2,128]{2,1,0:T(2,128)} %broadcast_in_dim.132), calls=%async_computation.8 | async-start | bytes 16384 | tf_op jit(solution)/shard_map/all_to_all | solution.py:21
  152.6 4.4 %gather_fusion = f32[1280,512]{1,0:T(8,128)} fusion(f32[256,512]{1,0:T(8,128)S(1)} %get-tuple-element.31, s32[2048]{0:T(1024)S(1)} %pad_clamp_fusion.1), kind=kCustom, calls=%fused_computation | custom fusion | bytes 5248000 | tf_op jit(solution)/shard_map/gather | solution.py:111
  157.1 3.2 %copy.20 = f32[1280,512]{0,1:T(8,128)} copy(f32[1280,512]{1,0:T(8,128)} %gather_fusion) | data formatting | bytes 5242880 | tf_op jit(solution)/shard_map/gather | solution.py:111
  160.3 4.4 %gather_fusion.1 = f32[1280,512]{1,0:T(8,128)} fusion(f32[256,512]{1,0:T(8,128)S(1)} %get-tuple-element.31, s32[2048]{0:T(1024)S(1)} %pad_clamp_fusion), kind=kCustom, calls=%fused_computation.1 | custom fusion | bytes 5248000 | tf_op jit(solution)/shard_map/gather | solution.py:112
  164.7 3.3 %copy.21 = f32[1280,512]{0,1:T(8,128)} copy(f32[1280,512]{1,0:T(8,128)} %gather_fusion.1) | data formatting | bytes 5242880 | tf_op jit(solution)/shard_map/gather | solution.py:112
  167.9 6.7 %all-to-all-done.8 = f32[8,2,128]{2,1,0:T(2,128)S(1)} async-done(((f32[8,2,128]{2,1,0:T(2,128)}), f32[8,2,128]{2,1,0:T(2,128)S(1)}, u32[]{:S(2)}, u32[]{:S(2)}) %all-to-all-start.8) | async-done | bytes 8224 | tf_op jit(solution)/shard_map/all_to_all | solution.py:21
  175.8 3.5 %multiply_convert_fusion = bf16[1280,512]{0,1:T(8,128)(2,1)S(1)} fusion(f32[1280,512]{0,1:T(8,128)} %copy.21, f32[1280,512]{0,1:T(8,128)} %copy.20, f32[1280,512]{0,1:T(8,128)S(1)} %get-tuple-element.44, f32[1280]{0:T(1024)} %copy-done.5, f32[1280]{0:T(1024)S(1)} %get-tuple-element.27, f32[1280]{0:T(1024)} %copy-done.6, f32[1280]{0:T(1024)S(1)} %get-tuple-element.26, ...), kind=kLoop, calls=%fused_computation.4 | loop fusion | flops 6553600 | bytes 9205760 | tf_op jit(solution)/shard_map/convert_element_type | solution.py:127
  180.8 11.2 %all_to_all.75 = f16[4,320,256]{2,1,0:T(8,128)(2,1)S(1)} all-to-all(f16[4,320,256]{2,1,0:T(8,128)(2,1)S(1)} %bitcast.33), channel_id=1, replica_groups=mesh['x'=4,'core'=2,'y'=4,'zh'=8,'zl'=4] {'y'}, dimensions={0} | all-to-all | bytes 1310720 | tf_op jit(solution)/shard_map/all_to_all | solution.py:27
  192.2 9.5 %all_to_all.76 = f16[4,80,256]{2,1,0:T(8,128)(2,1)S(1)} all-to-all(f16[4,80,256]{2,1,0:T(8,128)(2,1)S(1)} %bitcast.35), channel_id=1, replica_groups=mesh['x'=4,'core'=2,'y'=4,'zh'=8,'zl'=4] {'zl'}, dimensions={0} | all-to-all | bytes 327680 | tf_op jit(solution)/shard_map/all_to_all | solution.py:27
  202.4 15.6 %all-to-all-start.11 = ((f16[8,80,256]{2,1,0:T(8,128)(2,1)}), f16[8,80,256]{2,1,0:T(8,128)(2,1)S(1)}, u32[]{:S(2)}, u32[]{:S(2)}) async-start(f16[8,80,256]{2,1,0:T(8,128)(2,1)} %broadcast_in_dim.137), calls=%async_computation.11 | async-start | bytes 655360 | tf_op jit(solution)/shard_map/all_to_all | solution.py:21
  222.5 2.5 collective-permute-start.1
  224.9 4.6 %collective-permute-start.3 = (f32[32,512]{1,0:T(8,128)S(1)}, f32[32,512]{1,0:T(8,128)S(1)}, u32[]{:S(2)}, u32[]{:S(2)}) collective-permute-start(f32[32,512]{1,0:T(8,128)S(1)} %get-tuple-element.39), channel_id=1, source_target_pairs={{0,768},{256,0},{512,256},{768,512},{1,769},{257,1},{513,257},{769... | collective-permute-start | bytes 196616 | tf_op jit(solution)/shard_map/ppermute | solution.py:39
  231.5 5.7 %collective-permute-done.2 = f32[32,512]{1,0:T(8,128)S(1)} collective-permute-done((f32[32,512]{1,0:T(8,128)S(1)}, f32[32,512]{1,0:T(8,128)S(1)}, u32[]{:S(2)}, u32[]{:S(2)}) %collective-permute-start.2) | collective-permute-done | bytes 65568 | tf_op jit(solution)/shard_map/ppermute | solution.py:39
  239.1 3.4 %collective-permute-start.5 = (f32[32,512]{1,0:T(8,128)S(1)}, f32[32,512]{1,0:T(8,128)S(1)}, u32[]{:S(2)}, u32[]{:S(2)}) collective-permute-start(f32[32,512]{1,0:T(8,128)S(1)} %add_add_fusion), channel_id=1, source_target_pairs={{0,512},{256,768},{512,0},{768,256},{1,513},{257,769},{513,1},{769... | collective-permute-start | bytes 196616 | tf_op jit(solution)/shard_map/ppermute | solution.py:39
  242.5 3.7 %collective-permute-start.4 = (f32[32,512]{1,0:T(8,128)S(1)}, f32[32,512]{1,0:T(8,128)S(1)}, u32[]{:S(2)}, u32[]{:S(2)}) collective-permute-start(f32[32,512]{1,0:T(8,128)S(1)} %add_add_fusion), channel_id=1, source_target_pairs={{0,768},{256,0},{512,256},{768,512},{1,769},{257,1},{513,257},{769... | collective-permute-start | bytes 196616 | tf_op jit(solution)/shard_map/ppermute | solution.py:39
  246.2 3.1 %collective-permute-done.4 = f32[32,512]{1,0:T(8,128)S(1)} collective-permute-done((f32[32,512]{1,0:T(8,128)S(1)}, f32[32,512]{1,0:T(8,128)S(1)}, u32[]{:S(2)}, u32[]{:S(2)}) %collective-permute-start.4) | collective-permute-done | bytes 65568 | tf_op jit(solution)/shard_map/ppermute | solution.py:39
  249.3 9.0 %all-to-all-done.11 = f16[8,80,256]{2,1,0:T(8,128)(2,1)S(1)} async-done(((f16[8,80,256]{2,1,0:T(8,128)(2,1)}), f16[8,80,256]{2,1,0:T(8,128)(2,1)S(1)}, u32[]{:S(2)}, u32[]{:S(2)}) %all-to-all-start.11) | async-done | bytes 327712 | tf_op jit(solution)/shard_map/all_to_all | solution.py:21
  259.0 4.0 %all-to-all-start.12 = ((f16[4,80,256]{2,1,0:T(8,128)(2,1)}), f16[4,80,256]{2,1,0:T(8,128)(2,1)S(1)}, u32[]{:S(2)}, u32[]{:S(2)}) async-start(f16[4,80,256]{2,1,0:T(8,128)(2,1)} %broadcast_in_dim.138), calls=%async_computation.12 | async-start | bytes 327680 | tf_op jit(solution)/shard_map/all_to_all | solution.py:21
  265.2 3.4 %all-to-all-done.12 = f16[4,80,256]{2,1,0:T(8,128)(2,1)S(1)} async-done(((f16[4,80,256]{2,1,0:T(8,128)(2,1)}), f16[4,80,256]{2,1,0:T(8,128)(2,1)S(1)}, u32[]{:S(2)}, u32[]{:S(2)}) %all-to-all-start.12) | async-done | bytes 163872 | tf_op jit(solution)/shard_map/all_to_all | solution.py:21
  269.4 3.5 %all-to-all-start.13 = ((f16[4,320,256]{2,1,0:T(8,128)(2,1)}), f16[4,320,256]{2,1,0:T(8,128)(2,1)S(1)}, u32[]{:S(2)}, u32[]{:S(2)}) async-start(f16[4,320,256]{2,1,0:T(8,128)(2,1)} %broadcast_in_dim.140), calls=%async_computation.13 | async-start | bytes 1310720 | tf_op jit(solution)/shard_map/all_to_all | solution.py:21
  274.0 7.7 %all-to-all-done.13 = f16[4,320,256]{2,1,0:T(8,128)(2,1)S(1)} async-done(((f16[4,320,256]{2,1,0:T(8,128)(2,1)}), f16[4,320,256]{2,1,0:T(8,128)(2,1)S(1)}, u32[]{:S(2)}, u32[]{:S(2)}) %all-to-all-start.13) | async-done | bytes 655392 | tf_op jit(solution)/shard_map/all_to_all | solution.py:21
  (105 shorter events, 33.6 us)
Async XLA Ops:
  0.6 9.5 %copy-start.2 = (bf16[256,512]{1,0:T(8,128)(2,1)S(1)}, bf16[256,512]{1,0:T(8,128)(2,1)}, u32[]{:S(2)}) copy-start(bf16[256,512]{1,0:T(8,128)(2,1)} %param.7) | copy-start | bytes 786436
  0.6 9.2 %copy-start = (bf16[1280,256]{1,0:T(8,128)(2,1)S(1)}, bf16[1280,256]{1,0:T(8,128)(2,1)}, u32[]{:S(2)}) copy-start(bf16[1280,256]{1,0:T(8,128)(2,1)} %param.5) | copy-start | bytes 1966084
  5.5 9.8 %all-to-all-start = ((f32[8,4,128]{2,1,0:T(4,128)}), f32[8,4,128]{2,1,0:T(4,128)}, u32[]{:S(2)}, u32[]{:S(2)}) async-start(f32[8,4,128]{2,1,0:T(4,128)} %broadcast_in_dim.117), calls=%async_computation | async-start | bytes 32768 | tf_op jit(solution)/shard_map/all_to_all | solution.py:21
  79.9 49.5 %copy-start.7 = (s32[1280]{0:T(1024)S(1)}, s32[1280]{0:T(1024)}, u32[]{:S(2)}) copy-start(s32[1280]{0:T(1024)} %param.9) | copy-start | bytes 15364
  89.0 52.3 %copy-start.8 = (s32[1280]{0:T(1024)S(1)}, s32[1280]{0:T(1024)}, u32[]{:S(2)}) copy-start(s32[1280]{0:T(1024)} %param.8) | copy-start | bytes 15364
  126.1 8.6 %all-to-all-start.6 = ((f32[8,4,128]{2,1,0:T(4,128)}), f32[8,4,128]{2,1,0:T(4,128)S(1)}, u32[]{:S(2)}, u32[]{:S(2)}) async-start(f32[8,4,128]{2,1,0:T(4,128)} %broadcast_in_dim.127), calls=%async_computation.6 | async-start | bytes 32768 | tf_op jit(solution)/shard_map/all_to_all | solution.py:21
  129.4 27.6 %copy-start.5 = (f32[1280]{0:T(1024)}, f32[1280]{0:T(1024)S(1)}, u32[]{:S(2)}) copy-start(f32[1280]{0:T(1024)S(1)} %get-tuple-element.15) | copy-start | bytes 15364
  129.4 27.6 %copy-start.6 = (f32[1280]{0:T(1024)}, f32[1280]{0:T(1024)S(1)}, u32[]{:S(2)}) copy-start(f32[1280]{0:T(1024)S(1)} %get-tuple-element.14) | copy-start | bytes 15364
  136.5 11.4 %all-to-all-start.7 = ((f32[16,2,128]{2,1,0:T(2,128)}), f32[16,2,128]{2,1,0:T(2,128)S(1)}, u32[]{:S(2)}, u32[]{:S(2)}) async-start(f32[16,2,128]{2,1,0:T(2,128)} %broadcast_in_dim.129), calls=%async_computation.7 | async-start | bytes 32768 | tf_op jit(solution)/shard_map/all_to_all | solution.py:21
  149.2 25.4 %all-to-all-start.8 = ((f32[8,2,128]{2,1,0:T(2,128)}), f32[8,2,128]{2,1,0:T(2,128)S(1)}, u32[]{:S(2)}, u32[]{:S(2)}) async-start(f32[8,2,128]{2,1,0:T(2,128)} %broadcast_in_dim.132), calls=%async_computation.8 | async-start | bytes 16384 | tf_op jit(solution)/shard_map/all_to_all | solution.py:21
  175.8 3.5 %copy-start.1 = (bf16[1280,256]{1,0:T(8,128)(2,1)S(1)}, bf16[1280,256]{1,0:T(8,128)(2,1)}, u32[]{:S(2)}) copy-start(bf16[1280,256]{1,0:T(8,128)(2,1)} %param.5) | copy-start | bytes 1966084
  179.3 1.1 copy-start.3
  192.1 26.0 %copy-start.4 = (bf16[1280,512]{0,1:T(8,128)(2,1)S(1)}, bf16[1280,512]{0,1:T(8,128)(2,1)}, u32[]{:S(2)}) copy-start(bf16[1280,512]{0,1:T(8,128)(2,1)} %copy-done.3) | copy-start | bytes 3932164
  202.4 55.9 %all-to-all-start.11 = ((f16[8,80,256]{2,1,0:T(8,128)(2,1)}), f16[8,80,256]{2,1,0:T(8,128)(2,1)S(1)}, u32[]{:S(2)}, u32[]{:S(2)}) async-start(f16[8,80,256]{2,1,0:T(8,128)(2,1)} %broadcast_in_dim.137), calls=%async_computation.11 | async-start | bytes 655360 | tf_op jit(solution)/shard_map/all_to_all | solution.py:21
  218.9 3.4 %collective-permute-start = (f32[128,512]{1,0:T(8,128)S(1)}, f32[128,512]{1,0:T(8,128)S(1)}, u32[]{:S(2)}, u32[]{:S(2)}) collective-permute-start(f32[128,512]{1,0:T(8,128)S(1)} %constant_dynamic-slice_fusion.4), channel_id=1, source_target_pairs={{0,128},{128,0},{1,129},{129,1},{2,130},{130,2},{3,131},{131,3},{4... | collective-permute-start | bytes 786440 | tf_op jit(solution)/shard_map/ppermute | solution.py:39
  222.5 9.0 %collective-permute-start.1 = (f32[32,512]{1,0:T(8,128)S(1)}, f32[32,512]{1,0:T(8,128)S(1)}, u32[]{:S(2)}, u32[]{:S(2)}) collective-permute-start(f32[32,512]{1,0:T(8,128)S(1)} %get-tuple-element.38), channel_id=1, source_target_pairs={{0,256},{256,512},{512,768},{768,0},{1,257},{257,513},{513,769},{7... | collective-permute-start | bytes 196616 | tf_op jit(solution)/shard_map/ppermute | solution.py:39
  224.9 6.5 %collective-permute-start.3 = (f32[32,512]{1,0:T(8,128)S(1)}, f32[32,512]{1,0:T(8,128)S(1)}, u32[]{:S(2)}, u32[]{:S(2)}) collective-permute-start(f32[32,512]{1,0:T(8,128)S(1)} %get-tuple-element.39), channel_id=1, source_target_pairs={{0,768},{256,0},{512,256},{768,512},{1,769},{257,1},{513,257},{769... | collective-permute-start | bytes 196616 | tf_op jit(solution)/shard_map/ppermute | solution.py:39
  229.5 7.7 %collective-permute-start.2 = (f32[32,512]{1,0:T(8,128)S(1)}, f32[32,512]{1,0:T(8,128)S(1)}, u32[]{:S(2)}, u32[]{:S(2)}) collective-permute-start(f32[32,512]{1,0:T(8,128)S(1)} %get-tuple-element.40), channel_id=1, source_target_pairs={{0,512},{256,768},{512,0},{768,256},{1,513},{257,769},{513,1},{769... | collective-permute-start | bytes 196616 | tf_op jit(solution)/shard_map/ppermute | solution.py:39
  237.2 25.9 %collective-permute-start.6 = (f32[32,512]{1,0:T(8,128)S(1)}, f32[32,512]{1,0:T(8,128)S(1)}, u32[]{:S(2)}, u32[]{:S(2)}) collective-permute-start(f32[32,512]{1,0:T(8,128)S(1)} %add_add_fusion), channel_id=1, source_target_pairs={{0,256},{256,512},{512,768},{768,0},{1,257},{257,513},{513,769},{7... | collective-permute-start | bytes 196616 | tf_op jit(solution)/shard_map/ppermute | solution.py:39
  239.1 24.0 %collective-permute-start.5 = (f32[32,512]{1,0:T(8,128)S(1)}, f32[32,512]{1,0:T(8,128)S(1)}, u32[]{:S(2)}, u32[]{:S(2)}) collective-permute-start(f32[32,512]{1,0:T(8,128)S(1)} %add_add_fusion), channel_id=1, source_target_pairs={{0,512},{256,768},{512,0},{768,256},{1,513},{257,769},{513,1},{769... | collective-permute-start | bytes 196616 | tf_op jit(solution)/shard_map/ppermute | solution.py:39
  242.5 6.8 %collective-permute-start.4 = (f32[32,512]{1,0:T(8,128)S(1)}, f32[32,512]{1,0:T(8,128)S(1)}, u32[]{:S(2)}, u32[]{:S(2)}) collective-permute-start(f32[32,512]{1,0:T(8,128)S(1)} %add_add_fusion), channel_id=1, source_target_pairs={{0,768},{256,0},{512,256},{768,512},{1,769},{257,1},{513,257},{769... | collective-permute-start | bytes 196616 | tf_op jit(solution)/shard_map/ppermute | solution.py:39
  259.0 9.5 %all-to-all-start.12 = ((f16[4,80,256]{2,1,0:T(8,128)(2,1)}), f16[4,80,256]{2,1,0:T(8,128)(2,1)S(1)}, u32[]{:S(2)}, u32[]{:S(2)}) async-start(f16[4,80,256]{2,1,0:T(8,128)(2,1)} %broadcast_in_dim.138), calls=%async_computation.12 | async-start | bytes 327680 | tf_op jit(solution)/shard_map/all_to_all | solution.py:21
  263.2 9.7 %collective-permute-start.7 = (f32[128,512]{1,0:T(8,128)S(1)}, f32[128,512]{1,0:T(8,128)S(1)}, u32[]{:S(2)}, u32[]{:S(2)}) collective-permute-start(f32[128,512]{1,0:T(8,128)S(1)} %constant_dynamic-slice_fusion), channel_id=1, source_target_pairs={{0,128},{128,0},{1,129},{129,1},{2,130},{130,2},{3,131},{131,3},{4... | collective-permute-start | bytes 786440 | tf_op jit(solution)/shard_map/ppermute | solution.py:39
  269.4 12.2 %all-to-all-start.13 = ((f16[4,320,256]{2,1,0:T(8,128)(2,1)}), f16[4,320,256]{2,1,0:T(8,128)(2,1)S(1)}, u32[]{:S(2)}, u32[]{:S(2)}) async-start(f16[4,320,256]{2,1,0:T(8,128)(2,1)} %broadcast_in_dim.140), calls=%async_computation.13 | async-start | bytes 1310720 | tf_op jit(solution)/shard_map/all_to_all | solution.py:21

commit v8 on v7

--- a/solution.py
+++ b/solution.py
@@ -54,8 +54,13 @@
     own = lax.optimization_barrier(sum(sums[1:], sums[0]))
     got = [own] + [shifted(own, "x", step) for step in range(1, nx)]
     back = got[:1] + got[:0:-1]
-    start = (nx - x) % nx * piece
-    mine = lax.dynamic_slice_in_dim(jnp.concatenate(back + back, axis=0), start, half, 0)
+    return jnp.concatenate(back + back, axis=0)
+
+
+def dwn_join(ring):
+    core, x, nx = lax.axis_index("core"), lax.axis_index("x"), lax.axis_size("x")
+    half = ring.shape[0] // 2
+    mine = lax.dynamic_slice_in_dim(ring, (nx - x) % nx * (half // nx), half, 0)
     other = shifted(mine, "core", 1)
     low, high = jnp.where(core == 0, mine, other), jnp.where(core == 0, other, mine)
     return jnp.concatenate([low, high], axis=0)
@@ -83,9 +88,9 @@
     first_at, second_at = GLOBALS * image_here, GLOBALS * image_here + 1
     keep_first = (crop_global != 0).astype(jnp.float32)
     keep_second = (crop_global != 1).astype(jnp.float32)
-    prep = (first_at, second_at, keep_first, keep_second)
-    first_at, second_at, keep_first, keep_second = lax.optimization_barrier(prep)
-    keep_first, keep_second = keep_first[:, None], keep_second[:, None]
+    prep = (first_at, second_at, keep_first, keep_second, keep_first + keep_second)
+    first_at, second_at, keep_first, keep_second, count = lax.optimization_barrier(prep)
+    keep_first, keep_second, count = keep_first[:, None], keep_second[:, None], count[:, None]
     for step in range(ITERS):
         part_col = jnp.sum(q_mat, axis=0)
         col_tot = spread_sum(part_col, DP)
@@ -122,7 +127,6 @@
     second = second / of_crop(second_at)[:, None] / teach_total * teach_total
     probs = expo / total[:, None]
     target_rows = first * keep_first + second * keep_second
-    count = keep_first + keep_second
     scale_out = total_protos / 64.0
     grad_bf = (scale_out * (count * probs - target_rows) / 0.1).astype(jnp.bfloat16)
     dxn = lax.dot_general(
@@ -137,12 +141,14 @@
     dwn_part = lax.dot_general(
         x_bf, grad_bf, (((0,), (0,)), ((), ())), preferred_element_type=jnp.float32
     )
-    dwn_total = dwn_reduce(dwn_part)
+    dwn_ring = dwn_reduce(dwn_part)
     got = spread(dxn.astype(jnp.float16), "zh")
     dxn = jnp.sum(got.astype(jnp.float32), axis=0).astype(jnp.float16)
-    for axes in ("zl", "y"):
-        got = spread(dxn, axes)
-        dxn = got.reshape(-1, dxn.shape[1])
+    got = spread(dxn, "zl")
+    dxn, dwn_ring = lax.optimization_barrier((got.reshape(-1, dxn.shape[1]), dwn_ring))
+    got = spread(dxn, "y")
+    dxn = got.reshape(-1, dxn.shape[1])
+    dwn_total = dwn_join(dwn_ring)
     student_grad = x_scale * dxn.astype(jnp.float32)
     proto_grad = col_scale * (
         dwn_total - w_norm * jnp.sum(w_norm * dwn_total, axis=0, keepdims=True)

time: 284 us -> 299 us (1.053)
  the two profiles are of different devices: /device:TPU:32 before, /device:TPU:1 now
where the time goes in v8:
time: 299 us; the launch traced here: 297 us
  starting transfers between devices  92.8 us (31%)
  blocking collectives  87.2 us (29%)
  waiting for transfers between devices  71.7 us (24%)
  local copies, waits for them, and re-layouts  22.6 us (8%)
  other arithmetic  16.8 us (6%)
  matrix products  5.07 us (2%)
    all_to_all x8, waiting for transfers between devices, spread(): lax.all_to_all(jnp.broadcast_to(part[None], (n,) + part.shape), axes, 0, 0)  68.1 us
    all_to_all x3, blocking collectives, spread(): lax.all_to_all(jnp.broadcast_to(part[None], (n,) + part.shape), axes, 0, 0)  59.7 us
    all_to_all x8, starting transfers between devices, spread(): lax.all_to_all(jnp.broadcast_to(part[None], (n,) + part.shape), axes, 0, 0)  59.5 us
    ppermute x8, starting transfers between devices, shifted(): return lax.ppermute(part, axis, [(i, (i + step) % n) for i in range(n)])  33.3 us
    all_to_all x2, blocking collectives, swap(): return lax.all_to_all(pieces, axes, 0, 0)  18.1 us
    all_to_all x1, blocking collectives, on_device(): both = spread_sum(jnp.sum(lax.all_to_all(sent, NEAR, 0, 0), axis=0), 'zh')  9.41 us
    gather x2, local copies, waits for them, and re-layouts, on_device(): first = q_mat.at[first_at].get(mode='promise_in_bounds')  7.66 us
    gather x2, local copies, waits for them, and re-layouts, on_device(): second = q_mat.at[second_at].get(mode='promise_in_bounds')  7.65 us
  transfers between devices with their start and end apart: 16, of which 9 were waited for; matrix products, arithmetic and copies ran while one was open for 8% of the time, Pallas kernels for 0%

profile of v8, /device:TPU:1, one launch (start us, length us, event | category | flops | bytes accessed | tf_op | source)
XLA Modules:
  0.0 297.4 jit_solution(17807163414927852488)
XLA Ops:
  5.5 17.9 %all-to-all-start = ((f32[8,4,128]{2,1,0:T(4,128)}), f32[8,4,128]{2,1,0:T(4,128)}, u32[]{:S(2)}, u32[]{:S(2)}) async-start(f32[8,4,128]{2,1,0:T(4,128)} %broadcast_in_dim.61), calls=%async_computation | async-start | bytes 32768 | tf_op jit(solution)/shard_map/all_to_all | solution.py:21
  25.8 2.4 all-to-all-done
  30.2 9.4 %all_to_all.70 = f32[16,3,128]{2,1,0:T(4,128)S(1)} all-to-all(f32[16,3,128]{2,1,0:T(4,128)S(1)} %reshape.85), channel_id=1, replica_groups=mesh['x'=4,'core'=2,'y'=4,'zh'=8,'zl'=4] {'y','zl'}, dimensions={0} | all-to-all | bytes 49152 | tf_op jit(solution)/shard_map/all_to_all | solution.py:103
  39.7 39.6 %all_to_all.71 = f32[8,3,128]{2,1,0:T(4,128)S(1)} all-to-all(f32[8,3,128]{2,1,0:T(4,128)S(1)} %broadcast_in_dim.63), channel_id=1, replica_groups=mesh['x'=4,'core'=2,'y'=4,'zh'=8,'zl'=4] {'zh'}, dimensions={0} | all-to-all | bytes 24576 | tf_op jit(solution)/shard_map/all_to_all | solution.py:21
  80.5 10.6 %all_to_all.72 = f32[8,4,128]{2,1,0:T(4,128)S(1)} all-to-all(f32[8,4,128]{2,1,0:T(4,128)S(1)} %broadcast_in_dim.121), channel_id=1, replica_groups=mesh['x'=4,'core'=2,'y'=4,'zh'=8,'zl'=4] {'x','core'}, dimensions={0} | all-to-all | bytes 32768 | tf_op jit(solution)/shard_map/all_to_all | solution.py:21
  91.3 9.4 %all_to_all.73 = f32[16,3,128]{2,1,0:T(4,128)S(1)} all-to-all(f32[16,3,128]{2,1,0:T(4,128)S(1)} %broadcast_in_dim.123), channel_id=1, replica_groups=mesh['x'=4,'core'=2,'y'=4,'zh'=8,'zl'=4] {'y','zl'}, dimensions={0} | all-to-all | bytes 49152 | tf_op jit(solution)/shard_map/all_to_all | solution.py:21
  101.4 3.3 %all-to-all-start.5 = ((f32[8,2,128]{2,1,0:T(2,128)}), f32[8,2,128]{2,1,0:T(2,128)S(1)}, u32[]{:S(2)}, u32[]{:S(2)}) async-start(f32[8,2,128]{2,1,0:T(2,128)} %broadcast_in_dim.125), calls=%async_computation.5 | async-start | bytes 16384 | tf_op jit(solution)/shard_map/all_to_all | solution.py:21
  105.3 20.4 %all-to-all-done.5 = f32[8,2,128]{2,1,0:T(2,128)S(1)} async-done(((f32[8,2,128]{2,1,0:T(2,128)}), f32[8,2,128]{2,1,0:T(2,128)S(1)}, u32[]{:S(2)}, u32[]{:S(2)}) %all-to-all-start.5) | async-done | bytes 8224 | tf_op jit(solution)/shard_map/all_to_all | solution.py:21
  127.3 6.5 %all-to-all-start.6 = ((f32[8,4,128]{2,1,0:T(4,128)}), f32[8,4,128]{2,1,0:T(4,128)S(1)}, u32[]{:S(2)}, u32[]{:S(2)}) async-start(f32[8,4,128]{2,1,0:T(4,128)} %broadcast_in_dim.127), calls=%async_computation.6 | async-start | bytes 32768 | tf_op jit(solution)/shard_map/all_to_all | solution.py:21
  133.8 4.7 %all-to-all-done.6 = f32[8,4,128]{2,1,0:T(4,128)S(1)} async-done(((f32[8,4,128]{2,1,0:T(4,128)}), f32[8,4,128]{2,1,0:T(4,128)S(1)}, u32[]{:S(2)}, u32[]{:S(2)}) %all-to-all-start.6) | async-done | bytes 16416 | tf_op jit(solution)/shard_map/all_to_all | solution.py:21
  140.3 3.5 %all-to-all-start.7 = ((f32[16,2,128]{2,1,0:T(2,128)}), f32[16,2,128]{2,1,0:T(2,128)S(1)}, u32[]{:S(2)}, u32[]{:S(2)}) async-start(f32[16,2,128]{2,1,0:T(2,128)} %broadcast_in_dim.129), calls=%async_computation.7 | async-start | bytes 32768 | tf_op jit(solution)/shard_map/all_to_all | solution.py:21
  144.4 6.1 %all-to-all-done.7 = f32[16,2,128]{2,1,0:T(2,128)S(1)} async-done(((f32[16,2,128]{2,1,0:T(2,128)}), f32[16,2,128]{2,1,0:T(2,128)S(1)}, u32[]{:S(2)}, u32[]{:S(2)}) %all-to-all-start.7) | async-done | bytes 16416 | tf_op jit(solution)/shard_map/all_to_all | solution.py:21
  151.8 3.3 %all-to-all-start.8 = ((f32[8,2,128]{2,1,0:T(2,128)}), f32[8,2,128]{2,1,0:T(2,128)S(1)}, u32[]{:S(2)}, u32[]{:S(2)}) async-start(f32[8,2,128]{2,1,0:T(2,128)} %broadcast_in_dim.132), calls=%async_computation.8 | async-start | bytes 16384 | tf_op jit(solution)/shard_map/all_to_all | solution.py:21
  155.2 4.4 %gather_fusion = f32[1280,512]{1,0:T(8,128)} fusion(f32[256,512]{1,0:T(8,128)S(1)} %get-tuple-element.37, s32[2048]{0:T(1024)S(1)} %pad_clamp_fusion.1), kind=kCustom, calls=%fused_computation | custom fusion | bytes 5248000 | tf_op jit(solution)/shard_map/gather | solution.py:116
  159.6 3.2 %copy.20 = f32[1280,512]{0,1:T(8,128)} copy(f32[1280,512]{1,0:T(8,128)} %gather_fusion) | data formatting | bytes 5242880 | tf_op jit(solution)/shard_map/gather | solution.py:116
  162.9 4.4 %gather_fusion.1 = f32[1280,512]{1,0:T(8,128)} fusion(f32[256,512]{1,0:T(8,128)S(1)} %get-tuple-element.37, s32[2048]{0:T(1024)S(1)} %pad_clamp_fusion), kind=kCustom, calls=%fused_computation.1 | custom fusion | bytes 5248000 | tf_op jit(solution)/shard_map/gather | solution.py:117
  167.3 3.3 %copy.21 = f32[1280,512]{0,1:T(8,128)} copy(f32[1280,512]{1,0:T(8,128)} %gather_fusion.1) | data formatting | bytes 5242880 | tf_op jit(solution)/shard_map/gather | solution.py:117
  170.5 5.6 %all-to-all-done.8 = f32[8,2,128]{2,1,0:T(2,128)S(1)} async-done(((f32[8,2,128]{2,1,0:T(2,128)}), f32[8,2,128]{2,1,0:T(2,128)S(1)}, u32[]{:S(2)}, u32[]{:S(2)}) %all-to-all-start.8) | async-done | bytes 8224 | tf_op jit(solution)/shard_map/all_to_all | solution.py:21
  177.3 3.5 %multiply_convert_fusion = bf16[1280,512]{0,1:T(8,128)(2,1)S(1)} fusion(f32[1280,512]{0,1:T(8,128)} %copy.21, f32[1280,512]{0,1:T(8,128)} %copy.20, f32[1280,512]{0,1:T(8,128)S(1)} %get-tuple-element.50, f32[1280]{0:T(1024)} %get-tuple-element.27, f32[1280]{0:T(1024)S(1)} %get-tuple-element.33, f32[1280]{0:T(1024)} %get-tuple-element.25, ...), kind=kLoop, calls=%fused_computation.4 | loop fusion | flops 6553600 | bytes 9205760 | tf_op jit(solution)/shard_map/convert_element_type | solution.py:131
  182.3 10.1 %all_to_all.74 = f16[4,320,256]{2,1,0:T(8,128)(2,1)S(1)} all-to-all(f16[4,320,256]{2,1,0:T(8,128)(2,1)S(1)} %bitcast.33), channel_id=1, replica_groups=mesh['x'=4,'core'=2,'y'=4,'zh'=8,'zl'=4] {'y'}, dimensions={0} | all-to-all | bytes 1310720 | tf_op jit(solution)/shard_map/all_to_all | solution.py:27
  192.5 8.0 %all_to_all.75 = f16[4,80,256]{2,1,0:T(8,128)(2,1)S(1)} all-to-all(f16[4,80,256]{2,1,0:T(8,128)(2,1)S(1)} %bitcast.35), channel_id=1, replica_groups=mesh['x'=4,'core'=2,'y'=4,'zh'=8,'zl'=4] {'zl'}, dimensions={0} | all-to-all | bytes 327680 | tf_op jit(solution)/shard_map/all_to_all | solution.py:27
  201.4 16.2 %all-to-all-start.11 = ((f16[8,80,256]{2,1,0:T(8,128)(2,1)}), f16[8,80,256]{2,1,0:T(8,128)(2,1)S(1)}, u32[]{:S(2)}, u32[]{:S(2)}) async-start(f16[8,80,256]{2,1,0:T(8,128)(2,1)} %broadcast_in_dim.137), calls=%async_computation.11 | async-start | bytes 655360 | tf_op jit(solution)/shard_map/all_to_all | solution.py:21
  218.4 6.6 %collective-permute-start = (f32[128,512]{1,0:T(8,128)S(1)}, f32[128,512]{1,0:T(8,128)S(1)}, u32[]{:S(2)}, u32[]{:S(2)}) collective-permute-start(f32[128,512]{1,0:T(8,128)S(1)} %constant_dynamic-slice_fusion.4), channel_id=1, source_target_pairs={{0,128},{128,0},{1,129},{129,1},{2,130},{130,2},{3,131},{131,3},{4... | collective-permute-start | bytes 786440 | tf_op jit(solution)/shard_map/ppermute | solution.py:39
  228.5 4.3 %collective-permute-start.3 = (f32[32,512]{1,0:T(8,128)S(1)}, f32[32,512]{1,0:T(8,128)S(1)}, u32[]{:S(2)}, u32[]{:S(2)}) collective-permute-start(f32[32,512]{1,0:T(8,128)S(1)} %get-tuple-element.45), channel_id=1, source_target_pairs={{0,768},{256,0},{512,256},{768,512},{1,769},{257,1},{513,257},{769... | collective-permute-start | bytes 196616 | tf_op jit(solution)/shard_map/ppermute | solution.py:39
  234.7 19.0 %all-to-all-done.11 = f16[8,80,256]{2,1,0:T(8,128)(2,1)S(1)} async-done(((f16[8,80,256]{2,1,0:T(8,128)(2,1)}), f16[8,80,256]{2,1,0:T(8,128)(2,1)S(1)}, u32[]{:S(2)}, u32[]{:S(2)}) %all-to-all-start.11) | async-done | bytes 327712 | tf_op jit(solution)/shard_map/all_to_all | solution.py:21
  254.5 5.2 %all-to-all-start.12 = ((f16[4,80,256]{2,1,0:T(8,128)(2,1)}), f16[4,80,256]{2,1,0:T(8,128)(2,1)S(1)}, u32[]{:S(2)}, u32[]{:S(2)}) async-start(f16[4,80,256]{2,1,0:T(8,128)(2,1)} %broadcast_in_dim.138), calls=%async_computation.12 | async-start | bytes 327680 | tf_op jit(solution)/shard_map/all_to_all | solution.py:21
  262.0 3.7 %collective-permute-start.5 = (f32[32,512]{1,0:T(8,128)S(1)}, f32[32,512]{1,0:T(8,128)S(1)}, u32[]{:S(2)}, u32[]{:S(2)}) collective-permute-start(f32[32,512]{1,0:T(8,128)S(1)} %add_add_fusion), channel_id=1, source_target_pairs={{0,512},{256,768},{512,0},{768,256},{1,513},{257,769},{513,1},{769... | collective-permute-start | bytes 196616 | tf_op jit(solution)/shard_map/ppermute | solution.py:39
  265.7 2.8 collective-permute-start.4
  268.5 2.5 collective-permute-done.4
  271.1 9.6 %collective-permute-start.7 = (f32[128,512]{1,0:T(8,128)S(1)}, f32[128,512]{1,0:T(8,128)S(1)}, u32[]{:S(2)}, u32[]{:S(2)}) collective-permute-start(f32[128,512]{1,0:T(8,128)S(1)} %constant_dynamic-slice_fusion), channel_id=1, source_target_pairs={{0,128},{128,0},{1,129},{129,1},{2,130},{130,2},{3,131},{131,3},{4... | collective-permute-start | bytes 786440 | tf_op jit(solution)/shard_map/ppermute | solution.py:39
  281.7 3.5 %all-to-all-start.13 = ((f16[4,320,256]{2,1,0:T(8,128)(2,1)}), f16[4,320,256]{2,1,0:T(8,128)(2,1)S(1)}, u32[]{:S(2)}, u32[]{:S(2)}) async-start(f16[4,320,256]{2,1,0:T(8,128)(2,1)} %broadcast_in_dim.139), calls=%async_computation.13 | async-start | bytes 1310720 | tf_op jit(solution)/shard_map/all_to_all | solution.py:21
  286.2 9.8 %all-to-all-done.13 = f16[4,320,256]{2,1,0:T(8,128)(2,1)S(1)} async-done(((f16[4,320,256]{2,1,0:T(8,128)(2,1)}), f16[4,320,256]{2,1,0:T(8,128)(2,1)S(1)}, u32[]{:S(2)}, u32[]{:S(2)}) %all-to-all-start.13) | async-done | bytes 655392 | tf_op jit(solution)/shard_map/all_to_all | solution.py:21
  (102 shorter events, 33.1 us)
Async XLA Ops:
  0.6 23.1 %copy-start.2 = (bf16[256,512]{1,0:T(8,128)(2,1)S(1)}, bf16[256,512]{1,0:T(8,128)(2,1)}, u32[]{:S(2)}) copy-start(bf16[256,512]{1,0:T(8,128)(2,1)} %param.7) | copy-start | bytes 786436
  0.6 22.8 %copy-start = (bf16[1280,256]{1,0:T(8,128)(2,1)S(1)}, bf16[1280,256]{1,0:T(8,128)(2,1)}, u32[]{:S(2)}) copy-start(bf16[1280,256]{1,0:T(8,128)(2,1)} %param.5) | copy-start | bytes 1966084
  5.5 22.7 %all-to-all-start = ((f32[8,4,128]{2,1,0:T(4,128)}), f32[8,4,128]{2,1,0:T(4,128)}, u32[]{:S(2)}, u32[]{:S(2)}) async-start(f32[8,4,128]{2,1,0:T(4,128)} %broadcast_in_dim.61), calls=%async_computation | async-start | bytes 32768 | tf_op jit(solution)/shard_map/all_to_all | solution.py:21
  29.0 75.8 %copy-start.5 = (s32[1280]{0:T(1024)S(1)}, s32[1280]{0:T(1024)}, u32[]{:S(2)}) copy-start(s32[1280]{0:T(1024)} %param.9) | copy-start | bytes 15364
  79.3 54.5 %copy-start.6 = (s32[1280]{0:T(1024)S(1)}, s32[1280]{0:T(1024)}, u32[]{:S(2)}) copy-start(s32[1280]{0:T(1024)} %param.8) | copy-start | bytes 15364
  101.4 24.4 %all-to-all-start.5 = ((f32[8,2,128]{2,1,0:T(2,128)}), f32[8,2,128]{2,1,0:T(2,128)S(1)}, u32[]{:S(2)}, u32[]{:S(2)}) async-start(f32[8,2,128]{2,1,0:T(2,128)} %broadcast_in_dim.125), calls=%async_computation.5 | async-start | bytes 16384 | tf_op jit(solution)/shard_map/all_to_all | solution.py:21
  127.3 11.1 %all-to-all-start.6 = ((f32[8,4,128]{2,1,0:T(4,128)}), f32[8,4,128]{2,1,0:T(4,128)S(1)}, u32[]{:S(2)}, u32[]{:S(2)}) async-start(f32[8,4,128]{2,1,0:T(4,128)} %broadcast_in_dim.127), calls=%async_computation.6 | async-start | bytes 32768 | tf_op jit(solution)/shard_map/all_to_all | solution.py:21
  140.3 10.2 %all-to-all-start.7 = ((f32[16,2,128]{2,1,0:T(2,128)}), f32[16,2,128]{2,1,0:T(2,128)S(1)}, u32[]{:S(2)}, u32[]{:S(2)}) async-start(f32[16,2,128]{2,1,0:T(2,128)} %broadcast_in_dim.129), calls=%async_computation.7 | async-start | bytes 32768 | tf_op jit(solution)/shard_map/all_to_all | solution.py:21
  151.8 24.3 %all-to-all-start.8 = ((f32[8,2,128]{2,1,0:T(2,128)}), f32[8,2,128]{2,1,0:T(2,128)S(1)}, u32[]{:S(2)}, u32[]{:S(2)}) async-start(f32[8,2,128]{2,1,0:T(2,128)} %broadcast_in_dim.132), calls=%async_computation.8 | async-start | bytes 16384 | tf_op jit(solution)/shard_map/all_to_all | solution.py:21
  177.3 3.5 %copy-start.1 = (bf16[1280,256]{1,0:T(8,128)(2,1)S(1)}, bf16[1280,256]{1,0:T(8,128)(2,1)}, u32[]{:S(2)}) copy-start(bf16[1280,256]{1,0:T(8,128)(2,1)} %param.5) | copy-start | bytes 1966084
  180.8 1.1 copy-start.3
  192.5 25.1 %copy-start.4 = (bf16[1280,512]{0,1:T(8,128)(2,1)S(1)}, bf16[1280,512]{0,1:T(8,128)(2,1)}, u32[]{:S(2)}) copy-start(bf16[1280,512]{0,1:T(8,128)(2,1)} %copy-done.3) | copy-start | bytes 3932164
  201.4 52.4 %all-to-all-start.11 = ((f16[8,80,256]{2,1,0:T(8,128)(2,1)}), f16[8,80,256]{2,1,0:T(8,128)(2,1)S(1)}, u32[]{:S(2)}, u32[]{:S(2)}) async-start(f16[8,80,256]{2,1,0:T(8,128)(2,1)} %broadcast_in_dim.137), calls=%async_computation.11 | async-start | bytes 655360 | tf_op jit(solution)/shard_map/all_to_all | solution.py:21
  218.4 7.8 %collective-permute-start = (f32[128,512]{1,0:T(8,128)S(1)}, f32[128,512]{1,0:T(8,128)S(1)}, u32[]{:S(2)}, u32[]{:S(2)}) collective-permute-start(f32[128,512]{1,0:T(8,128)S(1)} %constant_dynamic-slice_fusion.4), channel_id=1, source_target_pairs={{0,128},{128,0},{1,129},{129,1},{2,130},{130,2},{3,131},{131,3},{4... | collective-permute-start | bytes 786440 | tf_op jit(solution)/shard_map/ppermute | solution.py:39
  226.3 33.4 %collective-permute-start.1 = (f32[32,512]{1,0:T(8,128)S(1)}, f32[32,512]{1,0:T(8,128)S(1)}, u32[]{:S(2)}, u32[]{:S(2)}) collective-permute-start(f32[32,512]{1,0:T(8,128)S(1)} %get-tuple-element.44), channel_id=1, source_target_pairs={{0,256},{256,512},{512,768},{768,0},{1,257},{257,513},{513,769},{7... | collective-permute-start | bytes 196616 | tf_op jit(solution)/shard_map/ppermute | solution.py:39
  228.5 31.2 %collective-permute-start.3 = (f32[32,512]{1,0:T(8,128)S(1)}, f32[32,512]{1,0:T(8,128)S(1)}, u32[]{:S(2)}, u32[]{:S(2)}) collective-permute-start(f32[32,512]{1,0:T(8,128)S(1)} %get-tuple-element.45), channel_id=1, source_target_pairs={{0,768},{256,0},{512,256},{768,512},{1,769},{257,1},{513,257},{769... | collective-permute-start | bytes 196616 | tf_op jit(solution)/shard_map/ppermute | solution.py:39
  232.8 26.9 %collective-permute-start.2 = (f32[32,512]{1,0:T(8,128)S(1)}, f32[32,512]{1,0:T(8,128)S(1)}, u32[]{:S(2)}, u32[]{:S(2)}) collective-permute-start(f32[32,512]{1,0:T(8,128)S(1)} %get-tuple-element.46), channel_id=1, source_target_pairs={{0,512},{256,768},{512,0},{768,256},{1,513},{257,769},{513,1},{769... | collective-permute-start | bytes 196616 | tf_op jit(solution)/shard_map/ppermute | solution.py:39
  254.5 16.6 %all-to-all-start.12 = ((f16[4,80,256]{2,1,0:T(8,128)(2,1)}), f16[4,80,256]{2,1,0:T(8,128)(2,1)S(1)}, u32[]{:S(2)}, u32[]{:S(2)}) async-start(f16[4,80,256]{2,1,0:T(8,128)(2,1)} %broadcast_in_dim.138), calls=%async_computation.12 | async-start | bytes 327680 | tf_op jit(solution)/shard_map/all_to_all | solution.py:21
  259.8 11.2 %collective-permute-start.6 = (f32[32,512]{1,0:T(8,128)S(1)}, f32[32,512]{1,0:T(8,128)S(1)}, u32[]{:S(2)}, u32[]{:S(2)}) collective-permute-start(f32[32,512]{1,0:T(8,128)S(1)} %add_add_fusion), channel_id=1, source_target_pairs={{0,256},{256,512},{512,768},{768,0},{1,257},{257,513},{513,769},{7... | collective-permute-start | bytes 196616 | tf_op jit(solution)/shard_map/ppermute | solution.py:39
  262.0 9.0 %collective-permute-start.5 = (f32[32,512]{1,0:T(8,128)S(1)}, f32[32,512]{1,0:T(8,128)S(1)}, u32[]{:S(2)}, u32[]{:S(2)}) collective-permute-start(f32[32,512]{1,0:T(8,128)S(1)} %add_add_fusion), channel_id=1, source_target_pairs={{0,512},{256,768},{512,0},{768,256},{1,513},{257,769},{513,1},{769... | collective-permute-start | bytes 196616 | tf_op jit(solution)/shard_map/ppermute | solution.py:39
  265.7 5.3 %collective-permute-start.4 = (f32[32,512]{1,0:T(8,128)S(1)}, f32[32,512]{1,0:T(8,128)S(1)}, u32[]{:S(2)}, u32[]{:S(2)}) collective-permute-start(f32[32,512]{1,0:T(8,128)S(1)} %add_add_fusion), channel_id=1, source_target_pairs={{0,768},{256,0},{512,256},{768,512},{1,769},{257,1},{513,257},{769... | collective-permute-start | bytes 196616 | tf_op jit(solution)/shard_map/ppermute | solution.py:39
  271.1 14.0 %collective-permute-start.7 = (f32[128,512]{1,0:T(8,128)S(1)}, f32[128,512]{1,0:T(8,128)S(1)}, u32[]{:S(2)}, u32[]{:S(2)}) collective-permute-start(f32[128,512]{1,0:T(8,128)S(1)} %constant_dynamic-slice_fusion), channel_id=1, source_target_pairs={{0,128},{128,0},{1,129},{129,1},{2,130},{130,2},{3,131},{131,3},{4... | collective-permute-start | bytes 786440 | tf_op jit(solution)/shard_map/ppermute | solution.py:39
  281.7 14.4 %all-to-all-start.13 = ((f16[4,320,256]{2,1,0:T(8,128)(2,1)}), f16[4,320,256]{2,1,0:T(8,128)(2,1)S(1)}, u32[]{:S(2)}, u32[]{:S(2)}) async-start(f16[4,320,256]{2,1,0:T(8,128)(2,1)} %broadcast_in_dim.139), calls=%async_computation.13 | async-start | bytes 1310720 | tf_op jit(solution)/shard_map/all_to_all | solution.py:21

commit v9 on v8

--- a/solution.py
+++ b/solution.py
@@ -144,9 +144,8 @@
     dwn_ring = dwn_reduce(dwn_part)
     got = spread(dxn.astype(jnp.float16), "zh")
     dxn = jnp.sum(got.astype(jnp.float32), axis=0).astype(jnp.float16)
-    got = spread(dxn, "zl")
-    dxn, dwn_ring = lax.optimization_barrier((got.reshape(-1, dxn.shape[1]), dwn_ring))
-    got = spread(dxn, "y")
+    dxn, dwn_ring = lax.optimization_barrier((dxn, dwn_ring))
+    got = spread(dxn, NEAR)
     dxn = got.reshape(-1, dxn.shape[1])
     dwn_total = dwn_join(dwn_ring)
     student_grad = x_scale * dxn.astype(jnp.float32)

time: 299 us -> 285 us (0.953)
  the two profiles are of different devices: /device:TPU:1 before, /device:TPU:128 now
where the time goes in v9:
time: 285 us; the launch traced here: 284 us
  blocking collectives  96.7 us (34%)
  starting transfers between devices  74.5 us (26%)
  waiting for transfers between devices  67.9 us (24%)
  local copies, waits for them, and re-layouts  21.9 us (8%)
  other arithmetic  16.8 us (6%)
  matrix products  5.08 us (2%)
    all_to_all x3, blocking collectives, spread(): lax.all_to_all(jnp.broadcast_to(part[None], (n,) + part.shape), axes, 0, 0)  59.6 us
    all_to_all x7, waiting for transfers between devices, spread(): lax.all_to_all(jnp.broadcast_to(part[None], (n,) + part.shape), axes, 0, 0)  56.2 us
    all_to_all x7, starting transfers between devices, spread(): lax.all_to_all(jnp.broadcast_to(part[None], (n,) + part.shape), axes, 0, 0)  52.7 us
    ppermute x8, starting transfers between devices, shifted(): return lax.ppermute(part, axis, [(i, (i + step) % n) for i in range(n)])  21.8 us
    all_to_all x2, blocking collectives, swap(): return lax.all_to_all(pieces, axes, 0, 0)  20.6 us
    all_to_all x1, blocking collectives, on_device(): both = spread_sum(jnp.sum(lax.all_to_all(sent, NEAR, 0, 0), axis=0), 'zh')  16.4 us
    ppermute x8, waiting for transfers between devices, shifted(): return lax.ppermute(part, axis, [(i, (i + step) % n) for i in range(n)])  11.7 us
    gather x2, local copies, waits for them, and re-layouts, on_device(): first = q_mat.at[first_at].get(mode='promise_in_bounds')  7.66 us
  transfers between devices with their start and end apart: 15, of which 11 were waited for; matrix products, arithmetic and copies ran while one was open for 7% of the time, Pallas kernels for 0%

profile of v9, /device:TPU:128, one launch (start us, length us, event | category | flops | bytes accessed | tf_op | source)
XLA Modules:
  0.0 284.0 jit_solution(6341047561351676683)
XLA Ops:
  2.8 2.1 fusion.34
  5.5 4.3 %all-to-all-start = ((f32[8,4,128]{2,1,0:T(4,128)}), f32[8,4,128]{2,1,0:T(4,128)}, u32[]{:S(2)}, u32[]{:S(2)}) async-start(f32[8,4,128]{2,1,0:T(4,128)} %broadcast_in_dim.59), calls=%async_computation | async-start | bytes 32768 | tf_op jit(solution)/shard_map/all_to_all | solution.py:21
  12.2 3.1 %all-to-all-done = f32[8,4,128]{2,1,0:T(4,128)} async-done(((f32[8,4,128]{2,1,0:T(4,128)}), f32[8,4,128]{2,1,0:T(4,128)}, u32[]{:S(2)}, u32[]{:S(2)}) %all-to-all-start) | async-done | bytes 16416 | tf_op jit(solution)/shard_map/all_to_all | solution.py:21
  17.3 16.4 %all_to_all.65 = f32[16,3,128]{2,1,0:T(4,128)S(1)} all-to-all(f32[16,3,128]{2,1,0:T(4,128)S(1)} %reshape.79), channel_id=1, replica_groups=mesh['x'=4,'core'=2,'y'=4,'zh'=8,'zl'=4] {'y','zl'}, dimensions={0} | all-to-all | bytes 49152 | tf_op jit(solution)/shard_map/all_to_all | solution.py:103
  33.7 41.3 %all_to_all.66 = f32[8,3,128]{2,1,0:T(4,128)S(1)} all-to-all(f32[8,3,128]{2,1,0:T(4,128)S(1)} %broadcast_in_dim.113), channel_id=1, replica_groups=mesh['x'=4,'core'=2,'y'=4,'zh'=8,'zl'=4] {'zh'}, dimensions={0} | all-to-all | bytes 24576 | tf_op jit(solution)/shard_map/all_to_all | solution.py:21
  76.3 7.7 %all_to_all.67 = f32[8,4,128]{2,1,0:T(4,128)S(1)} all-to-all(f32[8,4,128]{2,1,0:T(4,128)S(1)} %broadcast_in_dim.115), channel_id=1, replica_groups=mesh['x'=4,'core'=2,'y'=4,'zh'=8,'zl'=4] {'x','core'}, dimensions={0} | all-to-all | bytes 32768 | tf_op jit(solution)/shard_map/all_to_all | solution.py:21
  84.2 10.6 %all_to_all.68 = f32[16,3,128]{2,1,0:T(4,128)S(1)} all-to-all(f32[16,3,128]{2,1,0:T(4,128)S(1)} %broadcast_in_dim.117), channel_id=1, replica_groups=mesh['x'=4,'core'=2,'y'=4,'zh'=8,'zl'=4] {'y','zl'}, dimensions={0} | all-to-all | bytes 49152 | tf_op jit(solution)/shard_map/all_to_all | solution.py:21
  95.4 8.6 %all-to-all-start.5 = ((f32[8,2,128]{2,1,0:T(2,128)}), f32[8,2,128]{2,1,0:T(2,128)S(1)}, u32[]{:S(2)}, u32[]{:S(2)}) async-start(f32[8,2,128]{2,1,0:T(2,128)} %broadcast_in_dim.119), calls=%async_computation.5 | async-start | bytes 16384 | tf_op jit(solution)/shard_map/all_to_all | solution.py:21
  104.6 16.2 %all-to-all-done.5 = f32[8,2,128]{2,1,0:T(2,128)S(1)} async-done(((f32[8,2,128]{2,1,0:T(2,128)}), f32[8,2,128]{2,1,0:T(2,128)S(1)}, u32[]{:S(2)}, u32[]{:S(2)}) %all-to-all-start.5) | async-done | bytes 8224 | tf_op jit(solution)/shard_map/all_to_all | solution.py:21
  122.4 3.3 %all-to-all-start.6 = ((f32[8,4,128]{2,1,0:T(4,128)}), f32[8,4,128]{2,1,0:T(4,128)S(1)}, u32[]{:S(2)}, u32[]{:S(2)}) async-start(f32[8,4,128]{2,1,0:T(4,128)} %broadcast_in_dim.121), calls=%async_computation.6 | async-start | bytes 32768 | tf_op jit(solution)/shard_map/all_to_all | solution.py:21
  125.8 5.3 %all-to-all-done.6 = f32[8,4,128]{2,1,0:T(4,128)S(1)} async-done(((f32[8,4,128]{2,1,0:T(4,128)}), f32[8,4,128]{2,1,0:T(4,128)S(1)}, u32[]{:S(2)}, u32[]{:S(2)}) %all-to-all-start.6) | async-done | bytes 16416 | tf_op jit(solution)/shard_map/all_to_all | solution.py:21
  132.8 3.5 %all-to-all-start.7 = ((f32[16,2,128]{2,1,0:T(2,128)}), f32[16,2,128]{2,1,0:T(2,128)S(1)}, u32[]{:S(2)}, u32[]{:S(2)}) async-start(f32[16,2,128]{2,1,0:T(2,128)} %broadcast_in_dim.123), calls=%async_computation.7 | async-start | bytes 32768 | tf_op jit(solution)/shard_map/all_to_all | solution.py:21
  136.9 7.3 %all-to-all-done.7 = f32[16,2,128]{2,1,0:T(2,128)S(1)} async-done(((f32[16,2,128]{2,1,0:T(2,128)}), f32[16,2,128]{2,1,0:T(2,128)S(1)}, u32[]{:S(2)}, u32[]{:S(2)}) %all-to-all-start.7) | async-done | bytes 16416 | tf_op jit(solution)/shard_map/all_to_all | solution.py:21
  145.5 8.7 %all-to-all-start.8 = ((f32[8,2,128]{2,1,0:T(2,128)}), f32[8,2,128]{2,1,0:T(2,128)S(1)}, u32[]{:S(2)}, u32[]{:S(2)}) async-start(f32[8,2,128]{2,1,0:T(2,128)} %broadcast_in_dim.126), calls=%async_computation.8 | async-start | bytes 16384 | tf_op jit(solution)/shard_map/all_to_all | solution.py:21
  154.2 4.4 %gather_fusion = f32[1280,512]{1,0:T(8,128)} fusion(f32[256,512]{1,0:T(8,128)S(1)} %get-tuple-element.37, s32[2048]{0:T(1024)S(1)} %pad_clamp_fusion.1), kind=kCustom, calls=%fused_computation | custom fusion | bytes 5248000 | tf_op jit(solution)/shard_map/gather | solution.py:116
  158.6 3.2 %copy.20 = f32[1280,512]{0,1:T(8,128)} copy(f32[1280,512]{1,0:T(8,128)} %gather_fusion) | data formatting | bytes 5242880 | tf_op jit(solution)/shard_map/gather | solution.py:116
  161.9 4.4 %gather_fusion.1 = f32[1280,512]{1,0:T(8,128)} fusion(f32[256,512]{1,0:T(8,128)S(1)} %get-tuple-element.37, s32[2048]{0:T(1024)S(1)} %pad_clamp_fusion), kind=kCustom, calls=%fused_computation.1 | custom fusion | bytes 5248000 | tf_op jit(solution)/shard_map/gather | solution.py:117
  166.3 3.3 %copy.21 = f32[1280,512]{0,1:T(8,128)} copy(f32[1280,512]{1,0:T(8,128)} %gather_fusion.1) | data formatting | bytes 5242880 | tf_op jit(solution)/shard_map/gather | solution.py:117
  172.3 3.5 %multiply_convert_fusion = bf16[1280,512]{0,1:T(8,128)(2,1)S(1)} fusion(f32[1280,512]{0,1:T(8,128)} %copy.21, f32[1280,512]{0,1:T(8,128)} %copy.20, f32[1280,512]{0,1:T(8,128)S(1)} %get-tuple-element.50, f32[1280]{0:T(1024)} %get-tuple-element.27, f32[1280]{0:T(1024)S(1)} %get-tuple-element.33, f32[1280]{0:T(1024)} %get-tuple-element.25, ...), kind=kLoop, calls=%fused_computation.4 | loop fusion | flops 6553600 | bytes 9205760 | tf_op jit(solution)/shard_map/convert_element_type | solution.py:131
  177.3 11.4 %all_to_all.69 = f16[4,320,256]{2,1,0:T(8,128)(2,1)S(1)} all-to-all(f16[4,320,256]{2,1,0:T(8,128)(2,1)S(1)} %bitcast.32), channel_id=1, replica_groups=mesh['x'=4,'core'=2,'y'=4,'zh'=8,'zl'=4] {'y'}, dimensions={0} | all-to-all | bytes 1310720 | tf_op jit(solution)/shard_map/all_to_all | solution.py:27
  188.8 9.2 %all_to_all.70 = f16[4,80,256]{2,1,0:T(8,128)(2,1)S(1)} all-to-all(f16[4,80,256]{2,1,0:T(8,128)(2,1)S(1)} %bitcast.33), channel_id=1, replica_groups=mesh['x'=4,'core'=2,'y'=4,'zh'=8,'zl'=4] {'zl'}, dimensions={0} | all-to-all | bytes 327680 | tf_op jit(solution)/shard_map/all_to_all | solution.py:27
  198.8 20.7 %all-to-all-start.11 = ((f16[8,80,256]{2,1,0:T(8,128)(2,1)}), f16[8,80,256]{2,1,0:T(8,128)(2,1)S(1)}, u32[]{:S(2)}, u32[]{:S(2)}) async-start(f16[8,80,256]{2,1,0:T(8,128)(2,1)} %broadcast_in_dim.131), calls=%async_computation.11 | async-start | bytes 655360 | tf_op jit(solution)/shard_map/all_to_all | solution.py:21
  223.9 2.5 collective-permute-start.1
  226.4 4.6 %collective-permute-start.3 = (f32[32,512]{1,0:T(8,128)S(1)}, f32[32,512]{1,0:T(8,128)S(1)}, u32[]{:S(2)}, u32[]{:S(2)}) collective-permute-start(f32[32,512]{1,0:T(8,128)S(1)} %get-tuple-element.45), channel_id=1, source_target_pairs={{0,768},{256,0},{512,256},{768,512},{1,769},{257,1},{513,257},{769... | collective-permute-start | bytes 196616 | tf_op jit(solution)/shard_map/ppermute | solution.py:39
  232.9 5.7 %collective-permute-done.2 = f32[32,512]{1,0:T(8,128)S(1)} collective-permute-done((f32[32,512]{1,0:T(8,128)S(1)}, f32[32,512]{1,0:T(8,128)S(1)}, u32[]{:S(2)}, u32[]{:S(2)}) %collective-permute-start.2) | collective-permute-done | bytes 65568 | tf_op jit(solution)/shard_map/ppermute | solution.py:39
  238.7 1.9 collective-permute-start.6
  240.6 3.4 %collective-permute-start.5 = (f32[32,512]{1,0:T(8,128)S(1)}, f32[32,512]{1,0:T(8,128)S(1)}, u32[]{:S(2)}, u32[]{:S(2)}) collective-permute-start(f32[32,512]{1,0:T(8,128)S(1)} %add_add_fusion), channel_id=1, source_target_pairs={{0,512},{256,768},{512,0},{768,256},{1,513},{257,769},{513,1},{769... | collective-permute-start | bytes 196616 | tf_op jit(solution)/shard_map/ppermute | solution.py:39
  244.0 3.7 %collective-permute-start.4 = (f32[32,512]{1,0:T(8,128)S(1)}, f32[32,512]{1,0:T(8,128)S(1)}, u32[]{:S(2)}, u32[]{:S(2)}) collective-permute-start(f32[32,512]{1,0:T(8,128)S(1)} %add_add_fusion), channel_id=1, source_target_pairs={{0,768},{256,0},{512,256},{768,512},{1,769},{257,1},{513,257},{769... | collective-permute-start | bytes 196616 | tf_op jit(solution)/shard_map/ppermute | solution.py:39
  247.7 3.1 %collective-permute-done.4 = f32[32,512]{1,0:T(8,128)S(1)} collective-permute-done((f32[32,512]{1,0:T(8,128)S(1)}, f32[32,512]{1,0:T(8,128)S(1)}, u32[]{:S(2)}, u32[]{:S(2)}) %collective-permute-start.4) | collective-permute-done | bytes 65568 | tf_op jit(solution)/shard_map/ppermute | solution.py:39
  250.8 7.8 %all-to-all-done.11 = f16[8,80,256]{2,1,0:T(8,128)(2,1)S(1)} async-done(((f16[8,80,256]{2,1,0:T(8,128)(2,1)}), f16[8,80,256]{2,1,0:T(8,128)(2,1)S(1)}, u32[]{:S(2)}, u32[]{:S(2)}) %all-to-all-start.11) | async-done | bytes 327712 | tf_op jit(solution)/shard_map/all_to_all | solution.py:21
  259.6 3.6 %all-to-all-start.12 = ((f16[16,80,256]{2,1,0:T(8,128)(2,1)}), f16[16,80,256]{2,1,0:T(8,128)(2,1)S(1)}, u32[]{:S(2)}, u32[]{:S(2)}) async-start(f16[16,80,256]{2,1,0:T(8,128)(2,1)} %broadcast_in_dim.132), calls=%async_computation.12 | async-start | bytes 1310720 | tf_op jit(solution)/shard_map/all_to_all | solution.py:21
  267.8 15.0 %all-to-all-done.12 = f16[16,80,256]{2,1,0:T(8,128)(2,1)S(1)} async-done(((f16[16,80,256]{2,1,0:T(8,128)(2,1)}), f16[16,80,256]{2,1,0:T(8,128)(2,1)S(1)}, u32[]{:S(2)}, u32[]{:S(2)}) %all-to-all-start.12) | async-done | bytes 655392 | tf_op jit(solution)/shard_map/all_to_all | solution.py:21
  (99 shorter events, 33.2 us)
Async XLA Ops:
  0.6 9.5 %copy-start.2 = (bf16[256,512]{1,0:T(8,128)(2,1)S(1)}, bf16[256,512]{1,0:T(8,128)(2,1)}, u32[]{:S(2)}) copy-start(bf16[256,512]{1,0:T(8,128)(2,1)} %param.7) | copy-start | bytes 786436
  0.6 9.2 %copy-start = (bf16[1280,256]{1,0:T(8,128)(2,1)S(1)}, bf16[1280,256]{1,0:T(8,128)(2,1)}, u32[]{:S(2)}) copy-start(bf16[1280,256]{1,0:T(8,128)(2,1)} %param.5) | copy-start | bytes 1966084
  5.5 9.8 %all-to-all-start = ((f32[8,4,128]{2,1,0:T(4,128)}), f32[8,4,128]{2,1,0:T(4,128)}, u32[]{:S(2)}, u32[]{:S(2)}) async-start(f32[8,4,128]{2,1,0:T(4,128)} %broadcast_in_dim.59), calls=%async_computation | async-start | bytes 32768 | tf_op jit(solution)/shard_map/all_to_all | solution.py:21
  16.0 88.0 %copy-start.5 = (s32[1280]{0:T(1024)S(1)}, s32[1280]{0:T(1024)}, u32[]{:S(2)}) copy-start(s32[1280]{0:T(1024)} %param.9) | copy-start | bytes 15364
  75.0 50.7 %copy-start.6 = (s32[1280]{0:T(1024)S(1)}, s32[1280]{0:T(1024)}, u32[]{:S(2)}) copy-start(s32[1280]{0:T(1024)} %param.8) | copy-start | bytes 15364
  95.4 25.4 %all-to-all-start.5 = ((f32[8,2,128]{2,1,0:T(2,128)}), f32[8,2,128]{2,1,0:T(2,128)S(1)}, u32[]{:S(2)}, u32[]{:S(2)}) async-start(f32[8,2,128]{2,1,0:T(2,128)} %broadcast_in_dim.119), calls=%async_computation.5 | async-start | bytes 16384 | tf_op jit(solution)/shard_map/all_to_all | solution.py:21
  122.4 8.6 %all-to-all-start.6 = ((f32[8,4,128]{2,1,0:T(4,128)}), f32[8,4,128]{2,1,0:T(4,128)S(1)}, u32[]{:S(2)}, u32[]{:S(2)}) async-start(f32[8,4,128]{2,1,0:T(4,128)} %broadcast_in_dim.121), calls=%async_computation.6 | async-start | bytes 32768 | tf_op jit(solution)/shard_map/all_to_all | solution.py:21
  132.8 11.4 %all-to-all-start.7 = ((f32[16,2,128]{2,1,0:T(2,128)}), f32[16,2,128]{2,1,0:T(2,128)S(1)}, u32[]{:S(2)}, u32[]{:S(2)}) async-start(f32[16,2,128]{2,1,0:T(2,128)} %broadcast_in_dim.123), calls=%async_computation.7 | async-start | bytes 32768 | tf_op jit(solution)/shard_map/all_to_all | solution.py:21
  145.5 25.6 %all-to-all-start.8 = ((f32[8,2,128]{2,1,0:T(2,128)}), f32[8,2,128]{2,1,0:T(2,128)S(1)}, u32[]{:S(2)}, u32[]{:S(2)}) async-start(f32[8,2,128]{2,1,0:T(2,128)} %broadcast_in_dim.126), calls=%async_computation.8 | async-start | bytes 16384 | tf_op jit(solution)/shard_map/all_to_all | solution.py:21
  172.3 3.5 %copy-start.1 = (bf16[1280,256]{1,0:T(8,128)(2,1)S(1)}, bf16[1280,256]{1,0:T(8,128)(2,1)}, u32[]{:S(2)}) copy-start(bf16[1280,256]{1,0:T(8,128)(2,1)} %param.5) | copy-start | bytes 1966084
  175.8 1.1 copy-start.3
  188.8 30.7 %copy-start.4 = (bf16[1280,512]{0,1:T(8,128)(2,1)S(1)}, bf16[1280,512]{0,1:T(8,128)(2,1)}, u32[]{:S(2)}) copy-start(bf16[1280,512]{0,1:T(8,128)(2,1)} %copy-done.3) | copy-start | bytes 3932164
  198.8 59.8 %all-to-all-start.11 = ((f16[8,80,256]{2,1,0:T(8,128)(2,1)}), f16[8,80,256]{2,1,0:T(8,128)(2,1)S(1)}, u32[]{:S(2)}, u32[]{:S(2)}) async-start(f16[8,80,256]{2,1,0:T(8,128)(2,1)} %broadcast_in_dim.131), calls=%async_computation.11 | async-start | bytes 655360 | tf_op jit(solution)/shard_map/all_to_all | solution.py:21
  220.4 3.4 %collective-permute-start = (f32[128,512]{1,0:T(8,128)S(1)}, f32[128,512]{1,0:T(8,128)S(1)}, u32[]{:S(2)}, u32[]{:S(2)}) collective-permute-start(f32[128,512]{1,0:T(8,128)S(1)} %constant_dynamic-slice_fusion.4), channel_id=1, source_target_pairs={{0,128},{128,0},{1,129},{129,1},{2,130},{130,2},{3,131},{131,3},{4... | collective-permute-start | bytes 786440 | tf_op jit(solution)/shard_map/ppermute | solution.py:39
  223.9 9.0 %collective-permute-start.1 = (f32[32,512]{1,0:T(8,128)S(1)}, f32[32,512]{1,0:T(8,128)S(1)}, u32[]{:S(2)}, u32[]{:S(2)}) collective-permute-start(f32[32,512]{1,0:T(8,128)S(1)} %get-tuple-element.44), channel_id=1, source_target_pairs={{0,256},{256,512},{512,768},{768,0},{1,257},{257,513},{513,769},{7... | collective-permute-start | bytes 196616 | tf_op jit(solution)/shard_map/ppermute | solution.py:39
  226.4 6.5 %collective-permute-start.3 = (f32[32,512]{1,0:T(8,128)S(1)}, f32[32,512]{1,0:T(8,128)S(1)}, u32[]{:S(2)}, u32[]{:S(2)}) collective-permute-start(f32[32,512]{1,0:T(8,128)S(1)} %get-tuple-element.45), channel_id=1, source_target_pairs={{0,768},{256,0},{512,256},{768,512},{1,769},{257,1},{513,257},{769... | collective-permute-start | bytes 196616 | tf_op jit(solution)/shard_map/ppermute | solution.py:39
  231.0 7.7 %collective-permute-start.2 = (f32[32,512]{1,0:T(8,128)S(1)}, f32[32,512]{1,0:T(8,128)S(1)}, u32[]{:S(2)}, u32[]{:S(2)}) collective-permute-start(f32[32,512]{1,0:T(8,128)S(1)} %get-tuple-element.46), channel_id=1, source_target_pairs={{0,512},{256,768},{512,0},{768,256},{1,513},{257,769},{513,1},{769... | collective-permute-start | bytes 196616 | tf_op jit(solution)/shard_map/ppermute | solution.py:39
  238.7 12.1 %collective-permute-start.6 = (f32[32,512]{1,0:T(8,128)S(1)}, f32[32,512]{1,0:T(8,128)S(1)}, u32[]{:S(2)}, u32[]{:S(2)}) collective-permute-start(f32[32,512]{1,0:T(8,128)S(1)} %add_add_fusion), channel_id=1, source_target_pairs={{0,256},{256,512},{512,768},{768,0},{1,257},{257,513},{513,769},{7... | collective-permute-start | bytes 196616 | tf_op jit(solution)/shard_map/ppermute | solution.py:39
  240.6 10.2 %collective-permute-start.5 = (f32[32,512]{1,0:T(8,128)S(1)}, f32[32,512]{1,0:T(8,128)S(1)}, u32[]{:S(2)}, u32[]{:S(2)}) collective-permute-start(f32[32,512]{1,0:T(8,128)S(1)} %add_add_fusion), channel_id=1, source_target_pairs={{0,512},{256,768},{512,0},{768,256},{1,513},{257,769},{513,1},{769... | collective-permute-start | bytes 196616 | tf_op jit(solution)/shard_map/ppermute | solution.py:39
  244.0 6.8 %collective-permute-start.4 = (f32[32,512]{1,0:T(8,128)S(1)}, f32[32,512]{1,0:T(8,128)S(1)}, u32[]{:S(2)}, u32[]{:S(2)}) collective-permute-start(f32[32,512]{1,0:T(8,128)S(1)} %add_add_fusion), channel_id=1, source_target_pairs={{0,768},{256,0},{512,256},{768,512},{1,769},{257,1},{513,257},{769... | collective-permute-start | bytes 196616 | tf_op jit(solution)/shard_map/ppermute | solution.py:39
  259.6 23.1 %all-to-all-start.12 = ((f16[16,80,256]{2,1,0:T(8,128)(2,1)}), f16[16,80,256]{2,1,0:T(8,128)(2,1)S(1)}, u32[]{:S(2)}, u32[]{:S(2)}) async-start(f16[16,80,256]{2,1,0:T(8,128)(2,1)} %broadcast_in_dim.132), calls=%async_computation.12 | async-start | bytes 1310720 | tf_op jit(solution)/shard_map/all_to_all | solution.py:21
  263.3 3.4 %collective-permute-start.7 = (f32[128,512]{1,0:T(8,128)S(1)}, f32[128,512]{1,0:T(8,128)S(1)}, u32[]{:S(2)}, u32[]{:S(2)}) collective-permute-start(f32[128,512]{1,0:T(8,128)S(1)} %constant_dynamic-slice_fusion), channel_id=1, source_target_pairs={{0,128},{128,0},{1,129},{129,1},{2,130},{130,2},{3,131},{131,3},{4... | collective-permute-start | bytes 786440 | tf_op jit(solution)/shard_map/ppermute | solution.py:39
